TPU v7x, 32 devices: a whole 2x2x4 slice. The times are simulated.
32 devices in a mesh: groups: 2 (over y), arow: 16 (over z, x, core).
Axes of the slice: x: 2, y: 2, z: 4, core: 2. Of those that a mesh axis runs over, the one named last changes fastest.
Arguments:
- feat_a: bfloat16 [64, 32, 256], P(('groups', 'arow')), parts along dimension 0, may hold values from -6 to 6
- feat_b: bfloat16 [32, 32, 256], P(('groups', 'arow')), parts along dimension 0, may hold values from -6 to 6
- a_first: float32 [8, 3, 3], replicated, may hold values from -2 to 2
- b_first: float32 [8, 3, 3], replicated, may hold values from -2 to 2
- bias_first: float32 [8], replicated, may hold values from -3 to 3
- a_second: float32 [8, 3, 3], replicated, may hold values from -1.5 to 1.5
- b_second: float32 [8, 3, 3], replicated, may hold values from -1.5 to 1.5
- bias_second: float32 [1], replicated, may hold values from -3 to 3
Outputs:
- matches: float32 [64, 32, 512], P(('groups', 'arow')), parts along dimension 0
There are 2 independent parts, one for each index of `groups`. A program takes and returns all parts, laid end to end along the dimension named above; an argument that names none is the same for every part. Nothing has to cross between parts.
All inputs are finite; a program needn't handle non-finite values.
Results may differ from a plain program's by a relative error of at most 0.0081.
Values may be sent and summed in bfloat16 or wider, within the bound.
No kernel may reach another device: no remote copies, remote signals or barrier semaphores. Data moves between devices by JAX's collectives and lax.ppermute only.
A program may use at most 128 MiB of HBM per device.

v0:
```python
import jax
import jax.numpy as jnp
from jax import lax
from jax.sharding import PartitionSpec as P

EPSILON = 1e-05


def padded(cells, sides, width):
    for axis, dim in sides:
        count = lax.axis_size(axis)
        ends = count - 1
        head = lax.slice_in_dim(cells, 0, width, axis=dim)
        tail = lax.slice_in_dim(cells, cells.shape[dim] - width, cells.shape[dim], axis=dim)
        cells = jnp.concatenate(
            [
                lax.ppermute(tail, axis, [(i, (i + 1) % count) for i in range(ends)]),
                cells,
                lax.ppermute(head, axis, [((i + 1) % count, i) for i in range(ends)]),
            ],
            axis=dim,
        )
    return cells


def shifted_zero(values, along, offset):
    extent = values.shape[along]
    if offset == 0:
        return values
    widths = [(0, 0)] * values.ndim
    if offset > 0:
        widths[along] = (0, offset)
        return lax.slice_in_dim(jnp.pad(values, widths), offset, offset + extent, axis=along)
    widths[along] = (-offset, 0)
    return lax.slice_in_dim(jnp.pad(values, widths), 0, extent, axis=along)


def conv_a(values, kernel):
    out_rows = values.shape[-3] - 2
    result = 0.0
    for row_tap in range(3):
        row_slab = lax.slice_in_dim(
            values, row_tap, row_tap + out_rows, axis=values.ndim - 3
        ).astype(jnp.float32)
        for col_tap in range(3):
            result = result + kernel[..., row_tap, col_tap][..., None, None, None] * shifted_zero(
                row_slab, values.ndim - 2, col_tap - 1
            )
    return result


def conv_b(values, kernel, map_width):
    flat_pos = lax.broadcasted_iota(jnp.int32, (values.shape[-1],), 0) % map_width
    result = 0.0
    for row_tap in range(3):
        for col_tap in range(3):
            shifted = shifted_zero(
                values, values.ndim - 1, (row_tap - 1) * map_width + (col_tap - 1)
            )
            inside = ((flat_pos + col_tap - 1 >= 0) & (flat_pos + col_tap - 1 < map_width)).astype(
                jnp.float32
            )
            result = result + kernel[..., row_tap, col_tap][..., None, None, None] * (
                shifted * inside
            )
    return result


def first_layer(correlation, kern_a, kern_b, bias_one, map_width):
    spread = conv_a(correlation, kern_a)
    return jax.nn.relu(conv_b(spread, kern_b, map_width) + bias_one[:, None, None, None]).astype(
        jnp.bfloat16
    )


def second_layer(hidden, kern_a, kern_b, bias_two, map_width):
    spread = conv_a(hidden, kern_a)
    summed = jnp.sum(conv_b(spread, kern_b, map_width), axis=0)
    return jax.nn.relu(summed + bias_two[0])


def on_device(feat_a, feat_b, a_first, b_first, bias_first, a_second, b_second, bias_second):
    map_width = feat_b.shape[1]
    channels = feat_a.shape[2]
    b_cells = feat_b.shape[0] * lax.axis_size("arow") * map_width
    a_rows = feat_a.reshape(-1, channels)
    tile_product = lax.dot_general(
        a_rows,
        lax.all_gather(feat_b, "arow", axis=0, tiled=True).reshape(-1, channels),
        (((1,), (1,)), ((), ())),
        preferred_element_type=jnp.float32,
    )
    correlation = (
        (tile_product * channels ** (-0.5))
        .astype(jnp.bfloat16)
        .reshape(feat_a.shape[0], map_width, b_cells)
    )
    correlation = padded(correlation, (("arow", 0),), 1)

    def network(kern_a1, kern_b1, kern_a2, kern_b2):
        hidden = first_layer(correlation, kern_a1, kern_b1, bias_first, map_width)
        hidden = padded(hidden, (("arow", 1),), 1)
        return second_layer(hidden, kern_a2, kern_b2, bias_second, map_width)

    score = network(a_first, b_first, a_second, b_second)
    score = score + network(b_first, a_first, b_second, a_second)
    best_over_a = lax.pmax(jnp.max(score, axis=(0, 1)), "arow")
    best_over_b = jnp.max(score, axis=2)[..., None]
    return score * (score / (best_over_a + EPSILON)) * (score / (best_over_b + EPSILON))


def solution(mesh):
    return jax.shard_map(
        on_device,
        mesh=mesh,
        in_specs=(
            P(("groups", "arow"), None, None),
            P(("groups", "arow"), None, None),
            P(),
            P(),
            P(),
            P(),
            P(),
            P(),
        ),
        out_specs=P(("groups", "arow"), None, None),
        check_vma=False,
    )
```

profile of v0, /device:TPU:0, one launch (start us, length us, event | category | flops | bytes accessed | tf_op | source)
XLA Modules:
  0.0 88.3 jit_solution(9698802883479565245)
XLA Ops:
  0.0 0.0 copy-start
  0.0 0.0 copy-start.1
  0.0 0.0 copy-start.2
  0.0 0.0 copy-start.3
  0.0 24.2 %all_gather.3 = bf16[16,32,256]{2,1,0:T(8,128)(2,1)S(1)} all-gather(bf16[1,32,256]{2,1,0:T(8,128)(2,1)} %param.9), channel_id=1, replica_groups=mesh['groups'=2,'arow'=16] {'arow'}, dimensions={0}, use_global_device_ids=true | all-gather | bytes 278528 | tf_op jit(solution)/shard_map/all_gather | solution.py:89
  24.2 0.0 copy-done
  24.2 0.2 fusion
  24.4 2.3 %collective-permute-start = (bf16[1,32,512]{2,1,0:T(8,128)(2,1)S(1)}, bf16[1,32,512]{2,1,0:T(8,128)(2,1)S(1)}, u32[]{:S(2)}, u32[]{:S(2)}) collective-permute-start(bf16[1,32,512]{2,1,0:T(8,128)(2,1)S(1)} %get-tuple-element.28), channel_id=1, source_target_pairs={{0,1},{1,2},{2,3},{3,4},{4,5},{5,6},{6,7},{7,8},{8,9},{9,10},{10,1... | collective-permute-start | bytes 98312 | tf_op jit(solution)/shard_map/ppermute | solution.py:17
  26.7 1.3 %collective-permute-start.1 = (bf16[1,32,512]{2,1,0:T(8,128)(2,1)S(1)}, bf16[1,32,512]{2,1,0:T(8,128)(2,1)S(1)}, u32[]{:S(2)}, u32[]{:S(2)}) collective-permute-start(bf16[1,32,512]{2,1,0:T(8,128)(2,1)S(1)} %get-tuple-element.29), channel_id=1, source_target_pairs={{1,0},{2,1},{3,2},{4,3},{5,4},{6,5},{7,6},{8,7},{9,8},{10,9},{11,1... | collective-permute-start | bytes 98312 | tf_op jit(solution)/shard_map/ppermute | solution.py:19
  28.0 0.8 slice_bitcast_fusion.34
  28.9 0.0 copy-done.1
  28.9 0.0 copy-done.2
  28.9 0.0 copy-done.3
  29.6 0.0 collective-permute-done
  29.6 0.1 collective-permute-done.1
  29.8 0.1 pad_slice_fusion.45
  29.8 0.7 multiply_add_fusion.1
  30.6 0.0 copy-start.4
  30.6 0.7 multiply_add_fusion
  31.3 0.0 copy-done.4
  31.3 2.5 %fusion.150 = (f32[8,2,32,512]{3,2,1,0:T(8,128)S(1)}, bf16[8,2,32,512]{3,2,1,0:T(8,128)(2,1)S(1)}) fusion(f32[8]{0:T(128)S(1)} %copy-done.4, f32[8,2,32,512]{3,2,1,0:T(8,128)S(1)} %multiply_add_fusion.1, f32[8]{0:T(128)S(1)} %get-tuple-element.64, f32[8]{0:T(128)S(1)} %get-tuple-element.65, f32[8]{0:T(128)S(1)} %get-tuple-element.58, ...), kind=kLoop, calls=%fused_computation.255 | loop fusion | flops 7864320 | bytes 2627904 | tf_op jit(solution)/shard_map/convert_element_type | solution.py:44
  33.8 4.1 %collective-permute-start.2 = (bf16[8,1,32,512]{3,2,1,0:T(8,128)(2,1)S(1)}, bf16[8,1,32,512]{3,2,1,0:T(8,128)(2,1)S(1)}, u32[]{:S(2)}, u32[]{:S(2)}) collective-permute-start(bf16[8,1,32,512]{3,2,1,0:T(8,128)(2,1)S(1)} %get-tuple-element.15), channel_id=1, source_target_pairs={{0,1},{1,2},{2,3},{3,4},{4,5},{5,6},{6,7},{7,8},{8,9},{9,10},{10,1... | collective-permute-start | bytes 786440 | tf_op jit(solution)/shard_map/ppermute | solution.py:17
  37.9 1.3 %collective-permute-start.3 = (bf16[8,1,32,512]{3,2,1,0:T(8,128)(2,1)S(1)}, bf16[8,1,32,512]{3,2,1,0:T(8,128)(2,1)S(1)}, u32[]{:S(2)}, u32[]{:S(2)}) collective-permute-start(bf16[8,1,32,512]{3,2,1,0:T(8,128)(2,1)S(1)} %get-tuple-element.14), channel_id=1, source_target_pairs={{1,0},{2,1},{3,2},{4,3},{5,4},{6,5},{7,6},{8,7},{9,8},{10,9},{11,1... | collective-permute-start | bytes 786440 | tf_op jit(solution)/shard_map/ppermute | solution.py:19
  39.2 2.5 %fusion.152 = (f32[8,2,32,512]{3,2,1,0:T(8,128)S(1)}, bf16[8,2,32,512]{3,2,1,0:T(8,128)(2,1)S(1)}) fusion(f32[8]{0:T(128)S(1)} %copy-done.4, f32[8,2,32,512]{3,2,1,0:T(8,128)S(1)} %multiply_add_fusion, f32[8]{0:T(128)S(1)} %get-tuple-element.55, f32[8]{0:T(128)S(1)} %get-tuple-element.56, f32[8]{0:T(128)S(1)} %get-tuple-element.49, ...), kind=kLoop, calls=%fused_computation.256 | loop fusion | flops 7864320 | bytes 2627904 | tf_op jit(solution)/shard_map/convert_element_type | solution.py:44
  41.7 3.0 %collective-permute-start.4 = (bf16[8,1,32,512]{3,2,1,0:T(8,128)(2,1)S(1)}, bf16[8,1,32,512]{3,2,1,0:T(8,128)(2,1)S(1)}, u32[]{:S(2)}, u32[]{:S(2)}) collective-permute-start(bf16[8,1,32,512]{3,2,1,0:T(8,128)(2,1)S(1)} %get-tuple-element.19), channel_id=1, source_target_pairs={{0,1},{1,2},{2,3},{3,4},{4,5},{5,6},{6,7},{7,8},{8,9},{9,10},{10,1... | collective-permute-start | bytes 786440 | tf_op jit(solution)/shard_map/ppermute | solution.py:17
  44.8 1.3 %collective-permute-start.5 = (bf16[8,1,32,512]{3,2,1,0:T(8,128)(2,1)S(1)}, bf16[8,1,32,512]{3,2,1,0:T(8,128)(2,1)S(1)}, u32[]{:S(2)}, u32[]{:S(2)}) collective-permute-start(bf16[8,1,32,512]{3,2,1,0:T(8,128)(2,1)S(1)} %get-tuple-element.18), channel_id=1, source_target_pairs={{1,0},{2,1},{3,2},{4,3},{5,4},{6,5},{7,6},{8,7},{9,8},{10,9},{11,1... | collective-permute-start | bytes 786440 | tf_op jit(solution)/shard_map/ppermute | solution.py:19
  46.1 0.0 collective-permute-done.2
  46.1 0.0 collective-permute-done.3
  46.1 0.1 fusion.135
  46.2 1.6 %fusion.35 = f32[8,2,32,512]{3,2,1,0:T(8,128)S(1)} fusion(f32[8,2,32,512]{3,2,1,0:T(8,128)S(1)} %get-tuple-element.13, f32[8,2,32,512]{3,2,1,0:T(8,128)S(1)} %get-tuple-element.8, f32[8,2,32,512]{3,2,1,0:T(8,128)S(1)} %get-tuple-element.12, f32[8]{0:T(128)S(1)} %get-tuple-element.37, f32[8]{0:T(128)S(1)} %get-tuple-element.38, f32[8]{0:T(128)S(1)} %get-tuple-element.31, ...), kind=kLoop, calls=%fused_computation.80 | loop fusion | flops 4456448 | bytes 4194592 | tf_op jit(solution)/shard_map/add | solution.py:46
  47.8 2.4 %fusion.132 = f32[2,32,512]{2,1,0:T(8,128)S(1)} fusion(f32[8,2,32,512]{3,2,1,0:T(8,128)S(1)} %fusion.35, f32[8]{0:T(128)S(1)} %get-tuple-element.46, f32[8]{0:T(128)S(1)} %get-tuple-element.47, f32[8]{0:T(128)S(1)} %get-tuple-element.40, f32[8]{0:T(128)S(1)} %get-tuple-element.41, f32[8]{0:T(128)S(1)} %get-tuple-element.42, f32[8]{0:T(128)S(1)} %get-tuple-element.43, ...), kind=kLoop, calls=%fused_computation.179 | loop fusion | flops 7045120 | bytes 1186080 | tf_op jit(solution)/shard_map/reduce_sum | solution.py:78
  50.3 0.0 collective-permute-done.4
  50.3 0.0 collective-permute-done.5
  50.3 0.1 fusion.133
  50.4 1.6 %fusion.99 = f32[8,2,32,512]{3,2,1,0:T(8,128)S(1)} fusion(f32[8,2,32,512]{3,2,1,0:T(8,128)S(1)} %get-tuple-element.17, f32[8,2,32,512]{3,2,1,0:T(8,128)S(1)} %get-tuple-element.10, f32[8,2,32,512]{3,2,1,0:T(8,128)S(1)} %get-tuple-element.16, f32[8]{0:T(128)S(1)} %get-tuple-element.46, f32[8]{0:T(128)S(1)} %get-tuple-element.47, f32[8]{0:T(128)S(1)} %get-tuple-element.40, ...), kind=kLoop, calls=%fused_computation.144 | loop fusion | flops 4456448 | bytes 4194592 | tf_op jit(solution)/shard_map/add | solution.py:46
  52.1 2.4 %fusion.131 = f32[2,32,512]{2,1,0:T(8,128)S(1)} fusion(f32[8,2,32,512]{3,2,1,0:T(8,128)S(1)} %fusion.99, f32[8]{0:T(128)S(1)} %get-tuple-element.37, f32[8]{0:T(128)S(1)} %get-tuple-element.38, f32[8]{0:T(128)S(1)} %get-tuple-element.31, f32[8]{0:T(128)S(1)} %get-tuple-element.32, f32[8]{0:T(128)S(1)} %get-tuple-element.33, f32[8]{0:T(128)S(1)} %get-tuple-element.34, ...), kind=kLoop, calls=%fused_computation.178 | loop fusion | flops 7045120 | bytes 1186080 | tf_op jit(solution)/shard_map/reduce_sum | solution.py:78
  54.5 0.1 fusion.149
  54.6 32.9 %pmax.7 = f32[512]{0:T(512)S(1)} all-reduce(f32[512]{0:T(512)S(1)} %get-tuple-element.5), channel_id=1, replica_groups=mesh['groups'=2,'arow'=16] {'arow'}, use_global_device_ids=true, to_apply=%region_3.4 | all-reduce | flops 512 | bytes 4096 | tf_op jit(solution)/shard_map/pmax | solution.py:107
  87.5 0.7 fusion.137
  (13 shorter events, 0.2 us)
Async XLA Ops:
  0.0 24.2 %copy-start = (bf16[2,32,256]{2,1,0:T(8,128)(2,1)S(1)}, bf16[2,32,256]{2,1,0:T(8,128)(2,1)}, u32[]{:S(2)}) copy-start(bf16[2,32,256]{2,1,0:T(8,128)(2,1)} %param.8) | copy-start | bytes 98308
  0.0 28.9 %copy-start.1 = (f32[8,3,3]{0,2,1:T(4,128)S(1)}, f32[8,3,3]{0,2,1:T(4,128)}, u32[]{:S(2)}) copy-start(f32[8,3,3]{0,2,1:T(4,128)} %param.11) | copy-start | bytes 868
  0.0 28.9 %copy-start.2 = (f32[8,3,3]{0,2,1:T(4,128)S(1)}, f32[8,3,3]{0,2,1:T(4,128)}, u32[]{:S(2)}) copy-start(f32[8,3,3]{0,2,1:T(4,128)} %param.13) | copy-start | bytes 868
  0.0 28.9 %copy-start.3 = (f32[8,3,3]{0,2,1:T(4,128)S(1)}, f32[8,3,3]{0,2,1:T(4,128)}, u32[]{:S(2)}) copy-start(f32[8,3,3]{0,2,1:T(4,128)} %param.14) | copy-start | bytes 868
  24.4 5.2 %collective-permute-start = (bf16[1,32,512]{2,1,0:T(8,128)(2,1)S(1)}, bf16[1,32,512]{2,1,0:T(8,128)(2,1)S(1)}, u32[]{:S(2)}, u32[]{:S(2)}) collective-permute-start(bf16[1,32,512]{2,1,0:T(8,128)(2,1)S(1)} %get-tuple-element.28), channel_id=1, source_target_pairs={{0,1},{1,2},{2,3},{3,4},{4,5},{5,6},{6,7},{7,8},{8,9},{9,10},{10,1... | collective-permute-start | bytes 98312 | tf_op jit(solution)/shard_map/ppermute | solution.py:17
  26.7 3.1 %collective-permute-start.1 = (bf16[1,32,512]{2,1,0:T(8,128)(2,1)S(1)}, bf16[1,32,512]{2,1,0:T(8,128)(2,1)S(1)}, u32[]{:S(2)}, u32[]{:S(2)}) collective-permute-start(bf16[1,32,512]{2,1,0:T(8,128)(2,1)S(1)} %get-tuple-element.29), channel_id=1, source_target_pairs={{1,0},{2,1},{3,2},{4,3},{5,4},{6,5},{7,6},{8,7},{9,8},{10,9},{11,1... | collective-permute-start | bytes 98312 | tf_op jit(solution)/shard_map/ppermute | solution.py:19
  30.6 0.7 copy-start.4
  33.8 12.2 %collective-permute-start.2 = (bf16[8,1,32,512]{3,2,1,0:T(8,128)(2,1)S(1)}, bf16[8,1,32,512]{3,2,1,0:T(8,128)(2,1)S(1)}, u32[]{:S(2)}, u32[]{:S(2)}) collective-permute-start(bf16[8,1,32,512]{3,2,1,0:T(8,128)(2,1)S(1)} %get-tuple-element.15), channel_id=1, source_target_pairs={{0,1},{1,2},{2,3},{3,4},{4,5},{5,6},{6,7},{7,8},{8,9},{9,10},{10,1... | collective-permute-start | bytes 786440 | tf_op jit(solution)/shard_map/ppermute | solution.py:17
  37.9 8.2 %collective-permute-start.3 = (bf16[8,1,32,512]{3,2,1,0:T(8,128)(2,1)S(1)}, bf16[8,1,32,512]{3,2,1,0:T(8,128)(2,1)S(1)}, u32[]{:S(2)}, u32[]{:S(2)}) collective-permute-start(bf16[8,1,32,512]{3,2,1,0:T(8,128)(2,1)S(1)} %get-tuple-element.14), channel_id=1, source_target_pairs={{1,0},{2,1},{3,2},{4,3},{5,4},{6,5},{7,6},{8,7},{9,8},{10,9},{11,1... | collective-permute-start | bytes 786440 | tf_op jit(solution)/shard_map/ppermute | solution.py:19
  41.7 8.6 %collective-permute-start.4 = (bf16[8,1,32,512]{3,2,1,0:T(8,128)(2,1)S(1)}, bf16[8,1,32,512]{3,2,1,0:T(8,128)(2,1)S(1)}, u32[]{:S(2)}, u32[]{:S(2)}) collective-permute-start(bf16[8,1,32,512]{3,2,1,0:T(8,128)(2,1)S(1)} %get-tuple-element.19), channel_id=1, source_target_pairs={{0,1},{1,2},{2,3},{3,4},{4,5},{5,6},{6,7},{7,8},{8,9},{9,10},{10,1... | collective-permute-start | bytes 786440 | tf_op jit(solution)/shard_map/ppermute | solution.py:17
  44.8 5.5 %collective-permute-start.5 = (bf16[8,1,32,512]{3,2,1,0:T(8,128)(2,1)S(1)}, bf16[8,1,32,512]{3,2,1,0:T(8,128)(2,1)S(1)}, u32[]{:S(2)}, u32[]{:S(2)}) collective-permute-start(bf16[8,1,32,512]{3,2,1,0:T(8,128)(2,1)S(1)} %get-tuple-element.18), channel_id=1, source_target_pairs={{1,0},{2,1},{3,2},{4,3},{5,4},{6,5},{7,6},{8,7},{9,8},{10,9},{11,1... | collective-permute-start | bytes 786440 | tf_op jit(solution)/shard_map/ppermute | solution.py:19
where the time goes:
time: 88.6 us; the launch traced here: 88.3 us
  blocking collectives  57.1 us (64%)
  other arithmetic  15.6 us (18%)
  starting transfers between devices  13.2 us (15%)
  local copies, waits for them, and re-layouts  1.06 us (1%)
  between operations  0.94 us (1%)
    pmax x1, blocking collectives, on_device(): best_over_a = lax.pmax(jnp.max(score, axis=(0, 1)), 'arow')  32.9 us
    all_gather x1, blocking collectives, on_device(): lax.all_gather(feat_b, 'arow', axis=0, tiled=True).reshape(-1, channels)  24.2 us
    ppermute x3, starting transfers between devices, padded(): lax.ppermute(tail, axis, [(i, (i + 1) % count) for i in range(ends)])  9.37 us
    convert_element_type x6, other arithmetic, conv_a(): row_slab = lax.slice_in_dim(values, row_tap, row_tap + out_rows, axis=val...  5.23 us
    reduce_sum x2, other arithmetic, second_layer(): summed = jnp.sum(conv_b(spread, kern_b, map_width), axis=0)  4.84 us
    add x4, other arithmetic, conv_a(): result + kernel[..., row_tap, col_tap][..., None, None, None] * shifted_z...  4.64 us
    ppermute x3, starting transfers between devices, padded(): lax.ppermute(head, axis, [((i + 1) % count, i) for i in range(ends)])  3.88 us
  transfers between devices with their start and end apart: 6, of which 1 were waited for; matrix products, arithmetic and copies ran while one was open for 9% of the time, Pallas kernels for 0%

commit v1 on v0

--- a/solution.py
+++ b/solution.py
@@ -1,9 +1,15 @@
+import functools
+
 import jax
 import jax.numpy as jnp
 from jax import lax
+from jax.experimental import pallas as pl
+from jax.experimental.pallas import tpu as pltpu
 from jax.sharding import PartitionSpec as P
 
 EPSILON = 1e-05
+F32 = jnp.float32
+BF16 = jnp.bfloat16
 
 
 def padded(cells, sides, width):
@@ -41,7 +47,7 @@
     for row_tap in range(3):
         row_slab = lax.slice_in_dim(
             values, row_tap, row_tap + out_rows, axis=values.ndim - 3
-        ).astype(jnp.float32)
+        ).astype(F32)
         for col_tap in range(3):
             result = result + kernel[..., row_tap, col_tap][..., None, None, None] * shifted_zero(
                 row_slab, values.ndim - 2, col_tap - 1
@@ -58,7 +64,7 @@
                 values, values.ndim - 1, (row_tap - 1) * map_width + (col_tap - 1)
             )
             inside = ((flat_pos + col_tap - 1 >= 0) & (flat_pos + col_tap - 1 < map_width)).astype(
-                jnp.float32
+                F32
             )
             result = result + kernel[..., row_tap, col_tap][..., None, None, None] * (
                 shifted * inside
@@ -69,7 +75,7 @@
 def first_layer(correlation, kern_a, kern_b, bias_one, map_width):
     spread = conv_a(correlation, kern_a)
     return jax.nn.relu(conv_b(spread, kern_b, map_width) + bias_one[:, None, None, None]).astype(
-        jnp.bfloat16
+        BF16
     )
 
 
@@ -79,7 +85,7 @@
     return jax.nn.relu(summed + bias_two[0])
 
 
-def on_device(feat_a, feat_b, a_first, b_first, bias_first, a_second, b_second, bias_second):
+def general(feat_a, feat_b, a_first, b_first, bias_first, a_second, b_second, bias_second):
     map_width = feat_b.shape[1]
     channels = feat_a.shape[2]
     b_cells = feat_b.shape[0] * lax.axis_size("arow") * map_width
@@ -88,11 +94,11 @@
         a_rows,
         lax.all_gather(feat_b, "arow", axis=0, tiled=True).reshape(-1, channels),
         (((1,), (1,)), ((), ())),
-        preferred_element_type=jnp.float32,
+        preferred_element_type=F32,
     )
     correlation = (
         (tile_product * channels ** (-0.5))
-        .astype(jnp.bfloat16)
+        .astype(BF16)
         .reshape(feat_a.shape[0], map_width, b_cells)
     )
     correlation = padded(correlation, (("arow", 0),), 1)
@@ -107,6 +113,310 @@
     best_over_a = lax.pmax(jnp.max(score, axis=(0, 1)), "arow")
     best_over_b = jnp.max(score, axis=2)[..., None]
     return score * (score / (best_over_a + EPSILON)) * (score / (best_over_b + EPSILON))
+
+
+def lane(shape):
+    return lax.broadcasted_iota(jnp.int32, shape, 1)
+
+
+def sublane(shape):
+    return lax.broadcasted_iota(jnp.int32, shape, 0)
+
+
+def two_terms(value):
+    high = value.astype(BF16)
+    return high, (value - high.astype(F32)).astype(BF16)
+
+
+def first_weights(taps, at_ref, k, width):
+    col = lane((width, 128)) % width
+    diag = [sublane((width, 128)) + 1 - col == w for w in range(3)]
+    row = lane((1, 128)) // width
+    for net in range(2):
+        lanes = slice(128 * net, 128 * net + 128)
+        for cr in range(6):
+            block = jnp.zeros((width, 128), F32)
+            for w in range(3):
+                per_lane = jnp.zeros((1, 128), F32)
+                for u in range(3):
+                    if 0 <= cr - u <= 3:
+                        per_lane = jnp.where(row == cr - u, taps[net][k * 9 + 3 * u + w], per_lane)
+                block = jnp.where(diag[w], per_lane, block)
+            high, low = two_terms(block)
+            at_ref[k, cr * width : (cr + 1) * width, lanes] = high
+            at_ref[k, (8 + cr) * width : (9 + cr) * width, lanes] = low
+        for base in (6, 14):
+            at_ref[k, base * width : (base + 2) * width, lanes] = jnp.zeros((2 * width, 128), BF16)
+
+
+def second_weights(taps, at_ref, k, width, keep):
+    col = lane((width, 128)) % width
+    diag = [sublane((width, 128)) + 1 - col == w for w in range(3)]
+    row = lane((1, 128)) // width
+    for net in range(2):
+        for hr in range(4):
+            block = jnp.zeros((width, 128), F32)
+            for w in range(3):
+                per_lane = jnp.zeros((1, 128), F32)
+                for u in range(3):
+                    if 0 <= hr - u <= 1:
+                        tap = taps[net][k * 9 + 3 * u + w]
+                        if hr in keep:
+                            tap = tap * keep[hr]
+                        per_lane = jnp.where(row == 2 * net + hr - u, tap, per_lane)
+                block = jnp.where(diag[w], per_lane, block)
+            high, low = two_terms(block)
+            rows = slice((4 * net + hr) * width, (4 * net + hr + 1) * width)
+            at_ref[k, rows, 0:128] = high
+            at_ref[k, rows, 128:256] = low
+
+
+def b_taps(load, weights, emit, width):
+    top = sublane((8, 128)) == 0
+    bottom = sublane((8, 128)) == 7
+
+    def column(jb):
+        even, odd = load(2 * jb), load(2 * jb + 1)
+        above = jnp.where(top, 0.0, pltpu.roll(odd, 1, 0))
+        below = jnp.where(bottom, 0.0, pltpu.roll(even, 7, 0))
+        return above, even, odd, below
+
+    window = [None, column(0), column(1)]
+    for jb in range(width):
+        sums = []
+        for par in range(2):
+            total = None
+            for t in range(3):
+                if window[t] is None:
+                    continue
+                for s in range(3):
+                    term = weights[3 * s + t] * window[t][par + s]
+                    total = term if total is None else total + term
+            sums.append(total)
+        emit(jb, sums[0], sums[1])
+        window = [window[1], window[2], column(jb + 2) if jb + 2 < width else None]
+
+
+def consensus_kernel(
+    offsets,
+    width,
+    info_ref,
+    a1_ref,
+    b1_ref,
+    bias1_ref,
+    a2_ref,
+    b2_ref,
+    bias2_ref,
+    own_ref,
+    mate_ref,
+    outer_ref,
+    score_ref,
+    part_ref,
+    best_ref,
+    fa_ref,
+    vf_ref,
+    vp_ref,
+    at1_ref,
+    at2_ref,
+    s_ref,
+    h_ref,
+    t_ref,
+    acc_ref,
+    nat_ref,
+):
+    half = len(offsets)
+    channels = own_ref.shape[2]
+    cells = 2 * half * width
+    index = info_ref[0]
+    parity = info_ref[1]
+    keep_low = info_ref[2].astype(F32)
+    keep_high = info_ref[3].astype(F32)
+    first = (a1_ref, b1_ref)
+    second = (a2_ref, b2_ref)
+
+    for k in range(8):
+        first_weights(first, at1_ref, k, width)
+        second_weights(second, at2_ref, k, width, {0: keep_low, 3: keep_high})
+
+    fa_ref[2:4] = own_ref[half : half + 2]
+    fa_ref[pl.ds(4 - 4 * parity, 2)] = mate_ref[half : half + 2]
+    keep_outer = (keep_low * keep_high).astype(BF16)
+    fa_ref[pl.ds(4 * parity, 2)] = outer_ref[...] * keep_outer
+    fa_ref[6:8] = jnp.zeros((2, width, channels), BF16)
+    rows = fa_ref[...].reshape(8 * width, channels)
+
+    for side, ref in enumerate((own_ref, mate_ref)):
+        product = lax.dot_general(
+            ref[0:half].reshape(half * width, channels),
+            rows,
+            (((1,), (1,)), ((), ())),
+            preferred_element_type=F32,
+        )
+        for g in range(half):
+            ib = index ^ (offsets[g] ^ side)
+            start = (ib % 2) * 8 + ib // 2
+            block = product[g * width : (g + 1) * width] * channels ** (-0.5)
+            for c in range(2):
+                vf_ref[c, pl.ds(start, width, stride=16), :] = block[
+                    :, 128 * c : 128 * c + 128
+                ]
+    for c in range(4):
+        vp_ref[:, 128 * c : 128 * c + 128] = vf_ref[c % 2].astype(BF16)
+
+    half_lanes = lane((1, 128)) < 64
+    for k in range(8):
+        s_ref[k % 2] = jnp.dot(vp_ref[...], at1_ref[k], preferred_element_type=F32)
+        for net in range(2):
+            bank = first[1 - net]
+            weights = [bank[k * 9 + tap] for tap in range(9)]
+            bias = bias1_ref[k]
+
+            def load(r, net=net, k=k):
+                return s_ref[k % 2, 8 * r : 8 * r + 8, 128 * net : 128 * net + 128]
+
+            def emit(jb, even, odd, net=net, k=k, bias=bias):
+                pair = jnp.concatenate([even, odd], axis=0)
+                h_ref[k % 2, 16 * jb : 16 * jb + 16, 128 * net : 128 * net + 128] = jnp.maximum(
+                    pair + bias, 0.0
+                ).astype(BF16)
+
+            b_taps(load, weights, emit, width)
+        both = jnp.dot(h_ref[k % 2], at2_ref[k], preferred_element_type=F32)
+        t_ref[k % 2] = both[:, 0:128] + both[:, 128:256]
+        weights = [
+            jnp.where(half_lanes, second[1][k * 9 + tap], second[0][k * 9 + tap])
+            for tap in range(9)
+        ]
+
+        def load(r, k=k):
+            return t_ref[k % 2, 8 * r : 8 * r + 8, :]
+
+        def emit(jb, even, odd, k=k):
+            pair = jnp.concatenate([even, odd], axis=0)
+            if k == 0:
+                acc_ref[16 * jb : 16 * jb + 16, :] = pair
+            elif k < 7:
+                acc_ref[16 * jb : 16 * jb + 16, :] += pair
+            else:
+                total = jnp.maximum(
+                    acc_ref[16 * jb : 16 * jb + 16, :] + pair + bias2_ref[0], 0.0
+                )
+                nat_ref[pl.ds(jb, 8, stride=2 * width), :] = total[0:8]
+                nat_ref[pl.ds(width + jb, 8, stride=2 * width), :] = total[8:16]
+
+        b_taps(load, weights, emit, width)
+
+    turned = jnp.transpose(nat_ref[...], (1, 0))
+    score = turned[0:64] + turned[64:128]
+    best_ref[...] = jnp.max(score, axis=0, keepdims=True)
+    best_b = jnp.max(score, axis=1, keepdims=True)
+    score_ref[...] = score
+    part_ref[...] = score * (score / (best_b + EPSILON))
+
+
+def consensus(info, filters, own, mate, outer, offsets, width):
+    half = len(offsets)
+    cells = 2 * half * width
+    channels = own.shape[2]
+    smem = pl.BlockSpec(memory_space=pltpu.SMEM)
+    vmem = pl.BlockSpec(memory_space=pltpu.VMEM)
+    a1, b1, bias1, a2, b2, bias2 = filters
+    return pl.pallas_call(
+        functools.partial(consensus_kernel, offsets, width),
+        out_shape=(
+            jax.ShapeDtypeStruct((2 * width, cells), F32),
+            jax.ShapeDtypeStruct((2 * width, cells), F32),
+            jax.ShapeDtypeStruct((1, cells), F32),
+        ),
+        in_specs=[smem] * 7 + [vmem] * 3,
+        out_specs=(vmem, vmem, vmem),
+        scratch_shapes=[
+            pltpu.VMEM((8, width, channels), BF16),
+            pltpu.VMEM((2, cells, 128), F32),
+            pltpu.VMEM((cells, 512), BF16),
+            pltpu.VMEM((8, 512, 256), BF16),
+            pltpu.VMEM((8, 256, 256), BF16),
+            pltpu.VMEM((2, cells, 256), F32),
+            pltpu.VMEM((2, cells, 256), BF16),
+            pltpu.VMEM((2, cells, 128), F32),
+            pltpu.VMEM((cells, 128), F32),
+            pltpu.VMEM((cells, 128), F32),
+        ],
+        compiler_params=pltpu.CompilerParams(vmem_limit_bytes=32 << 20),
+    )(
+        info,
+        a1.reshape(-1),
+        b1.reshape(-1),
+        bias1,
+        a2.reshape(-1),
+        b2.reshape(-1),
+        bias2,
+        own,
+        mate,
+        outer,
+    )
+
+
+def exchange(value, mask, count):
+    return lax.ppermute(value, "arow", [(i, i ^ mask) for i in range(count)])
+
+
+def outer_pairs(groups, count):
+    pairs = []
+    for g in range(groups):
+        for i in range(count):
+            j = i + 1 if i % 2 else i - 1
+            if 0 <= j < count:
+                pairs.append((g * count + i, g * count + j))
+            else:
+                other = g ^ 1 if (g ^ 1) < groups else g
+                pairs.append((g * count + i, other * count + i))
+    return pairs
+
+
+def fast(feat_a, feat_b, a_first, b_first, bias_first, a_second, b_second, bias_second):
+    count = lax.axis_size("arow")
+    groups = lax.axis_size("groups")
+    width = feat_b.shape[1]
+    index = lax.axis_index("arow")
+    masks = [(1 << b) | 1 for b in reversed(range(1, count.bit_length() - 1))]
+
+    held, offsets = feat_b, [0]
+    outer = None
+    for n, mask in enumerate(masks):
+        if n == 1:
+            tied, held = lax.optimization_barrier((feat_a, held))
+            outer = lax.ppermute(tied, ("groups", "arow"), outer_pairs(groups, count))
+        held = jnp.concatenate([held, exchange(held, mask, count)], axis=0)
+        offsets = offsets + [o ^ mask for o in offsets]
+    own = jnp.concatenate([held, feat_a], axis=0)
+    mate = exchange(own, 1, count)
+
+    info = jnp.stack(
+        [
+            index,
+            index % 2,
+            (index != 0).astype(jnp.int32),
+            (index != count - 1).astype(jnp.int32),
+        ]
+    ).astype(jnp.int32)
+    filters = (a_first, b_first, bias_first, a_second, b_second, bias_second)
+    score, part, best = consensus(info, filters, own, mate, outer, offsets, width)
+    for mask in masks + [1]:
+        best = jnp.maximum(best, exchange(best, mask, count))
+    out = part * (score / (best + EPSILON))
+    return out.reshape(feat_a.shape[0], width, -1)
+
+
+def on_device(feat_a, feat_b, *filters):
+    count = lax.axis_size("arow")
+    fits = (
+        feat_a.shape == (2, 32, 256)
+        and feat_b.shape == (1, 32, 256)
+        and count == 16
+        and filters[0].shape[0] == 8
+    )
+    return (fast if fits else general)(feat_a, feat_b, *filters)
 
 
 def solution(mesh):

time: 88.6 us -> 40 us (0.45)
  blocking collectives: 57.1 us -> 0 us
  other arithmetic: 15.6 us -> 1.5 us
  waiting for transfers between devices: 0.15 us -> 11.3 us
  Pallas kernels: 0 us -> 8.09 us
  local copies, waits for them, and re-layouts: 1.06 us -> 3.12 us
  starting transfers between devices: 13.2 us -> 14.9 us
    pmax x1 -> x0, blocking collectives: 32.9 us -> none  [on_device(): best_over_a = lax.pmax(jnp.max(score, axis=(0, 1)), 'arow')]
    all_gather x1 -> x0, blocking collectives: 24.2 us -> none  [on_device(): lax.all_gather(feat_b, 'arow', axis=0, tiled=True).reshape(-1, channels)]
    ppermute x6 -> x9, waiting for transfers between devices: 0.15 us -> 11.3 us  [the longest x8 11.3 us: exchange(): return lax.ppermute(value, 'arow', [(i, i ^ mask) for i in range(count)])]
    pallas_call x0 -> x1, Pallas kernels: none -> 8.09 us  [consensus(): pl.pallas_call(functools.partial(consensus_kernel, offsets, width), out_s...]
    convert_element_type x8 -> x0, other arithmetic: 5.25 us -> none  [the longest x6 5.23 us: conv_a(): row_slab = lax.slice_in_dim(values, row_tap, row_tap + out_rows, axis=val...]
    reduce_sum x2 -> x0, other arithmetic: 4.84 us -> none  [second_layer(): summed = jnp.sum(conv_b(spread, kern_b, map_width), axis=0)]
    add x6 -> x1, other arithmetic: 4.65 us -> 0.01 us  [fast(): out = part * (score / (best + EPSILON))]
    unnamed x10 -> x19, local copies, waits for them, and re-layouts: 0.02 us -> 2.72 us
  transfers between devices with their start and end apart: 6 -> 9, of which waited for: 1 -> 7; matrix products, arithmetic and copies ran while one was open for 9% -> 2% of each run, Pallas kernels for 0% -> 0%
where the time goes in v1:
time: 40 us; the launch traced here: 39.6 us
  starting transfers between devices  14.9 us (37%)
  waiting for transfers between devices  11.3 us (28%)
  Pallas kernels  8.09 us (20%)
  local copies, waits for them, and re-layouts  3.12 us (8%)
  other arithmetic  1.5 us (4%)
  between operations  0.72 us (2%)
    ppermute x8, starting transfers between devices, exchange(): return lax.ppermute(value, 'arow', [(i, i ^ mask) for i in range(count)])  12.8 us
    ppermute x8, waiting for transfers between devices, exchange(): return lax.ppermute(value, 'arow', [(i, i ^ mask) for i in range(count)])  11.3 us
    pallas_call x1, Pallas kernels, consensus(): pl.pallas_call(functools.partial(consensus_kernel, offsets, width), out_s...  8.09 us
    unnamed x19, local copies, waits for them, and re-layouts  2.72 us
    ppermute x1, starting transfers between devices, fast(): outer = lax.ppermute(tied, ('groups', 'arow'), outer_pairs(groups, count))  2.02 us
  transfers between devices with their start and end apart: 9, of which 7 were waited for; matrix products, arithmetic and copies ran while one was open for 2% of the time, Pallas kernels for 0%

profile of v1, /device:TPU:0, one launch (start us, length us, event | category | flops | bytes accessed | tf_op | source)
XLA Modules:
  0.0 39.6 jit_solution(11385471383055294884)
XLA Ops:
  0.0 3.5 %collective-permute-start = (bf16[1,32,256]{2,1,0:T(8,128)(2,1)}, bf16[1,32,256]{2,1,0:T(8,128)(2,1)S(1)}, u32[]{:S(2)}, u32[]{:S(2)}) collective-permute-start(bf16[1,32,256]{2,1,0:T(8,128)(2,1)} %param.9), channel_id=1, source_target_pairs={{0,9},{1,8},{2,11},{3,10},{4,13},{5,12},{6,15},{7,14},{8,1},{9,0},... | collective-permute-start | bytes 49160 | tf_op jit(solution)/shard_map/ppermute | solution.py:361
  3.5 1.7 %collective-permute-done = bf16[1,32,256]{2,1,0:T(8,128)(2,1)S(1)} collective-permute-done((bf16[1,32,256]{2,1,0:T(8,128)(2,1)}, bf16[1,32,256]{2,1,0:T(8,128)(2,1)S(1)}, u32[]{:S(2)}, u32[]{:S(2)}) %collective-permute-start) | collective-permute-done | bytes 16416 | tf_op jit(solution)/shard_map/ppermute | solution.py:361
  5.1 0.7 %pad_maximum_fusion.1 = bf16[2,32,256]{2,1,0:T(8,128)(2,1)S(1)} fusion(bf16[1,32,256]{2,1,0:T(8,128)(2,1)S(1)} %collective-permute-done, bf16[1,32,256]{2,1,0:T(8,128)(2,1)} %param.9), kind=kLoop, calls=%fused_computation.2 | loop fusion | flops 16384 | bytes 65536 | tf_op jit(solution)/shard_map/concatenate | solution.py:390
  5.9 1.9 %collective-permute-start.1 = (bf16[2,32,256]{2,1,0:T(8,128)(2,1)S(1)}, bf16[2,32,256]{2,1,0:T(8,128)(2,1)S(1)}, u32[]{:S(2)}, u32[]{:S(2)}) collective-permute-start(bf16[2,32,256]{2,1,0:T(8,128)(2,1)S(1)} %pad_maximum_fusion.1), channel_id=1, source_target_pairs={{0,5},{1,4},{2,7},{3,6},{4,1},{5,0},{6,3},{7,2},{8,13},{9,12},{10,... | collective-permute-start | bytes 98312 | tf_op jit(solution)/shard_map/ppermute | solution.py:361
  7.7 1.6 %collective-permute-done.1 = bf16[2,32,256]{2,1,0:T(8,128)(2,1)S(1)} collective-permute-done((bf16[2,32,256]{2,1,0:T(8,128)(2,1)S(1)}, bf16[2,32,256]{2,1,0:T(8,128)(2,1)S(1)}, u32[]{:S(2)}, u32[]{:S(2)}) %collective-permute-start.1) | collective-permute-done | bytes 32800 | tf_op jit(solution)/shard_map/ppermute | solution.py:361
  9.3 1.8 %collective-permute-start.2 = (bf16[4,32,256]{2,1,0:T(8,128)(2,1)S(1)}, bf16[4,32,256]{2,1,0:T(8,128)(2,1)S(1)}, u32[]{:S(2)}, u32[]{:S(2)}) collective-permute-start(bf16[4,32,256]{2,1,0:T(8,128)(2,1)S(1)} %pad_maximum_fusion), channel_id=1, source_target_pairs={{0,3},{1,2},{2,1},{3,0},{4,7},{5,6},{6,5},{7,4},{8,11},{9,10},{10,... | collective-permute-start | bytes 196616 | tf_op jit(solution)/shard_map/ppermute | solution.py:361
  11.1 0.0 copy-start.1
  11.1 2.2 %collective-permute-done.2 = bf16[4,32,256]{2,1,0:T(8,128)(2,1)S(1)} collective-permute-done((bf16[4,32,256]{2,1,0:T(8,128)(2,1)S(1)}, bf16[4,32,256]{2,1,0:T(8,128)(2,1)S(1)}, u32[]{:S(2)}, u32[]{:S(2)}) %collective-permute-start.2) | collective-permute-done | bytes 65568 | tf_op jit(solution)/shard_map/ppermute | solution.py:361
  13.3 0.0 copy-done.1
  13.3 0.4 collective-permute-start.3
  13.7 0.0 copy-start.2
  13.7 2.0 %collective-permute-start.4 = (bf16[2,32,256]{2,1,0:T(8,128)(2,1)S(1)}, bf16[2,32,256]{2,1,0:T(8,128)(2,1)S(1)}, u32[]{:S(2)}, u32[]{:S(2)}) collective-permute-start(bf16[2,32,256]{2,1,0:T(8,128)(2,1)S(1)} %copy-done.1), channel_id=1, source_target_pairs={{0,16},{1,2},{2,1},{3,4},{4,3},{5,6},{6,5},{7,8},{8,7},{9,10},{10,... | collective-permute-start | bytes 98312 | tf_op jit(solution)/shard_map/ppermute | solution.py:389
  15.7 0.1 pad_add_fusion.info_ref
  16.5 0.0 copy-done.2
  16.5 0.1 copy.13
  16.6 0.0 copy-start.3
  16.6 0.1 reshape.15.a1_ref
  16.7 0.6 %copy-done.3 = f32[8,3,3]{0,2,1:T(4,128)S(1)} copy-done((f32[8,3,3]{0,2,1:T(4,128)S(1)}, f32[8,3,3]{0,2,1:T(4,128)}, u32[]{:S(2)}) %copy-start.3) | copy-done | bytes 312
  17.3 0.1 copy.14
  17.4 0.0 copy-start.4
  17.4 0.1 reshape.16.b1_ref
  17.5 0.6 %copy-done.4 = f32[8,3,3]{0,2,1:T(4,128)S(1)} copy-done((f32[8,3,3]{0,2,1:T(4,128)S(1)}, f32[8,3,3]{0,2,1:T(4,128)}, u32[]{:S(2)}) %copy-start.4) | copy-done | bytes 312
  18.1 0.1 copy.15
  18.2 0.0 copy-start.5
  18.2 0.1 reshape.17.a2_ref
  18.3 0.6 %copy-done.5 = f32[8,3,3]{0,2,1:T(4,128)S(1)} copy-done((f32[8,3,3]{0,2,1:T(4,128)S(1)}, f32[8,3,3]{0,2,1:T(4,128)}, u32[]{:S(2)}) %copy-start.5) | copy-done | bytes 312
  18.9 0.1 copy.16
  19.0 0.0 copy-start
  19.0 0.1 reshape.18.b2_ref
  19.1 0.0 collective-permute-done.4.outer_ref
  19.1 0.0 collective-permute-done.3.mate_ref
  19.1 0.5 %copy-done = f32[8]{0:T(128)S(1)} copy-done((f32[8]{0:T(128)S(1)}, f32[8]{0:T(128)}, u32[]{:S(2)}) %copy-start) | copy-done | bytes 56
  19.6 8.1 %shard_map.82 = (f32[64,512]{1,0:T(8,128)S(1)}, f32[64,512]{1,0:T(8,128)S(1)}, f32[1,512]{1,0:T(1,128)S(1)}) custom-call(s32[4]{0:T(128)S(1)} %pad_add_fusion.info_ref, f32[72]{0:T(128)S(1)} %reshape.15.a1_ref, f32[72]{0:T(128)S(1)} %reshape.16.b1_ref, f32[8]{0:T(128)S(1)} %copy-done, f32[72]{0:T(128)S(1)} %reshape.17.a2_ref, f32[72]{0:T(128)S(1)} %reshape.18.b2_ref, ...), custom_call_target="tpu_custom_call" | custom-call | tf_op jit(solution)/shard_map/pallas_call | solution.py:324
  27.7 2.5 %collective-permute-start.5 = (f32[1,512]{1,0:T(1,128)S(1)}, f32[1,512]{1,0:T(1,128)S(1)}, u32[]{:S(2)}, u32[]{:S(2)}) collective-permute-start(f32[1,512]{1,0:T(1,128)S(1)} %get-tuple-element.14), channel_id=1, source_target_pairs={{0,9},{1,8},{2,11},{3,10},{4,13},{5,12},{6,15},{7,14},{8,1},{9,0},... | collective-permute-start | bytes 6152 | tf_op jit(solution)/shard_map/ppermute | solution.py:361
  30.2 1.5 %collective-permute-done.5 = f32[1,512]{1,0:T(1,128)S(1)} collective-permute-done((f32[1,512]{1,0:T(1,128)S(1)}, f32[1,512]{1,0:T(1,128)S(1)}, u32[]{:S(2)}, u32[]{:S(2)}) %collective-permute-start.5) | collective-permute-done | bytes 2080 | tf_op jit(solution)/shard_map/ppermute | solution.py:361
  31.7 1.4 %collective-permute-start.6 = (f32[1,512]{1,0:T(1,128)S(1)}, f32[1,512]{1,0:T(1,128)S(1)}, u32[]{:S(2)}, u32[]{:S(2)}) collective-permute-start(f32[1,512]{1,0:T(1,128)S(1)} %max.12), channel_id=1, source_target_pairs={{0,5},{1,4},{2,7},{3,6},{4,1},{5,0},{6,3},{7,2},{8,13},{9,12},{10,... | collective-permute-start | bytes 6152 | tf_op jit(solution)/shard_map/ppermute | solution.py:361
  33.1 1.7 %collective-permute-done.6 = f32[1,512]{1,0:T(1,128)S(1)} collective-permute-done((f32[1,512]{1,0:T(1,128)S(1)}, f32[1,512]{1,0:T(1,128)S(1)}, u32[]{:S(2)}, u32[]{:S(2)}) %collective-permute-start.6) | collective-permute-done | bytes 2080 | tf_op jit(solution)/shard_map/ppermute | solution.py:361
  34.7 1.4 %collective-permute-start.7 = (f32[1,512]{1,0:T(1,128)S(1)}, f32[1,512]{1,0:T(1,128)S(1)}, u32[]{:S(2)}, u32[]{:S(2)}) collective-permute-start(f32[1,512]{1,0:T(1,128)S(1)} %max.13), channel_id=1, source_target_pairs={{0,3},{1,2},{2,1},{3,0},{4,7},{5,6},{6,5},{7,4},{8,11},{9,10},{10,... | collective-permute-start | bytes 6152 | tf_op jit(solution)/shard_map/ppermute | solution.py:361
  36.1 1.6 %collective-permute-done.7 = f32[1,512]{1,0:T(1,128)S(1)} collective-permute-done((f32[1,512]{1,0:T(1,128)S(1)}, f32[1,512]{1,0:T(1,128)S(1)}, u32[]{:S(2)}, u32[]{:S(2)}) %collective-permute-start.7) | collective-permute-done | bytes 2080 | tf_op jit(solution)/shard_map/ppermute | solution.py:361
  37.7 0.1 collective-permute-start.8
  37.8 1.0 %collective-permute-done.8 = f32[1,512]{1,0:T(1,128)S(1)} collective-permute-done((f32[1,512]{1,0:T(1,128)S(1)}, f32[1,512]{1,0:T(1,128)S(1)}, u32[]{:S(2)}, u32[]{:S(2)}) %collective-permute-start.8) | collective-permute-done | bytes 2080 | tf_op jit(solution)/shard_map/ppermute | solution.py:361
  38.9 0.7 %divide_multiply_fusion = f32[64,512]{1,0:T(8,128)} fusion(f32[64,512]{1,0:T(8,128)S(1)} %get-tuple-element.12, f32[64,512]{1,0:T(8,128)S(1)} %get-tuple-element.13, f32[512]{0:T(512)S(1)} %bitcast.6), kind=kLoop, calls=%fused_computation | loop fusion | flops 65536 | bytes 395264 | tf_op jit(solution)/shard_map/mul | solution.py:407
  (9 shorter events, 0.0 us)
Async XLA Ops:
  0.0 5.1 %collective-permute-start = (bf16[1,32,256]{2,1,0:T(8,128)(2,1)}, bf16[1,32,256]{2,1,0:T(8,128)(2,1)S(1)}, u32[]{:S(2)}, u32[]{:S(2)}) collective-permute-start(bf16[1,32,256]{2,1,0:T(8,128)(2,1)} %param.9), channel_id=1, source_target_pairs={{0,9},{1,8},{2,11},{3,10},{4,13},{5,12},{6,15},{7,14},{8,1},{9,0},... | collective-permute-start | bytes 49160 | tf_op jit(solution)/shard_map/ppermute | solution.py:361
  5.9 3.5 %collective-permute-start.1 = (bf16[2,32,256]{2,1,0:T(8,128)(2,1)S(1)}, bf16[2,32,256]{2,1,0:T(8,128)(2,1)S(1)}, u32[]{:S(2)}, u32[]{:S(2)}) collective-permute-start(bf16[2,32,256]{2,1,0:T(8,128)(2,1)S(1)} %pad_maximum_fusion.1), channel_id=1, source_target_pairs={{0,5},{1,4},{2,7},{3,6},{4,1},{5,0},{6,3},{7,2},{8,13},{9,12},{10,... | collective-permute-start | bytes 98312 | tf_op jit(solution)/shard_map/ppermute | solution.py:361
  9.3 4.0 %collective-permute-start.2 = (bf16[4,32,256]{2,1,0:T(8,128)(2,1)S(1)}, bf16[4,32,256]{2,1,0:T(8,128)(2,1)S(1)}, u32[]{:S(2)}, u32[]{:S(2)}) collective-permute-start(bf16[4,32,256]{2,1,0:T(8,128)(2,1)S(1)} %pad_maximum_fusion), channel_id=1, source_target_pairs={{0,3},{1,2},{2,1},{3,0},{4,7},{5,6},{6,5},{7,4},{8,11},{9,10},{10,... | collective-permute-start | bytes 196616 | tf_op jit(solution)/shard_map/ppermute | solution.py:361
  11.1 2.2 %copy-start.1 = (bf16[2,32,256]{2,1,0:T(8,128)(2,1)S(1)}, bf16[2,32,256]{2,1,0:T(8,128)(2,1)}, u32[]{:S(2)}) copy-start(bf16[2,32,256]{2,1,0:T(8,128)(2,1)} %param.8) | copy-start | bytes 98308
  13.3 5.7 %collective-permute-start.3 = (bf16[10,32,256]{2,1,0:T(8,128)(2,1)S(1)}, bf16[10,32,256]{2,1,0:T(8,128)(2,1)S(1)}, u32[]{:S(2)}, u32[]{:S(2)}) collective-permute-start(bf16[10,32,256]{2,1,0:T(8,128)(2,1)S(1)} %constant_dynamic-update-slice_fusion.own_ref), channel_id=1, source_target_pairs={{0,1},{1,0},{2,3},{3,2},{4,5},{5,4},{6,7},{7,6},{8,9},{9,8},{10,11... | collective-permute-start | bytes 491528 | tf_op jit(solution)/shard_map/ppermute | solution.py:361
  13.7 2.8 %copy-start.2 = (f32[8,3,3]{0,2,1:T(4,128)S(1)}, f32[8,3,3]{0,2,1:T(4,128)}, u32[]{:S(2)}) copy-start(f32[8,3,3]{0,2,1:T(4,128)} %param.10) | copy-start | bytes 868
  13.7 5.3 %collective-permute-start.4 = (bf16[2,32,256]{2,1,0:T(8,128)(2,1)S(1)}, bf16[2,32,256]{2,1,0:T(8,128)(2,1)S(1)}, u32[]{:S(2)}, u32[]{:S(2)}) collective-permute-start(bf16[2,32,256]{2,1,0:T(8,128)(2,1)S(1)} %copy-done.1), channel_id=1, source_target_pairs={{0,16},{1,2},{2,1},{3,4},{4,3},{5,6},{6,5},{7,8},{8,7},{9,10},{10,... | collective-permute-start | bytes 98312 | tf_op jit(solution)/shard_map/ppermute | solution.py:389
  16.6 0.7 %copy-start.3 = (f32[8,3,3]{0,2,1:T(4,128)S(1)}, f32[8,3,3]{0,2,1:T(4,128)}, u32[]{:S(2)}) copy-start(f32[8,3,3]{0,2,1:T(4,128)} %param.11) | copy-start | bytes 868
  17.4 0.7 %copy-start.4 = (f32[8,3,3]{0,2,1:T(4,128)S(1)}, f32[8,3,3]{0,2,1:T(4,128)}, u32[]{:S(2)}) copy-start(f32[8,3,3]{0,2,1:T(4,128)} %param.13) | copy-start | bytes 868
  18.2 0.7 %copy-start.5 = (f32[8,3,3]{0,2,1:T(4,128)S(1)}, f32[8,3,3]{0,2,1:T(4,128)}, u32[]{:S(2)}) copy-start(f32[8,3,3]{0,2,1:T(4,128)} %param.14) | copy-start | bytes 868
  19.0 0.7 %copy-start = (f32[8]{0:T(128)S(1)}, f32[8]{0:T(128)}, u32[]{:S(2)}) copy-start(f32[8]{0:T(128)} %bias1_ref.1) | copy-start | bytes 100
  27.7 4.0 %collective-permute-start.5 = (f32[1,512]{1,0:T(1,128)S(1)}, f32[1,512]{1,0:T(1,128)S(1)}, u32[]{:S(2)}, u32[]{:S(2)}) collective-permute-start(f32[1,512]{1,0:T(1,128)S(1)} %get-tuple-element.14), channel_id=1, source_target_pairs={{0,9},{1,8},{2,11},{3,10},{4,13},{5,12},{6,15},{7,14},{8,1},{9,0},... | collective-permute-start | bytes 6152 | tf_op jit(solution)/shard_map/ppermute | solution.py:361
  31.7 3.0 %collective-permute-start.6 = (f32[1,512]{1,0:T(1,128)S(1)}, f32[1,512]{1,0:T(1,128)S(1)}, u32[]{:S(2)}, u32[]{:S(2)}) collective-permute-start(f32[1,512]{1,0:T(1,128)S(1)} %max.12), channel_id=1, source_target_pairs={{0,5},{1,4},{2,7},{3,6},{4,1},{5,0},{6,3},{7,2},{8,13},{9,12},{10,... | collective-permute-start | bytes 6152 | tf_op jit(solution)/shard_map/ppermute | solution.py:361
  34.7 3.0 %collective-permute-start.7 = (f32[1,512]{1,0:T(1,128)S(1)}, f32[1,512]{1,0:T(1,128)S(1)}, u32[]{:S(2)}, u32[]{:S(2)}) collective-permute-start(f32[1,512]{1,0:T(1,128)S(1)} %max.13), channel_id=1, source_target_pairs={{0,3},{1,2},{2,1},{3,0},{4,7},{5,6},{6,5},{7,4},{8,11},{9,10},{10,... | collective-permute-start | bytes 6152 | tf_op jit(solution)/shard_map/ppermute | solution.py:361
  37.7 1.2 %collective-permute-start.8 = (f32[1,512]{1,0:T(1,128)S(1)}, f32[1,512]{1,0:T(1,128)S(1)}, u32[]{:S(2)}, u32[]{:S(2)}) collective-permute-start(f32[1,512]{1,0:T(1,128)S(1)} %max.14), channel_id=1, source_target_pairs={{0,1},{1,0},{2,3},{3,2},{4,5},{5,4},{6,7},{7,6},{8,9},{9,8},{10,11... | collective-permute-start | bytes 6152 | tf_op jit(solution)/shard_map/ppermute | solution.py:361

commit v2 on v1

--- a/solution.py
+++ b/solution.py
@@ -140,7 +140,7 @@
                 per_lane = jnp.zeros((1, 128), F32)
                 for u in range(3):
                     if 0 <= cr - u <= 3:
-                        per_lane = jnp.where(row == cr - u, taps[net][k * 9 + 3 * u + w], per_lane)
+                        per_lane = jnp.where(row == cr - u, taps[net](u, w, k), per_lane)
                 block = jnp.where(diag[w], per_lane, block)
             high, low = two_terms(block)
             at_ref[k, cr * width : (cr + 1) * width, lanes] = high
@@ -160,7 +160,7 @@
                 per_lane = jnp.zeros((1, 128), F32)
                 for u in range(3):
                     if 0 <= hr - u <= 1:
-                        tap = taps[net][k * 9 + 3 * u + w]
+                        tap = taps[net](u, w, k)
                         if hr in keep:
                             tap = tap * keep[hr]
                         per_lane = jnp.where(row == 2 * net + hr - u, tap, per_lane)
@@ -197,16 +197,65 @@
         window = [window[1], window[2], column(jb + 2) if jb + 2 < width else None]
 
 
+def prepare_kernel(width, packed_ref, at1_ref, at2_ref, w1_ref, w2_ref):
+    index = lax.axis_index("arow")
+    keep = {
+        0: (index != 0).astype(F32),
+        3: (index != lax.axis_size("arow") - 1).astype(F32),
+    }
+
+    def bank(n):
+        return lambda u, w, k: packed_ref[3 * n + u, w, k]
+
+    first = (bank(0), bank(1))
+    second = (bank(2), bank(3))
+    half_lanes = lane((1, 128)) < 64
+    for k in range(8):
+        first_weights(first, at1_ref, k, width)
+        second_weights(second, at2_ref, k, width, keep)
+        for tap in range(9):
+            at = (tap // 3, tap % 3, k)
+            for net in range(2):
+                w1_ref[2 * k + net, tap : tap + 1] = jnp.full((1, 128), first[1 - net](*at), F32)
+            w2_ref[k, tap : tap + 1] = jnp.where(half_lanes, second[1](*at), second[0](*at))
+        for net in range(2):
+            w1_ref[2 * k + net, 9:10] = jnp.full((1, 128), packed_ref[12, 0, k], F32)
+
+
+def pack(bias, *banks):
+    packed = jnp.pad(bias.reshape(1, 1, 8), ((12, 0), (0, 2), (0, 0)))
+    for n, f in enumerate(banks):
+        packed += jnp.pad(f.transpose(1, 2, 0), ((3 * n, 10 - 3 * n), (0, 0), (0, 0)))
+    return packed
+
+
+def prepare(packed, width):
+    vmem = pl.BlockSpec(memory_space=pltpu.VMEM)
+    return pl.pallas_call(
+        functools.partial(prepare_kernel, width),
+        out_shape=(
+            jax.ShapeDtypeStruct((8, 512, 256), BF16),
+            jax.ShapeDtypeStruct((8, 256, 256), BF16),
+            jax.ShapeDtypeStruct((16, 16, 128), F32),
+            jax.ShapeDtypeStruct((8, 16, 128), F32),
+        ),
+        in_specs=[pl.BlockSpec(memory_space=pltpu.SMEM)],
+        out_specs=(vmem,) * 4,
+        compiler_params=pltpu.CompilerParams(vmem_limit_bytes=16 << 20),
+        cost_estimate=pl.CostEstimate(
+            flops=4_000_000, bytes_accessed=3_500_000, transcendentals=0
+        ),
+    )(packed)
+
+
 def consensus_kernel(
     offsets,
     width,
-    info_ref,
-    a1_ref,
-    b1_ref,
-    bias1_ref,
-    a2_ref,
-    b2_ref,
     bias2_ref,
+    at1_ref,
+    at2_ref,
+    w1_ref,
+    w2_ref,
     own_ref,
     mate_ref,
     outer_ref,
@@ -216,8 +265,6 @@
     fa_ref,
     vf_ref,
     vp_ref,
-    at1_ref,
-    at2_ref,
     s_ref,
     h_ref,
     t_ref,
@@ -226,22 +273,13 @@
 ):
     half = len(offsets)
     channels = own_ref.shape[2]
-    cells = 2 * half * width
-    index = info_ref[0]
-    parity = info_ref[1]
-    keep_low = info_ref[2].astype(F32)
-    keep_high = info_ref[3].astype(F32)
-    first = (a1_ref, b1_ref)
-    second = (a2_ref, b2_ref)
-
-    for k in range(8):
-        first_weights(first, at1_ref, k, width)
-        second_weights(second, at2_ref, k, width, {0: keep_low, 3: keep_high})
+    index = lax.axis_index("arow")
+    parity = index % 2
+    inside = jnp.logical_and(index != 0, index != lax.axis_size("arow") - 1)
 
     fa_ref[2:4] = own_ref[half : half + 2]
     fa_ref[pl.ds(4 - 4 * parity, 2)] = mate_ref[half : half + 2]
-    keep_outer = (keep_low * keep_high).astype(BF16)
-    fa_ref[pl.ds(4 * parity, 2)] = outer_ref[...] * keep_outer
+    fa_ref[pl.ds(4 * parity, 2)] = outer_ref[...] * inside.astype(BF16)
     fa_ref[6:8] = jnp.zeros((2, width, channels), BF16)
     rows = fa_ref[...].reshape(8 * width, channels)
 
@@ -263,13 +301,11 @@
     for c in range(4):
         vp_ref[:, 128 * c : 128 * c + 128] = vf_ref[c % 2].astype(BF16)
 
-    half_lanes = lane((1, 128)) < 64
     for k in range(8):
         s_ref[k % 2] = jnp.dot(vp_ref[...], at1_ref[k], preferred_element_type=F32)
         for net in range(2):
-            bank = first[1 - net]
-            weights = [bank[k * 9 + tap] for tap in range(9)]
-            bias = bias1_ref[k]
+            weights = [w1_ref[2 * k + net, tap : tap + 1] for tap in range(9)]
+            bias = w1_ref[2 * k + net, 9:10]
 
             def load(r, net=net, k=k):
                 return s_ref[k % 2, 8 * r : 8 * r + 8, 128 * net : 128 * net + 128]
@@ -283,10 +319,7 @@
             b_taps(load, weights, emit, width)
         both = jnp.dot(h_ref[k % 2], at2_ref[k], preferred_element_type=F32)
         t_ref[k % 2] = both[:, 0:128] + both[:, 128:256]
-        weights = [
-            jnp.where(half_lanes, second[1][k * 9 + tap], second[0][k * 9 + tap])
-            for tap in range(9)
-        ]
+        weights = [w2_ref[k, tap : tap + 1] for tap in range(9)]
 
         def load(r, k=k):
             return t_ref[k % 2, 8 * r : 8 * r + 8, :]
@@ -314,13 +347,11 @@
     part_ref[...] = score * (score / (best_b + EPSILON))
 
 
-def consensus(info, filters, own, mate, outer, offsets, width):
+def consensus(bias_second, weights, own, mate, outer, offsets, width):
     half = len(offsets)
     cells = 2 * half * width
     channels = own.shape[2]
-    smem = pl.BlockSpec(memory_space=pltpu.SMEM)
     vmem = pl.BlockSpec(memory_space=pltpu.VMEM)
-    a1, b1, bias1, a2, b2, bias2 = filters
     return pl.pallas_call(
         functools.partial(consensus_kernel, offsets, width),
         out_shape=(
@@ -328,14 +359,12 @@
             jax.ShapeDtypeStruct((2 * width, cells), F32),
             jax.ShapeDtypeStruct((1, cells), F32),
         ),
-        in_specs=[smem] * 7 + [vmem] * 3,
+        in_specs=[pl.BlockSpec(memory_space=pltpu.SMEM)] + [vmem] * 7,
         out_specs=(vmem, vmem, vmem),
         scratch_shapes=[
             pltpu.VMEM((8, width, channels), BF16),
             pltpu.VMEM((2, cells, 128), F32),
             pltpu.VMEM((cells, 512), BF16),
-            pltpu.VMEM((8, 512, 256), BF16),
-            pltpu.VMEM((8, 256, 256), BF16),
             pltpu.VMEM((2, cells, 256), F32),
             pltpu.VMEM((2, cells, 256), BF16),
             pltpu.VMEM((2, cells, 128), F32),
@@ -343,18 +372,10 @@
             pltpu.VMEM((cells, 128), F32),
         ],
         compiler_params=pltpu.CompilerParams(vmem_limit_bytes=32 << 20),
-    )(
-        info,
-        a1.reshape(-1),
-        b1.reshape(-1),
-        bias1,
-        a2.reshape(-1),
-        b2.reshape(-1),
-        bias2,
-        own,
-        mate,
-        outer,
-    )
+        cost_estimate=pl.CostEstimate(
+            flops=2_000_000_000, bytes_accessed=4_500_000, transcendentals=0
+        ),
+    )(bias_second, *weights, own, mate, outer)
 
 
 def exchange(value, mask, count):
@@ -378,30 +399,28 @@
     count = lax.axis_size("arow")
     groups = lax.axis_size("groups")
     width = feat_b.shape[1]
-    index = lax.axis_index("arow")
     masks = [(1 << b) | 1 for b in reversed(range(1, count.bit_length() - 1))]
 
+    rows = feat_a.shape[0]
+    near = lax.optimization_barrier(jnp.concatenate([feat_a, feat_b], axis=0))
+    near_a, near_b = near[:rows], near[rows:]
+    packed = pack(bias_first, a_first, b_first, a_second, b_second)
     held, offsets = feat_b, [0]
-    outer = None
     for n, mask in enumerate(masks):
         if n == 1:
-            tied, held = lax.optimization_barrier((feat_a, held))
-            outer = lax.ppermute(tied, ("groups", "arow"), outer_pairs(groups, count))
-        held = jnp.concatenate([held, exchange(held, mask, count)], axis=0)
+            held, packed = lax.optimization_barrier((held, packed))
+            weights = prepare(packed, width)
+        if n == 2:
+            feat_a, held, weights = lax.optimization_barrier((feat_a, held, weights))
+            outer = lax.ppermute(feat_a, ("groups", "arow"), outer_pairs(groups, count))
+        received = exchange(held, mask, count)
+        held = jnp.concatenate([near_b if n == 0 else held, received], axis=0)
         offsets = offsets + [o ^ mask for o in offsets]
-    own = jnp.concatenate([held, feat_a], axis=0)
+    held, outer, bias_second = lax.optimization_barrier((held, outer, bias_second))
+    own = jnp.concatenate([held, near_a], axis=0)
     mate = exchange(own, 1, count)
 
-    info = jnp.stack(
-        [
-            index,
-            index % 2,
-            (index != 0).astype(jnp.int32),
-            (index != count - 1).astype(jnp.int32),
-        ]
-    ).astype(jnp.int32)
-    filters = (a_first, b_first, bias_first, a_second, b_second, bias_second)
-    score, part, best = consensus(info, filters, own, mate, outer, offsets, width)
+    score, part, best = consensus(bias_second, weights, own, mate, outer, offsets, width)
     for mask in masks + [1]:
         best = jnp.maximum(best, exchange(best, mask, count))
     out = part * (score / (best + EPSILON))

time: 40 us -> 35.2 us (0.88)
  local copies, waits for them, and re-layouts: 3.12 us -> 0.01 us
  starting transfers between devices: 14.9 us -> 13.6 us
  waiting for transfers between devices: 11.3 us -> 10 us
  other arithmetic: 1.5 us -> 2.27 us
    ppermute x8, waiting for transfers between devices: 11.3 us -> 8.28 us  [exchange(): return lax.ppermute(value, 'arow', [(i, i ^ mask) for i in range(count)])]
    unnamed x19 -> x0, local copies, waits for them, and re-layouts: 2.72 us -> none
    pallas_call x0 -> x1, Pallas kernels: none -> 1.91 us  [prepare(): pl.pallas_call(functools.partial(prepare_kernel, width), out_shape=(jax.S...]
    ppermute x1, waiting for transfers between devices: 0.01 us -> 1.72 us  [fast(): outer = lax.ppermute(feat_a, ('groups', 'arow'), outer_pairs(groups, count))]
    pallas_call x1, Pallas kernels: 8.09 us -> 6.43 us  [consensus(): pl.pallas_call(functools.partial(consensus_kernel, offsets, width), out_s...]
    ppermute x8, starting transfers between devices: 12.8 us -> 12.1 us  [exchange(): return lax.ppermute(value, 'arow', [(i, i ^ mask) for i in range(count)])]
    add x0 -> x1, other arithmetic: none -> 0.75 us  [pack(): packed += jnp.pad(f.transpose(1, 2, 0), ((3 * n, 10 - 3 * n), (0, 0), (0,...]
    ppermute x1, starting transfers between devices: 2.02 us -> 1.52 us  [fast(): outer = lax.ppermute(feat_a, ('groups', 'arow'), outer_pairs(groups, count))]
  transfers between devices with their start and end apart: 9 -> 9, of which waited for: 7 -> 8; matrix products, arithmetic and copies ran while one was open for 2% -> 4% of each run, Pallas kernels for 0% -> 5%
where the time goes in v2:
time: 35.2 us; the launch traced here: 34.9 us
  starting transfers between devices  13.6 us (39%)
  waiting for transfers between devices  10 us (28%)
  Pallas kernels  8.34 us (24%)
  other arithmetic  2.27 us (6%)
  between operations  0.72 us (2%)
    ppermute x8, starting transfers between devices, exchange(): return lax.ppermute(value, 'arow', [(i, i ^ mask) for i in range(count)])  12.1 us
    ppermute x8, waiting for transfers between devices, exchange(): return lax.ppermute(value, 'arow', [(i, i ^ mask) for i in range(count)])  8.28 us
    pallas_call x1, Pallas kernels, consensus(): pl.pallas_call(functools.partial(consensus_kernel, offsets, width), out_s...  6.43 us
    pallas_call x1, Pallas kernels, prepare(): pl.pallas_call(functools.partial(prepare_kernel, width), out_shape=(jax.S...  1.91 us
    ppermute x1, waiting for transfers between devices, fast(): outer = lax.ppermute(feat_a, ('groups', 'arow'), outer_pairs(groups, count))  1.72 us
    ppermute x1, starting transfers between devices, fast(): outer = lax.ppermute(feat_a, ('groups', 'arow'), outer_pairs(groups, count))  1.52 us
    concatenate x1, other arithmetic, fast(): near = lax.optimization_barrier(jnp.concatenate([feat_a, feat_b], axis=0))  0.78 us
    add x1, other arithmetic, pack(): packed += jnp.pad(f.transpose(1, 2, 0), ((3 * n, 10 - 3 * n), (0, 0), (0,...  0.75 us
  transfers between devices with their start and end apart: 9, of which 8 were waited for; matrix products, arithmetic and copies ran while one was open for 4% of the time, Pallas kernels for 5%

profile of v2, /device:TPU:0, one launch (start us, length us, event | category | flops | bytes accessed | tf_op | source)
XLA Modules:
  0.0 34.9 jit_solution(15901994723008020914)
XLA Ops:
  0.0 3.5 %collective-permute-start = (bf16[1,32,256]{2,1,0:T(8,128)(2,1)}, bf16[1,32,256]{2,1,0:T(8,128)(2,1)S(1)}, u32[]{:S(2)}, u32[]{:S(2)}) collective-permute-start(bf16[1,32,256]{2,1,0:T(8,128)(2,1)} %param.9), channel_id=1, source_target_pairs={{0,9},{1,8},{2,11},{3,10},{4,13},{5,12},{6,15},{7,14},{8,1},{9,0},... | collective-permute-start | bytes 49160 | tf_op jit(solution)/shard_map/ppermute | solution.py:382
  3.5 0.8 %pad_maximum_fusion.3 = bf16[3,32,256]{2,1,0:T(8,128)(2,1)S(1)} fusion(bf16[1,32,256]{2,1,0:T(8,128)(2,1)} %param.9, bf16[2,32,256]{2,1,0:T(8,128)(2,1)} %param.8), kind=kLoop, calls=%fused_computation.4 | loop fusion | flops 24576 | bytes 98304 | tf_op jit(solution)/shard_map/concatenate | solution.py:405
  4.3 0.8 %pad_add_fusion.packed_ref = f32[13,3,8]{2,1,0:T(4,128)S(1)} fusion(f32[3,3,8]{2,1,0:T(4,128)} %bitcast.8, f32[3,3,8]{2,1,0:T(4,128)} %bitcast.9, f32[3,3,8]{2,1,0:T(4,128)} %bitcast.10, f32[3,3,8]{2,1,0:T(4,128)} %bitcast.11, f32[1,1,8]{2,1,0:T(1,128)} %bitcast.12), kind=kLoop, calls=%fused_computation.6 | loop fusion | flops 1248 | bytes 2432 | tf_op jit(solution)/shard_map/add | solution.py:228
  5.0 0.1 collective-permute-done
  5.1 1.9 %collective-permute-start.1 = (bf16[2,32,256]{2,1,0:T(8,128)(2,1)S(1)}, bf16[2,32,256]{2,1,0:T(8,128)(2,1)S(1)}, u32[]{:S(2)}, u32[]{:S(2)}) collective-permute-start(bf16[2,32,256]{2,1,0:T(8,128)(2,1)S(1)} %pad_maximum_fusion.4), channel_id=1, source_target_pairs={{0,5},{1,4},{2,7},{3,6},{4,1},{5,0},{6,3},{7,2},{8,13},{9,12},{10,... | collective-permute-start | bytes 98312 | tf_op jit(solution)/shard_map/ppermute | solution.py:382
  7.0 1.9 %shard_map.82 = (bf16[8,512,256]{2,1,0:T(8,128)(2,1)S(1)}, bf16[8,256,256]{2,1,0:T(8,128)(2,1)S(1)}, f32[16,16,128]{2,1,0:T(8,128)S(1)}, f32[8,16,128]{2,1,0:T(8,128)S(1)}) custom-call(f32[13,3,8]{2,1,0:T(4,128)S(1)} %pad_add_fusion.packed_ref), custom_call_target="tpu_custom_call" | custom-call | flops 4000000 | bytes 3500000 | tf_op jit(solution)/shard_map/pallas_call | solution.py:234
  8.9 0.0 collective-permute-done.1
  9.0 1.6 %collective-permute-start.2 = (bf16[4,32,256]{2,1,0:T(8,128)(2,1)S(1)}, bf16[4,32,256]{2,1,0:T(8,128)(2,1)S(1)}, u32[]{:S(2)}, u32[]{:S(2)}) collective-permute-start(bf16[4,32,256]{2,1,0:T(8,128)(2,1)S(1)} %pad_maximum_fusion.2), channel_id=1, source_target_pairs={{0,3},{1,2},{2,1},{3,0},{4,7},{5,6},{6,5},{7,4},{8,11},{9,10},{10,... | collective-permute-start | bytes 196616 | tf_op jit(solution)/shard_map/ppermute | solution.py:382
  10.5 1.5 %collective-permute-start.3 = (bf16[2,32,256]{2,1,0:T(8,128)(2,1)}, bf16[2,32,256]{2,1,0:T(8,128)(2,1)S(1)}, u32[]{:S(2)}, u32[]{:S(2)}) collective-permute-start(bf16[2,32,256]{2,1,0:T(8,128)(2,1)} %param.8), channel_id=1, source_target_pairs={{0,16},{1,2},{2,1},{3,4},{4,3},{5,6},{6,5},{7,8},{8,7},{9,10},{10,... | collective-permute-start | bytes 98312 | tf_op jit(solution)/shard_map/ppermute | solution.py:415
  12.0 0.9 %collective-permute-done.2 = bf16[4,32,256]{2,1,0:T(8,128)(2,1)S(1)} collective-permute-done((bf16[4,32,256]{2,1,0:T(8,128)(2,1)S(1)}, bf16[4,32,256]{2,1,0:T(8,128)(2,1)S(1)}, u32[]{:S(2)}, u32[]{:S(2)}) %collective-permute-start.2) | collective-permute-done | bytes 65568 | tf_op jit(solution)/shard_map/ppermute | solution.py:382
  12.9 1.7 %collective-permute-done.3.outer_ref = bf16[2,32,256]{2,1,0:T(8,128)(2,1)S(1)} collective-permute-done((bf16[2,32,256]{2,1,0:T(8,128)(2,1)}, bf16[2,32,256]{2,1,0:T(8,128)(2,1)S(1)}, u32[]{:S(2)}, u32[]{:S(2)}) %collective-permute-start.3) | collective-permute-done | bytes 32800 | tf_op jit(solution)/shard_map/ppermute | solution.py:415
  14.7 0.1 collective-permute-start.4
  15.4 0.7 %collective-permute-done.4.mate_ref = bf16[10,32,256]{2,1,0:T(8,128)(2,1)S(1)} collective-permute-done((bf16[10,32,256]{2,1,0:T(8,128)(2,1)S(1)}, bf16[10,32,256]{2,1,0:T(8,128)(2,1)S(1)}, u32[]{:S(2)}, u32[]{:S(2)}) %collective-permute-start.4) | collective-permute-done | bytes 163872 | tf_op jit(solution)/shard_map/ppermute | solution.py:382
  16.1 6.4 %shard_map.83 = (f32[64,512]{1,0:T(8,128)S(1)}, f32[64,512]{1,0:T(8,128)S(1)}, f32[1,512]{1,0:T(1,128)S(1)}) custom-call(f32[1]{0:T(128)S(6)} %copy.9.bias2_ref, bf16[8,512,256]{2,1,0:T(8,128)(2,1)S(1)} %get-tuple-element.32.at1_ref, bf16[8,256,256]{2,1,0:T(8,128)(2,1)S(1)} %get-tuple-element.33.at2_ref, f32[16,16,128]{2,1,0:T(8,128)S(1)} %get-tuple-element.34.w1_ref, ...), custom_call_target="tpu_custom_call" | custom-call | flops 2000000000 | bytes 4500000 | tf_op jit(solution)/shard_map/pallas_call | solution.py:355
  22.6 3.2 %collective-permute-start.5 = (f32[1,512]{1,0:T(1,128)S(1)}, f32[1,512]{1,0:T(1,128)S(1)}, u32[]{:S(2)}, u32[]{:S(2)}) collective-permute-start(f32[1,512]{1,0:T(1,128)S(1)} %get-tuple-element.40), channel_id=1, source_target_pairs={{0,9},{1,8},{2,11},{3,10},{4,13},{5,12},{6,15},{7,14},{8,1},{9,0},... | collective-permute-start | bytes 6152 | tf_op jit(solution)/shard_map/ppermute | solution.py:382
  25.7 1.3 %collective-permute-done.5 = f32[1,512]{1,0:T(1,128)S(1)} collective-permute-done((f32[1,512]{1,0:T(1,128)S(1)}, f32[1,512]{1,0:T(1,128)S(1)}, u32[]{:S(2)}, u32[]{:S(2)}) %collective-permute-start.5) | collective-permute-done | bytes 2080 | tf_op jit(solution)/shard_map/ppermute | solution.py:382
  27.1 1.4 %collective-permute-start.6 = (f32[1,512]{1,0:T(1,128)S(1)}, f32[1,512]{1,0:T(1,128)S(1)}, u32[]{:S(2)}, u32[]{:S(2)}) collective-permute-start(f32[1,512]{1,0:T(1,128)S(1)} %max.12), channel_id=1, source_target_pairs={{0,5},{1,4},{2,7},{3,6},{4,1},{5,0},{6,3},{7,2},{8,13},{9,12},{10,... | collective-permute-start | bytes 6152 | tf_op jit(solution)/shard_map/ppermute | solution.py:382
  28.5 1.6 %collective-permute-done.6 = f32[1,512]{1,0:T(1,128)S(1)} collective-permute-done((f32[1,512]{1,0:T(1,128)S(1)}, f32[1,512]{1,0:T(1,128)S(1)}, u32[]{:S(2)}, u32[]{:S(2)}) %collective-permute-start.6) | collective-permute-done | bytes 2080 | tf_op jit(solution)/shard_map/ppermute | solution.py:382
  30.1 0.2 collective-permute-start.7
  30.3 2.8 %collective-permute-done.7 = f32[1,512]{1,0:T(1,128)S(1)} collective-permute-done((f32[1,512]{1,0:T(1,128)S(1)}, f32[1,512]{1,0:T(1,128)S(1)}, u32[]{:S(2)}, u32[]{:S(2)}) %collective-permute-start.7) | collective-permute-done | bytes 2080 | tf_op jit(solution)/shard_map/ppermute | solution.py:382
  33.1 0.3 collective-permute-start.8
  33.4 0.8 %collective-permute-done.8 = f32[1,512]{1,0:T(1,128)S(1)} collective-permute-done((f32[1,512]{1,0:T(1,128)S(1)}, f32[1,512]{1,0:T(1,128)S(1)}, u32[]{:S(2)}, u32[]{:S(2)}) %collective-permute-start.8) | collective-permute-done | bytes 2080 | tf_op jit(solution)/shard_map/ppermute | solution.py:382
  34.3 0.7 %divide_multiply_fusion = f32[64,512]{1,0:T(8,128)} fusion(f32[64,512]{1,0:T(8,128)S(1)} %get-tuple-element.38, f32[64,512]{1,0:T(8,128)S(1)} %get-tuple-element.39, f32[512]{0:T(512)S(1)} %bitcast.7), kind=kLoop, calls=%fused_computation.2 | loop fusion | flops 65536 | bytes 395264 | tf_op jit(solution)/shard_map/mul | solution.py:426
  (10 shorter events, 0.1 us)
Async XLA Ops:
  0.0 5.1 %collective-permute-start = (bf16[1,32,256]{2,1,0:T(8,128)(2,1)}, bf16[1,32,256]{2,1,0:T(8,128)(2,1)S(1)}, u32[]{:S(2)}, u32[]{:S(2)}) collective-permute-start(bf16[1,32,256]{2,1,0:T(8,128)(2,1)} %param.9), channel_id=1, source_target_pairs={{0,9},{1,8},{2,11},{3,10},{4,13},{5,12},{6,15},{7,14},{8,1},{9,0},... | collective-permute-start | bytes 49160 | tf_op jit(solution)/shard_map/ppermute | solution.py:382
  5.1 3.8 %collective-permute-start.1 = (bf16[2,32,256]{2,1,0:T(8,128)(2,1)S(1)}, bf16[2,32,256]{2,1,0:T(8,128)(2,1)S(1)}, u32[]{:S(2)}, u32[]{:S(2)}) collective-permute-start(bf16[2,32,256]{2,1,0:T(8,128)(2,1)S(1)} %pad_maximum_fusion.4), channel_id=1, source_target_pairs={{0,5},{1,4},{2,7},{3,6},{4,1},{5,0},{6,3},{7,2},{8,13},{9,12},{10,... | collective-permute-start | bytes 98312 | tf_op jit(solution)/shard_map/ppermute | solution.py:382
  9.0 4.0 %collective-permute-start.2 = (bf16[4,32,256]{2,1,0:T(8,128)(2,1)S(1)}, bf16[4,32,256]{2,1,0:T(8,128)(2,1)S(1)}, u32[]{:S(2)}, u32[]{:S(2)}) collective-permute-start(bf16[4,32,256]{2,1,0:T(8,128)(2,1)S(1)} %pad_maximum_fusion.2), channel_id=1, source_target_pairs={{0,3},{1,2},{2,1},{3,0},{4,7},{5,6},{6,5},{7,4},{8,11},{9,10},{10,... | collective-permute-start | bytes 196616 | tf_op jit(solution)/shard_map/ppermute | solution.py:382
  10.5 4.1 %collective-permute-start.3 = (bf16[2,32,256]{2,1,0:T(8,128)(2,1)}, bf16[2,32,256]{2,1,0:T(8,128)(2,1)S(1)}, u32[]{:S(2)}, u32[]{:S(2)}) collective-permute-start(bf16[2,32,256]{2,1,0:T(8,128)(2,1)} %param.8), channel_id=1, source_target_pairs={{0,16},{1,2},{2,1},{3,4},{4,3},{5,6},{6,5},{7,8},{8,7},{9,10},{10,... | collective-permute-start | bytes 98312 | tf_op jit(solution)/shard_map/ppermute | solution.py:415
  14.7 1.5 %collective-permute-start.4 = (bf16[10,32,256]{2,1,0:T(8,128)(2,1)S(1)}, bf16[10,32,256]{2,1,0:T(8,128)(2,1)S(1)}, u32[]{:S(2)}, u32[]{:S(2)}) collective-permute-start(bf16[10,32,256]{2,1,0:T(8,128)(2,1)S(1)} %pad_maximum_fusion.own_ref), channel_id=1, source_target_pairs={{0,1},{1,0},{2,3},{3,2},{4,5},{5,4},{6,7},{7,6},{8,9},{9,8},{10,11... | collective-permute-start | bytes 491528 | tf_op jit(solution)/shard_map/ppermute | solution.py:382
  22.6 4.5 %collective-permute-start.5 = (f32[1,512]{1,0:T(1,128)S(1)}, f32[1,512]{1,0:T(1,128)S(1)}, u32[]{:S(2)}, u32[]{:S(2)}) collective-permute-start(f32[1,512]{1,0:T(1,128)S(1)} %get-tuple-element.40), channel_id=1, source_target_pairs={{0,9},{1,8},{2,11},{3,10},{4,13},{5,12},{6,15},{7,14},{8,1},{9,0},... | collective-permute-start | bytes 6152 | tf_op jit(solution)/shard_map/ppermute | solution.py:382
  27.1 3.0 %collective-permute-start.6 = (f32[1,512]{1,0:T(1,128)S(1)}, f32[1,512]{1,0:T(1,128)S(1)}, u32[]{:S(2)}, u32[]{:S(2)}) collective-permute-start(f32[1,512]{1,0:T(1,128)S(1)} %max.12), channel_id=1, source_target_pairs={{0,5},{1,4},{2,7},{3,6},{4,1},{5,0},{6,3},{7,2},{8,13},{9,12},{10,... | collective-permute-start | bytes 6152 | tf_op jit(solution)/shard_map/ppermute | solution.py:382
  30.1 3.0 %collective-permute-start.7 = (f32[1,512]{1,0:T(1,128)S(1)}, f32[1,512]{1,0:T(1,128)S(1)}, u32[]{:S(2)}, u32[]{:S(2)}) collective-permute-start(f32[1,512]{1,0:T(1,128)S(1)} %max.13), channel_id=1, source_target_pairs={{0,3},{1,2},{2,1},{3,0},{4,7},{5,6},{6,5},{7,4},{8,11},{9,10},{10,... | collective-permute-start | bytes 6152 | tf_op jit(solution)/shard_map/ppermute | solution.py:382
  33.1 1.2 %collective-permute-start.8 = (f32[1,512]{1,0:T(1,128)S(1)}, f32[1,512]{1,0:T(1,128)S(1)}, u32[]{:S(2)}, u32[]{:S(2)}) collective-permute-start(f32[1,512]{1,0:T(1,128)S(1)} %max.14), channel_id=1, source_target_pairs={{0,1},{1,0},{2,3},{3,2},{4,5},{5,4},{6,7},{7,6},{8,9},{9,8},{10,11... | collective-permute-start | bytes 6152 | tf_op jit(solution)/shard_map/ppermute | solution.py:382

commit v3 on v2

--- a/solution.py
+++ b/solution.py
@@ -194,6 +194,7 @@
                     total = term if total is None else total + term
             sums.append(total)
         emit(jb, sums[0], sums[1])
+        yield
         window = [window[1], window[2], column(jb + 2) if jb + 2 < width else None]
 
 
@@ -243,7 +244,7 @@
         out_specs=(vmem,) * 4,
         compiler_params=pltpu.CompilerParams(vmem_limit_bytes=16 << 20),
         cost_estimate=pl.CostEstimate(
-            flops=4_000_000, bytes_accessed=3_500_000, transcendentals=0
+            flops=500_000_000, bytes_accessed=3_500_000, transcendentals=0
         ),
     )(packed)
 
@@ -301,30 +302,36 @@
     for c in range(4):
         vp_ref[:, 128 * c : 128 * c + 128] = vf_ref[c % 2].astype(BF16)
 
-    for k in range(8):
+    def spread(k):
         s_ref[k % 2] = jnp.dot(vp_ref[...], at1_ref[k], preferred_element_type=F32)
+
+    def hide(k):
         for net in range(2):
             weights = [w1_ref[2 * k + net, tap : tap + 1] for tap in range(9)]
             bias = w1_ref[2 * k + net, 9:10]
 
-            def load(r, net=net, k=k):
+            def load(r):
                 return s_ref[k % 2, 8 * r : 8 * r + 8, 128 * net : 128 * net + 128]
 
-            def emit(jb, even, odd, net=net, k=k, bias=bias):
+            def emit(jb, even, odd):
                 pair = jnp.concatenate([even, odd], axis=0)
                 h_ref[k % 2, 16 * jb : 16 * jb + 16, 128 * net : 128 * net + 128] = jnp.maximum(
                     pair + bias, 0.0
                 ).astype(BF16)
 
-            b_taps(load, weights, emit, width)
+            yield from b_taps(load, weights, emit, width)
+
+    def gather_rows(k):
         both = jnp.dot(h_ref[k % 2], at2_ref[k], preferred_element_type=F32)
         t_ref[k % 2] = both[:, 0:128] + both[:, 128:256]
+
+    def gather_taps(k):
         weights = [w2_ref[k, tap : tap + 1] for tap in range(9)]
 
-        def load(r, k=k):
+        def load(r):
             return t_ref[k % 2, 8 * r : 8 * r + 8, :]
 
-        def emit(jb, even, odd, k=k):
+        def emit(jb, even, odd):
             pair = jnp.concatenate([even, odd], axis=0)
             if k == 0:
                 acc_ref[16 * jb : 16 * jb + 16, :] = pair
@@ -337,7 +344,19 @@
                 nat_ref[pl.ds(jb, 8, stride=2 * width), :] = total[0:8]
                 nat_ref[pl.ds(width + jb, 8, stride=2 * width), :] = total[8:16]
 
-        b_taps(load, weights, emit, width)
+        yield from b_taps(load, weights, emit, width)
+
+    for step in range(11):
+        if step < 8:
+            spread(step)
+        if 2 <= step < 10:
+            gather_rows(step - 2)
+        ones = hide(step - 1) if 1 <= step < 9 else iter(())
+        twos = gather_taps(step - 3) if step >= 3 else iter(())
+        for _ in range(width):
+            next(ones, None)
+            next(twos, None)
+            next(ones, None)
 
     turned = jnp.transpose(nat_ref[...], (1, 0))
     score = turned[0:64] + turned[64:128]
@@ -408,15 +427,17 @@
     held, offsets = feat_b, [0]
     for n, mask in enumerate(masks):
         if n == 1:
-            held, packed = lax.optimization_barrier((held, packed))
+            feat_a, held, packed = lax.optimization_barrier((feat_a, held, packed))
+            outer = lax.ppermute(feat_a, ("groups", "arow"), outer_pairs(groups, count))
+        if n == 2:
+            packed, outer = lax.optimization_barrier((packed, outer))
             weights = prepare(packed, width)
-        if n == 2:
-            feat_a, held, weights = lax.optimization_barrier((feat_a, held, weights))
-            outer = lax.ppermute(feat_a, ("groups", "arow"), outer_pairs(groups, count))
         received = exchange(held, mask, count)
         held = jnp.concatenate([near_b if n == 0 else held, received], axis=0)
         offsets = offsets + [o ^ mask for o in offsets]
-    held, outer, bias_second = lax.optimization_barrier((held, outer, bias_second))
+    held, outer, weights, bias_second = lax.optimization_barrier(
+        (held, outer, weights, bias_second)
+    )
     own = jnp.concatenate([held, near_a], axis=0)
     mate = exchange(own, 1, count)
 

time: 35.2 us -> 33 us (0.937)
  waiting for transfers between devices: 10 us -> 6.89 us
  starting transfers between devices: 13.6 us -> 15.2 us
  Pallas kernels: 8.34 us -> 7.72 us
    ppermute x8, waiting for transfers between devices: 8.28 us -> 6.16 us  [exchange(): return lax.ppermute(value, 'arow', [(i, i ^ mask) for i in range(count)])]
    ppermute x8, starting transfers between devices: 12.1 us -> 13.6 us  [exchange(): return lax.ppermute(value, 'arow', [(i, i ^ mask) for i in range(count)])]
    ppermute x1, waiting for transfers between devices: 1.72 us -> 0.73 us  [fast(): outer = lax.ppermute(feat_a, ('groups', 'arow'), outer_pairs(groups, count))]
    pallas_call x1, Pallas kernels: 6.43 us -> 5.81 us  [consensus(): pl.pallas_call(functools.partial(consensus_kernel, offsets, width), out_s...]
  transfers between devices with their start and end apart: 9 -> 9, of which waited for: 8 -> 8; matrix products, arithmetic and copies ran while one was open for 4% -> 5% of each run, Pallas kernels for 5% -> 6%
where the time goes in v3:
time: 33 us; the launch traced here: 32.8 us
  starting transfers between devices  15.2 us (46%)
  Pallas kernels  7.72 us (23%)
  waiting for transfers between devices  6.89 us (21%)
  other arithmetic  2.27 us (7%)
  between operations  0.72 us (2%)
    ppermute x8, starting transfers between devices, exchange(): return lax.ppermute(value, 'arow', [(i, i ^ mask) for i in range(count)])  13.6 us
    ppermute x8, waiting for transfers between devices, exchange(): return lax.ppermute(value, 'arow', [(i, i ^ mask) for i in range(count)])  6.16 us
    pallas_call x1, Pallas kernels, consensus(): pl.pallas_call(functools.partial(consensus_kernel, offsets, width), out_s...  5.81 us
    pallas_call x1, Pallas kernels, prepare(): pl.pallas_call(functools.partial(prepare_kernel, width), out_shape=(jax.S...  1.91 us
    ppermute x1, starting transfers between devices, fast(): outer = lax.ppermute(feat_a, ('groups', 'arow'), outer_pairs(groups, count))  1.52 us
    concatenate x1, other arithmetic, fast(): near = lax.optimization_barrier(jnp.concatenate([feat_a, feat_b], axis=0))  0.78 us
    add x1, other arithmetic, pack(): packed += jnp.pad(f.transpose(1, 2, 0), ((3 * n, 10 - 3 * n), (0, 0), (0,...  0.75 us
    ppermute x1, waiting for transfers between devices, fast(): outer = lax.ppermute(feat_a, ('groups', 'arow'), outer_pairs(groups, count))  0.73 us
  transfers between devices with their start and end apart: 9, of which 8 were waited for; matrix products, arithmetic and copies ran while one was open for 5% of the time, Pallas kernels for 6%

profile of v3, /device:TPU:0, one launch (start us, length us, event | category | flops | bytes accessed | tf_op | source)
XLA Modules:
  0.0 32.8 jit_solution(12535979420655438242)
XLA Ops:
  0.0 3.5 %collective-permute-start = (bf16[1,32,256]{2,1,0:T(8,128)(2,1)}, bf16[1,32,256]{2,1,0:T(8,128)(2,1)S(1)}, u32[]{:S(2)}, u32[]{:S(2)}) collective-permute-start(bf16[1,32,256]{2,1,0:T(8,128)(2,1)} %param.9), channel_id=1, source_target_pairs={{0,9},{1,8},{2,11},{3,10},{4,13},{5,12},{6,15},{7,14},{8,1},{9,0},... | collective-permute-start | bytes 49160 | tf_op jit(solution)/shard_map/ppermute | solution.py:401
  3.5 0.8 %pad_maximum_fusion.3 = bf16[3,32,256]{2,1,0:T(8,128)(2,1)S(1)} fusion(bf16[1,32,256]{2,1,0:T(8,128)(2,1)} %param.9, bf16[2,32,256]{2,1,0:T(8,128)(2,1)} %param.8), kind=kLoop, calls=%fused_computation.4 | loop fusion | flops 24576 | bytes 98304 | tf_op jit(solution)/shard_map/concatenate | solution.py:424
  4.3 0.8 %pad_add_fusion.packed_ref = f32[13,3,8]{2,1,0:T(4,128)S(1)} fusion(f32[3,3,8]{2,1,0:T(4,128)} %bitcast.8, f32[3,3,8]{2,1,0:T(4,128)} %bitcast.9, f32[3,3,8]{2,1,0:T(4,128)} %bitcast.10, f32[3,3,8]{2,1,0:T(4,128)} %bitcast.11, f32[1,1,8]{2,1,0:T(1,128)} %bitcast.12), kind=kLoop, calls=%fused_computation.6 | loop fusion | flops 1248 | bytes 2432 | tf_op jit(solution)/shard_map/add | solution.py:229
  5.0 0.1 collective-permute-done
  5.1 1.9 %collective-permute-start.1 = (bf16[2,32,256]{2,1,0:T(8,128)(2,1)S(1)}, bf16[2,32,256]{2,1,0:T(8,128)(2,1)S(1)}, u32[]{:S(2)}, u32[]{:S(2)}) collective-permute-start(bf16[2,32,256]{2,1,0:T(8,128)(2,1)S(1)} %pad_maximum_fusion.4), channel_id=1, source_target_pairs={{0,5},{1,4},{2,7},{3,6},{4,1},{5,0},{6,3},{7,2},{8,13},{9,12},{10,... | collective-permute-start | bytes 98312 | tf_op jit(solution)/shard_map/ppermute | solution.py:401
  7.0 1.5 %collective-permute-start.3 = (bf16[2,32,256]{2,1,0:T(8,128)(2,1)}, bf16[2,32,256]{2,1,0:T(8,128)(2,1)S(1)}, u32[]{:S(2)}, u32[]{:S(2)}) collective-permute-start(bf16[2,32,256]{2,1,0:T(8,128)(2,1)} %param.8), channel_id=1, source_target_pairs={{0,16},{1,2},{2,1},{3,4},{4,3},{5,6},{6,5},{7,8},{8,7},{9,10},{10,... | collective-permute-start | bytes 98312 | tf_op jit(solution)/shard_map/ppermute | solution.py:431
  8.5 0.1 collective-permute-done.1
  8.6 1.8 %collective-permute-start.2 = (bf16[4,32,256]{2,1,0:T(8,128)(2,1)S(1)}, bf16[4,32,256]{2,1,0:T(8,128)(2,1)S(1)}, u32[]{:S(2)}, u32[]{:S(2)}) collective-permute-start(bf16[4,32,256]{2,1,0:T(8,128)(2,1)S(1)} %pad_maximum_fusion.2), channel_id=1, source_target_pairs={{0,3},{1,2},{2,1},{3,0},{4,7},{5,6},{6,5},{7,4},{8,11},{9,10},{10,... | collective-permute-start | bytes 196616 | tf_op jit(solution)/shard_map/ppermute | solution.py:401
  10.4 0.7 %collective-permute-done.3.outer_ref = bf16[2,32,256]{2,1,0:T(8,128)(2,1)S(1)} collective-permute-done((bf16[2,32,256]{2,1,0:T(8,128)(2,1)}, bf16[2,32,256]{2,1,0:T(8,128)(2,1)S(1)}, u32[]{:S(2)}, u32[]{:S(2)}) %collective-permute-start.3) | collective-permute-done | bytes 32800 | tf_op jit(solution)/shard_map/ppermute | solution.py:431
  11.2 1.9 %shard_map.82 = (bf16[8,512,256]{2,1,0:T(8,128)(2,1)S(1)}, bf16[8,256,256]{2,1,0:T(8,128)(2,1)S(1)}, f32[16,16,128]{2,1,0:T(8,128)S(1)}, f32[8,16,128]{2,1,0:T(8,128)S(1)}) custom-call(f32[13,3,8]{2,1,0:T(4,128)S(1)} %pad_add_fusion.packed_ref), custom_call_target="tpu_custom_call" | custom-call | flops 500000000 | bytes 3500000 | tf_op jit(solution)/shard_map/pallas_call | solution.py:235
  13.1 0.0 collective-permute-done.2
  13.1 0.2 collective-permute-start.4
  14.0 0.6 %collective-permute-done.4.mate_ref = bf16[10,32,256]{2,1,0:T(8,128)(2,1)S(1)} collective-permute-done((bf16[10,32,256]{2,1,0:T(8,128)(2,1)S(1)}, bf16[10,32,256]{2,1,0:T(8,128)(2,1)S(1)}, u32[]{:S(2)}, u32[]{:S(2)}) %collective-permute-start.4) | collective-permute-done | bytes 163872 | tf_op jit(solution)/shard_map/ppermute | solution.py:401
  14.6 5.8 %shard_map.83 = (f32[64,512]{1,0:T(8,128)S(1)}, f32[64,512]{1,0:T(8,128)S(1)}, f32[1,512]{1,0:T(1,128)S(1)}) custom-call(f32[1]{0:T(128)S(6)} %copy.9.bias2_ref, bf16[8,512,256]{2,1,0:T(8,128)(2,1)S(1)} %get-tuple-element.34.at1_ref, bf16[8,256,256]{2,1,0:T(8,128)(2,1)S(1)} %get-tuple-element.35.at2_ref, f32[16,16,128]{2,1,0:T(8,128)S(1)} %get-tuple-element.36.w1_ref, ...), custom_call_target="tpu_custom_call" | custom-call | flops 2000000000 | bytes 4500000 | tf_op jit(solution)/shard_map/pallas_call | solution.py:374
  20.4 3.2 %collective-permute-start.5 = (f32[1,512]{1,0:T(1,128)S(1)}, f32[1,512]{1,0:T(1,128)S(1)}, u32[]{:S(2)}, u32[]{:S(2)}) collective-permute-start(f32[1,512]{1,0:T(1,128)S(1)} %get-tuple-element.42), channel_id=1, source_target_pairs={{0,9},{1,8},{2,11},{3,10},{4,13},{5,12},{6,15},{7,14},{8,1},{9,0},... | collective-permute-start | bytes 6152 | tf_op jit(solution)/shard_map/ppermute | solution.py:401
  23.6 1.3 %collective-permute-done.5 = f32[1,512]{1,0:T(1,128)S(1)} collective-permute-done((f32[1,512]{1,0:T(1,128)S(1)}, f32[1,512]{1,0:T(1,128)S(1)}, u32[]{:S(2)}, u32[]{:S(2)}) %collective-permute-start.5) | collective-permute-done | bytes 2080 | tf_op jit(solution)/shard_map/ppermute | solution.py:401
  24.9 1.4 %collective-permute-start.6 = (f32[1,512]{1,0:T(1,128)S(1)}, f32[1,512]{1,0:T(1,128)S(1)}, u32[]{:S(2)}, u32[]{:S(2)}) collective-permute-start(f32[1,512]{1,0:T(1,128)S(1)} %max.12), channel_id=1, source_target_pairs={{0,5},{1,4},{2,7},{3,6},{4,1},{5,0},{6,3},{7,2},{8,13},{9,12},{10,... | collective-permute-start | bytes 6152 | tf_op jit(solution)/shard_map/ppermute | solution.py:401
  26.3 1.6 %collective-permute-done.6 = f32[1,512]{1,0:T(1,128)S(1)} collective-permute-done((f32[1,512]{1,0:T(1,128)S(1)}, f32[1,512]{1,0:T(1,128)S(1)}, u32[]{:S(2)}, u32[]{:S(2)}) %collective-permute-start.6) | collective-permute-done | bytes 2080 | tf_op jit(solution)/shard_map/ppermute | solution.py:401
  27.9 1.4 %collective-permute-start.7 = (f32[1,512]{1,0:T(1,128)S(1)}, f32[1,512]{1,0:T(1,128)S(1)}, u32[]{:S(2)}, u32[]{:S(2)}) collective-permute-start(f32[1,512]{1,0:T(1,128)S(1)} %max.13), channel_id=1, source_target_pairs={{0,3},{1,2},{2,1},{3,0},{4,7},{5,6},{6,5},{7,4},{8,11},{9,10},{10,... | collective-permute-start | bytes 6152 | tf_op jit(solution)/shard_map/ppermute | solution.py:401
  29.3 1.6 %collective-permute-done.7 = f32[1,512]{1,0:T(1,128)S(1)} collective-permute-done((f32[1,512]{1,0:T(1,128)S(1)}, f32[1,512]{1,0:T(1,128)S(1)}, u32[]{:S(2)}, u32[]{:S(2)}) %collective-permute-start.7) | collective-permute-done | bytes 2080 | tf_op jit(solution)/shard_map/ppermute | solution.py:401
  30.9 0.3 collective-permute-start.8
  31.2 0.8 %collective-permute-done.8 = f32[1,512]{1,0:T(1,128)S(1)} collective-permute-done((f32[1,512]{1,0:T(1,128)S(1)}, f32[1,512]{1,0:T(1,128)S(1)}, u32[]{:S(2)}, u32[]{:S(2)}) %collective-permute-start.8) | collective-permute-done | bytes 2080 | tf_op jit(solution)/shard_map/ppermute | solution.py:401
  32.1 0.7 %divide_multiply_fusion = f32[64,512]{1,0:T(8,128)} fusion(f32[64,512]{1,0:T(8,128)S(1)} %get-tuple-element.40, f32[64,512]{1,0:T(8,128)S(1)} %get-tuple-element.41, f32[512]{0:T(512)S(1)} %bitcast.7), kind=kLoop, calls=%fused_computation.2 | loop fusion | flops 65536 | bytes 395264 | tf_op jit(solution)/shard_map/mul | solution.py:447
  (10 shorter events, 0.1 us)
Async XLA Ops:
  0.0 5.1 %collective-permute-start = (bf16[1,32,256]{2,1,0:T(8,128)(2,1)}, bf16[1,32,256]{2,1,0:T(8,128)(2,1)S(1)}, u32[]{:S(2)}, u32[]{:S(2)}) collective-permute-start(bf16[1,32,256]{2,1,0:T(8,128)(2,1)} %param.9), channel_id=1, source_target_pairs={{0,9},{1,8},{2,11},{3,10},{4,13},{5,12},{6,15},{7,14},{8,1},{9,0},... | collective-permute-start | bytes 49160 | tf_op jit(solution)/shard_map/ppermute | solution.py:401
  5.1 3.5 %collective-permute-start.1 = (bf16[2,32,256]{2,1,0:T(8,128)(2,1)S(1)}, bf16[2,32,256]{2,1,0:T(8,128)(2,1)S(1)}, u32[]{:S(2)}, u32[]{:S(2)}) collective-permute-start(bf16[2,32,256]{2,1,0:T(8,128)(2,1)S(1)} %pad_maximum_fusion.4), channel_id=1, source_target_pairs={{0,5},{1,4},{2,7},{3,6},{4,1},{5,0},{6,3},{7,2},{8,13},{9,12},{10,... | collective-permute-start | bytes 98312 | tf_op jit(solution)/shard_map/ppermute | solution.py:401
  7.0 4.1 %collective-permute-start.3 = (bf16[2,32,256]{2,1,0:T(8,128)(2,1)}, bf16[2,32,256]{2,1,0:T(8,128)(2,1)S(1)}, u32[]{:S(2)}, u32[]{:S(2)}) collective-permute-start(bf16[2,32,256]{2,1,0:T(8,128)(2,1)} %param.8), channel_id=1, source_target_pairs={{0,16},{1,2},{2,1},{3,4},{4,3},{5,6},{6,5},{7,8},{8,7},{9,10},{10,... | collective-permute-start | bytes 98312 | tf_op jit(solution)/shard_map/ppermute | solution.py:431
  8.6 4.4 %collective-permute-start.2 = (bf16[4,32,256]{2,1,0:T(8,128)(2,1)S(1)}, bf16[4,32,256]{2,1,0:T(8,128)(2,1)S(1)}, u32[]{:S(2)}, u32[]{:S(2)}) collective-permute-start(bf16[4,32,256]{2,1,0:T(8,128)(2,1)S(1)} %pad_maximum_fusion.2), channel_id=1, source_target_pairs={{0,3},{1,2},{2,1},{3,0},{4,7},{5,6},{6,5},{7,4},{8,11},{9,10},{10,... | collective-permute-start | bytes 196616 | tf_op jit(solution)/shard_map/ppermute | solution.py:401
  13.1 1.5 %collective-permute-start.4 = (bf16[10,32,256]{2,1,0:T(8,128)(2,1)S(1)}, bf16[10,32,256]{2,1,0:T(8,128)(2,1)S(1)}, u32[]{:S(2)}, u32[]{:S(2)}) collective-permute-start(bf16[10,32,256]{2,1,0:T(8,128)(2,1)S(1)} %pad_maximum_fusion.own_ref), channel_id=1, source_target_pairs={{0,1},{1,0},{2,3},{3,2},{4,5},{5,4},{6,7},{7,6},{8,9},{9,8},{10,11... | collective-permute-start | bytes 491528 | tf_op jit(solution)/shard_map/ppermute | solution.py:401
  20.4 4.5 %collective-permute-start.5 = (f32[1,512]{1,0:T(1,128)S(1)}, f32[1,512]{1,0:T(1,128)S(1)}, u32[]{:S(2)}, u32[]{:S(2)}) collective-permute-start(f32[1,512]{1,0:T(1,128)S(1)} %get-tuple-element.42), channel_id=1, source_target_pairs={{0,9},{1,8},{2,11},{3,10},{4,13},{5,12},{6,15},{7,14},{8,1},{9,0},... | collective-permute-start | bytes 6152 | tf_op jit(solution)/shard_map/ppermute | solution.py:401
  24.9 3.0 %collective-permute-start.6 = (f32[1,512]{1,0:T(1,128)S(1)}, f32[1,512]{1,0:T(1,128)S(1)}, u32[]{:S(2)}, u32[]{:S(2)}) collective-permute-start(f32[1,512]{1,0:T(1,128)S(1)} %max.12), channel_id=1, source_target_pairs={{0,5},{1,4},{2,7},{3,6},{4,1},{5,0},{6,3},{7,2},{8,13},{9,12},{10,... | collective-permute-start | bytes 6152 | tf_op jit(solution)/shard_map/ppermute | solution.py:401
  27.9 3.0 %collective-permute-start.7 = (f32[1,512]{1,0:T(1,128)S(1)}, f32[1,512]{1,0:T(1,128)S(1)}, u32[]{:S(2)}, u32[]{:S(2)}) collective-permute-start(f32[1,512]{1,0:T(1,128)S(1)} %max.13), channel_id=1, source_target_pairs={{0,3},{1,2},{2,1},{3,0},{4,7},{5,6},{6,5},{7,4},{8,11},{9,10},{10,... | collective-permute-start | bytes 6152 | tf_op jit(solution)/shard_map/ppermute | solution.py:401
  30.9 1.2 %collective-permute-start.8 = (f32[1,512]{1,0:T(1,128)S(1)}, f32[1,512]{1,0:T(1,128)S(1)}, u32[]{:S(2)}, u32[]{:S(2)}) collective-permute-start(f32[1,512]{1,0:T(1,128)S(1)} %max.14), channel_id=1, source_target_pairs={{0,1},{1,0},{2,3},{3,2},{4,5},{5,4},{6,7},{7,6},{8,9},{9,8},{10,11... | collective-permute-start | bytes 6152 | tf_op jit(solution)/shard_map/ppermute | solution.py:401

commit v4 on v3

--- a/solution.py
+++ b/solution.py
@@ -171,6 +171,16 @@
             at_ref[k, rows, 128:256] = low
 
 
+def minimal_filter(taps):
+    parts = [[], [], [], []]
+    for t in range(3):
+        ends = 0.5 * (taps[t] + taps[6 + t])
+        middle = 0.5 * taps[3 + t]
+        for part, row in zip(parts, (taps[t], ends + middle, ends - middle, taps[6 + t])):
+            part.append(row)
+    return sum(parts, [])
+
+
 def b_taps(load, weights, emit, width):
     top = sublane((8, 128)) == 0
     bottom = sublane((8, 128)) == 7
@@ -179,23 +189,27 @@
         even, odd = load(2 * jb), load(2 * jb + 1)
         above = jnp.where(top, 0.0, pltpu.roll(odd, 1, 0))
         below = jnp.where(bottom, 0.0, pltpu.roll(even, 7, 0))
-        return above, even, odd, below
+        return above - odd, even + odd, odd - even, even - below
 
     window = [None, column(0), column(1)]
     for jb in range(width):
         sums = []
-        for par in range(2):
+        for part in range(4):
             total = None
             for t in range(3):
                 if window[t] is None:
                     continue
-                for s in range(3):
-                    term = weights[3 * s + t] * window[t][par + s]
-                    total = term if total is None else total + term
+                term = weights[3 * part + t] * window[t][part]
+                total = term if total is None else total + term
             sums.append(total)
-        emit(jb, sums[0], sums[1])
+        emit(jb, sums)
         yield
         window = [window[1], window[2], column(jb + 2) if jb + 2 < width else None]
+
+
+def pair_of(sums):
+    first, second, third, fourth = sums
+    return jnp.concatenate([first + second + third, second - third - fourth], axis=0)
 
 
 def prepare_kernel(width, packed_ref, at1_ref, at2_ref, w1_ref, w2_ref):
@@ -214,13 +228,17 @@
     for k in range(8):
         first_weights(first, at1_ref, k, width)
         second_weights(second, at2_ref, k, width, keep)
-        for tap in range(9):
-            at = (tap // 3, tap % 3, k)
-            for net in range(2):
-                w1_ref[2 * k + net, tap : tap + 1] = jnp.full((1, 128), first[1 - net](*at), F32)
-            w2_ref[k, tap : tap + 1] = jnp.where(half_lanes, second[1](*at), second[0](*at))
+        places = [(tap // 3, tap % 3, k) for tap in range(9)]
         for net in range(2):
-            w1_ref[2 * k + net, 9:10] = jnp.full((1, 128), packed_ref[12, 0, k], F32)
+            rows = minimal_filter([jnp.full((1, 128), first[1 - net](*at), F32) for at in places])
+            for n, row in enumerate(rows):
+                w1_ref[2 * k + net, n : n + 1] = row
+            w1_ref[2 * k + net, 12:13] = jnp.full((1, 128), packed_ref[12, 0, k], F32)
+        rows = minimal_filter(
+            [jnp.where(half_lanes, second[1](*at), second[0](*at)) for at in places]
+        )
+        for n, row in enumerate(rows):
+            w2_ref[k, n : n + 1] = row
 
 
 def pack(bias, *banks):
@@ -307,17 +325,17 @@
 
     def hide(k):
         for net in range(2):
-            weights = [w1_ref[2 * k + net, tap : tap + 1] for tap in range(9)]
-            bias = w1_ref[2 * k + net, 9:10]
+            weights = [w1_ref[2 * k + net, n : n + 1] for n in range(12)]
+            bias = w1_ref[2 * k + net, 12:13]
 
             def load(r):
                 return s_ref[k % 2, 8 * r : 8 * r + 8, 128 * net : 128 * net + 128]
 
-            def emit(jb, even, odd):
-                pair = jnp.concatenate([even, odd], axis=0)
+            def emit(jb, sums):
+                sums[1] = sums[1] + bias
                 h_ref[k % 2, 16 * jb : 16 * jb + 16, 128 * net : 128 * net + 128] = jnp.maximum(
-                    pair + bias, 0.0
-                ).astype(BF16)
+                    pair_of(sums).astype(BF16), 0
+                )
 
             yield from b_taps(load, weights, emit, width)
 
@@ -326,21 +344,19 @@
         t_ref[k % 2] = both[:, 0:128] + both[:, 128:256]
 
     def gather_taps(k):
-        weights = [w2_ref[k, tap : tap + 1] for tap in range(9)]
+        weights = [w2_ref[k, n : n + 1] for n in range(12)]
 
         def load(r):
             return t_ref[k % 2, 8 * r : 8 * r + 8, :]
 
-        def emit(jb, even, odd):
-            pair = jnp.concatenate([even, odd], axis=0)
-            if k == 0:
-                acc_ref[16 * jb : 16 * jb + 16, :] = pair
-            elif k < 7:
-                acc_ref[16 * jb : 16 * jb + 16, :] += pair
+        def emit(jb, sums):
+            if k > 0:
+                sums = [acc_ref[part, 8 * jb : 8 * jb + 8, :] + sums[part] for part in range(4)]
+            if k < 7:
+                for part in range(4):
+                    acc_ref[part, 8 * jb : 8 * jb + 8, :] = sums[part]
             else:
-                total = jnp.maximum(
-                    acc_ref[16 * jb : 16 * jb + 16, :] + pair + bias2_ref[0], 0.0
-                )
+                total = jnp.maximum(pair_of(sums) + bias2_ref[0], 0.0)
                 nat_ref[pl.ds(jb, 8, stride=2 * width), :] = total[0:8]
                 nat_ref[pl.ds(width + jb, 8, stride=2 * width), :] = total[8:16]
 
@@ -387,7 +403,7 @@
             pltpu.VMEM((2, cells, 256), F32),
             pltpu.VMEM((2, cells, 256), BF16),
             pltpu.VMEM((2, cells, 128), F32),
-            pltpu.VMEM((cells, 128), F32),
+            pltpu.VMEM((4, cells // 2, 128), F32),
             pltpu.VMEM((cells, 128), F32),
         ],
         compiler_params=pltpu.CompilerParams(vmem_limit_bytes=32 << 20),

time: 33 us -> 32.5 us (0.985)
  Pallas kernels: 7.72 us -> 7.19 us
    pallas_call x1, Pallas kernels: 5.81 us -> 5.23 us  [consensus(): pl.pallas_call(functools.partial(consensus_kernel, offsets, width), out_s...]
where the time goes in v4:
time: 32.5 us; the launch traced here: 32.2 us
  starting transfers between devices  15.1 us (46%)
  Pallas kernels  7.19 us (22%)
  waiting for transfers between devices  6.94 us (21%)
  other arithmetic  2.27 us (7%)
  between operations  0.72 us (2%)
    ppermute x8, starting transfers between devices, exchange(): return lax.ppermute(value, 'arow', [(i, i ^ mask) for i in range(count)])  13.6 us
    ppermute x8, waiting for transfers between devices, exchange(): return lax.ppermute(value, 'arow', [(i, i ^ mask) for i in range(count)])  6.2 us
    pallas_call x1, Pallas kernels, consensus(): pl.pallas_call(functools.partial(consensus_kernel, offsets, width), out_s...  5.23 us
    pallas_call x1, Pallas kernels, prepare(): pl.pallas_call(functools.partial(prepare_kernel, width), out_shape=(jax.S...  1.96 us
    ppermute x1, starting transfers between devices, fast(): outer = lax.ppermute(feat_a, ('groups', 'arow'), outer_pairs(groups, count))  1.52 us
    concatenate x1, other arithmetic, fast(): near = lax.optimization_barrier(jnp.concatenate([feat_a, feat_b], axis=0))  0.78 us
    add x1, other arithmetic, pack(): packed += jnp.pad(f.transpose(1, 2, 0), ((3 * n, 10 - 3 * n), (0, 0), (0,...  0.75 us
    ppermute x1, waiting for transfers between devices, fast(): outer = lax.ppermute(feat_a, ('groups', 'arow'), outer_pairs(groups, count))  0.73 us
  transfers between devices with their start and end apart: 9, of which 8 were waited for; matrix products, arithmetic and copies ran while one was open for 5% of the time, Pallas kernels for 6%

profile of v4, /device:TPU:0, one launch (start us, length us, event | category | flops | bytes accessed | tf_op | source)
XLA Modules:
  0.0 32.2 jit_solution(13328027231604518392)
XLA Ops:
  0.0 3.5 %collective-permute-start = (bf16[1,32,256]{2,1,0:T(8,128)(2,1)}, bf16[1,32,256]{2,1,0:T(8,128)(2,1)S(1)}, u32[]{:S(2)}, u32[]{:S(2)}) collective-permute-start(bf16[1,32,256]{2,1,0:T(8,128)(2,1)} %param.9), channel_id=1, source_target_pairs={{0,9},{1,8},{2,11},{3,10},{4,13},{5,12},{6,15},{7,14},{8,1},{9,0},... | collective-permute-start | bytes 49160 | tf_op jit(solution)/shard_map/ppermute | solution.py:417
  3.5 0.8 %pad_maximum_fusion.3 = bf16[3,32,256]{2,1,0:T(8,128)(2,1)S(1)} fusion(bf16[1,32,256]{2,1,0:T(8,128)(2,1)} %param.9, bf16[2,32,256]{2,1,0:T(8,128)(2,1)} %param.8), kind=kLoop, calls=%fused_computation.4 | loop fusion | flops 24576 | bytes 98304 | tf_op jit(solution)/shard_map/concatenate | solution.py:440
  4.3 0.8 %pad_add_fusion.packed_ref = f32[13,3,8]{2,1,0:T(4,128)S(1)} fusion(f32[3,3,8]{2,1,0:T(4,128)} %bitcast.8, f32[3,3,8]{2,1,0:T(4,128)} %bitcast.9, f32[3,3,8]{2,1,0:T(4,128)} %bitcast.10, f32[3,3,8]{2,1,0:T(4,128)} %bitcast.11, f32[1,1,8]{2,1,0:T(1,128)} %bitcast.12), kind=kLoop, calls=%fused_computation.6 | loop fusion | flops 1248 | bytes 2432 | tf_op jit(solution)/shard_map/add | solution.py:247
  5.0 0.1 collective-permute-done
  5.1 1.9 %collective-permute-start.1 = (bf16[2,32,256]{2,1,0:T(8,128)(2,1)S(1)}, bf16[2,32,256]{2,1,0:T(8,128)(2,1)S(1)}, u32[]{:S(2)}, u32[]{:S(2)}) collective-permute-start(bf16[2,32,256]{2,1,0:T(8,128)(2,1)S(1)} %pad_maximum_fusion.4), channel_id=1, source_target_pairs={{0,5},{1,4},{2,7},{3,6},{4,1},{5,0},{6,3},{7,2},{8,13},{9,12},{10,... | collective-permute-start | bytes 98312 | tf_op jit(solution)/shard_map/ppermute | solution.py:417
  7.0 1.5 %collective-permute-start.3 = (bf16[2,32,256]{2,1,0:T(8,128)(2,1)}, bf16[2,32,256]{2,1,0:T(8,128)(2,1)S(1)}, u32[]{:S(2)}, u32[]{:S(2)}) collective-permute-start(bf16[2,32,256]{2,1,0:T(8,128)(2,1)} %param.8), channel_id=1, source_target_pairs={{0,16},{1,2},{2,1},{3,4},{4,3},{5,6},{6,5},{7,8},{8,7},{9,10},{10,... | collective-permute-start | bytes 98312 | tf_op jit(solution)/shard_map/ppermute | solution.py:447
  8.5 0.1 collective-permute-done.1
  8.6 1.8 %collective-permute-start.2 = (bf16[4,32,256]{2,1,0:T(8,128)(2,1)S(1)}, bf16[4,32,256]{2,1,0:T(8,128)(2,1)S(1)}, u32[]{:S(2)}, u32[]{:S(2)}) collective-permute-start(bf16[4,32,256]{2,1,0:T(8,128)(2,1)S(1)} %pad_maximum_fusion.2), channel_id=1, source_target_pairs={{0,3},{1,2},{2,1},{3,0},{4,7},{5,6},{6,5},{7,4},{8,11},{9,10},{10,... | collective-permute-start | bytes 196616 | tf_op jit(solution)/shard_map/ppermute | solution.py:417
  10.4 0.7 %collective-permute-done.3.outer_ref = bf16[2,32,256]{2,1,0:T(8,128)(2,1)S(1)} collective-permute-done((bf16[2,32,256]{2,1,0:T(8,128)(2,1)}, bf16[2,32,256]{2,1,0:T(8,128)(2,1)S(1)}, u32[]{:S(2)}, u32[]{:S(2)}) %collective-permute-start.3) | collective-permute-done | bytes 32800 | tf_op jit(solution)/shard_map/ppermute | solution.py:447
  11.2 2.0 %shard_map.82 = (bf16[8,512,256]{2,1,0:T(8,128)(2,1)S(1)}, bf16[8,256,256]{2,1,0:T(8,128)(2,1)S(1)}, f32[16,16,128]{2,1,0:T(8,128)S(1)}, f32[8,16,128]{2,1,0:T(8,128)S(1)}) custom-call(f32[13,3,8]{2,1,0:T(4,128)S(1)} %pad_add_fusion.packed_ref), custom_call_target="tpu_custom_call" | custom-call | flops 500000000 | bytes 3500000 | tf_op jit(solution)/shard_map/pallas_call | solution.py:253
  13.1 0.0 collective-permute-done.2
  13.2 0.2 collective-permute-start.4
  14.0 0.6 %collective-permute-done.4.mate_ref = bf16[10,32,256]{2,1,0:T(8,128)(2,1)S(1)} collective-permute-done((bf16[10,32,256]{2,1,0:T(8,128)(2,1)S(1)}, bf16[10,32,256]{2,1,0:T(8,128)(2,1)S(1)}, u32[]{:S(2)}, u32[]{:S(2)}) %collective-permute-start.4) | collective-permute-done | bytes 163872 | tf_op jit(solution)/shard_map/ppermute | solution.py:417
  14.6 5.2 %shard_map.83 = (f32[64,512]{1,0:T(8,128)S(1)}, f32[64,512]{1,0:T(8,128)S(1)}, f32[1,512]{1,0:T(1,128)S(1)}) custom-call(f32[1]{0:T(128)S(6)} %copy.9.bias2_ref, bf16[8,512,256]{2,1,0:T(8,128)(2,1)S(1)} %get-tuple-element.34.at1_ref, bf16[8,256,256]{2,1,0:T(8,128)(2,1)S(1)} %get-tuple-element.35.at2_ref, f32[16,16,128]{2,1,0:T(8,128)S(1)} %get-tuple-element.36.w1_ref, ...), custom_call_target="tpu_custom_call" | custom-call | flops 2000000000 | bytes 4500000 | tf_op jit(solution)/shard_map/pallas_call | solution.py:390
  19.9 3.2 %collective-permute-start.5 = (f32[1,512]{1,0:T(1,128)S(1)}, f32[1,512]{1,0:T(1,128)S(1)}, u32[]{:S(2)}, u32[]{:S(2)}) collective-permute-start(f32[1,512]{1,0:T(1,128)S(1)} %get-tuple-element.42), channel_id=1, source_target_pairs={{0,9},{1,8},{2,11},{3,10},{4,13},{5,12},{6,15},{7,14},{8,1},{9,0},... | collective-permute-start | bytes 6152 | tf_op jit(solution)/shard_map/ppermute | solution.py:417
  23.0 1.3 %collective-permute-done.5 = f32[1,512]{1,0:T(1,128)S(1)} collective-permute-done((f32[1,512]{1,0:T(1,128)S(1)}, f32[1,512]{1,0:T(1,128)S(1)}, u32[]{:S(2)}, u32[]{:S(2)}) %collective-permute-start.5) | collective-permute-done | bytes 2080 | tf_op jit(solution)/shard_map/ppermute | solution.py:417
  24.4 1.3 %collective-permute-start.6 = (f32[1,512]{1,0:T(1,128)S(1)}, f32[1,512]{1,0:T(1,128)S(1)}, u32[]{:S(2)}, u32[]{:S(2)}) collective-permute-start(f32[1,512]{1,0:T(1,128)S(1)} %max.12), channel_id=1, source_target_pairs={{0,5},{1,4},{2,7},{3,6},{4,1},{5,0},{6,3},{7,2},{8,13},{9,12},{10,... | collective-permute-start | bytes 6152 | tf_op jit(solution)/shard_map/ppermute | solution.py:417
  25.7 1.7 %collective-permute-done.6 = f32[1,512]{1,0:T(1,128)S(1)} collective-permute-done((f32[1,512]{1,0:T(1,128)S(1)}, f32[1,512]{1,0:T(1,128)S(1)}, u32[]{:S(2)}, u32[]{:S(2)}) %collective-permute-start.6) | collective-permute-done | bytes 2080 | tf_op jit(solution)/shard_map/ppermute | solution.py:417
  27.4 1.4 %collective-permute-start.7 = (f32[1,512]{1,0:T(1,128)S(1)}, f32[1,512]{1,0:T(1,128)S(1)}, u32[]{:S(2)}, u32[]{:S(2)}) collective-permute-start(f32[1,512]{1,0:T(1,128)S(1)} %max.13), channel_id=1, source_target_pairs={{0,3},{1,2},{2,1},{3,0},{4,7},{5,6},{6,5},{7,4},{8,11},{9,10},{10,... | collective-permute-start | bytes 6152 | tf_op jit(solution)/shard_map/ppermute | solution.py:417
  28.8 1.6 %collective-permute-done.7 = f32[1,512]{1,0:T(1,128)S(1)} collective-permute-done((f32[1,512]{1,0:T(1,128)S(1)}, f32[1,512]{1,0:T(1,128)S(1)}, u32[]{:S(2)}, u32[]{:S(2)}) %collective-permute-start.7) | collective-permute-done | bytes 2080 | tf_op jit(solution)/shard_map/ppermute | solution.py:417
  30.4 0.3 %collective-permute-start.8 = (f32[1,512]{1,0:T(1,128)S(1)}, f32[1,512]{1,0:T(1,128)S(1)}, u32[]{:S(2)}, u32[]{:S(2)}) collective-permute-start(f32[1,512]{1,0:T(1,128)S(1)} %max.14), channel_id=1, source_target_pairs={{0,1},{1,0},{2,3},{3,2},{4,5},{5,4},{6,7},{7,6},{8,9},{9,8},{10,11... | collective-permute-start | bytes 6152 | tf_op jit(solution)/shard_map/ppermute | solution.py:417
  30.7 0.8 %collective-permute-done.8 = f32[1,512]{1,0:T(1,128)S(1)} collective-permute-done((f32[1,512]{1,0:T(1,128)S(1)}, f32[1,512]{1,0:T(1,128)S(1)}, u32[]{:S(2)}, u32[]{:S(2)}) %collective-permute-start.8) | collective-permute-done | bytes 2080 | tf_op jit(solution)/shard_map/ppermute | solution.py:417
  31.6 0.7 %divide_multiply_fusion = f32[64,512]{1,0:T(8,128)} fusion(f32[64,512]{1,0:T(8,128)S(1)} %get-tuple-element.40, f32[64,512]{1,0:T(8,128)S(1)} %get-tuple-element.41, f32[512]{0:T(512)S(1)} %bitcast.7), kind=kLoop, calls=%fused_computation.2 | loop fusion | flops 65536 | bytes 395264 | tf_op jit(solution)/shard_map/mul | solution.py:463
  (10 shorter events, 0.1 us)
Async XLA Ops:
  0.0 5.1 %collective-permute-start = (bf16[1,32,256]{2,1,0:T(8,128)(2,1)}, bf16[1,32,256]{2,1,0:T(8,128)(2,1)S(1)}, u32[]{:S(2)}, u32[]{:S(2)}) collective-permute-start(bf16[1,32,256]{2,1,0:T(8,128)(2,1)} %param.9), channel_id=1, source_target_pairs={{0,9},{1,8},{2,11},{3,10},{4,13},{5,12},{6,15},{7,14},{8,1},{9,0},... | collective-permute-start | bytes 49160 | tf_op jit(solution)/shard_map/ppermute | solution.py:417
  5.1 3.5 %collective-permute-start.1 = (bf16[2,32,256]{2,1,0:T(8,128)(2,1)S(1)}, bf16[2,32,256]{2,1,0:T(8,128)(2,1)S(1)}, u32[]{:S(2)}, u32[]{:S(2)}) collective-permute-start(bf16[2,32,256]{2,1,0:T(8,128)(2,1)S(1)} %pad_maximum_fusion.4), channel_id=1, source_target_pairs={{0,5},{1,4},{2,7},{3,6},{4,1},{5,0},{6,3},{7,2},{8,13},{9,12},{10,... | collective-permute-start | bytes 98312 | tf_op jit(solution)/shard_map/ppermute | solution.py:417
  7.0 4.1 %collective-permute-start.3 = (bf16[2,32,256]{2,1,0:T(8,128)(2,1)}, bf16[2,32,256]{2,1,0:T(8,128)(2,1)S(1)}, u32[]{:S(2)}, u32[]{:S(2)}) collective-permute-start(bf16[2,32,256]{2,1,0:T(8,128)(2,1)} %param.8), channel_id=1, source_target_pairs={{0,16},{1,2},{2,1},{3,4},{4,3},{5,6},{6,5},{7,8},{8,7},{9,10},{10,... | collective-permute-start | bytes 98312 | tf_op jit(solution)/shard_map/ppermute | solution.py:447
  8.6 4.5 %collective-permute-start.2 = (bf16[4,32,256]{2,1,0:T(8,128)(2,1)S(1)}, bf16[4,32,256]{2,1,0:T(8,128)(2,1)S(1)}, u32[]{:S(2)}, u32[]{:S(2)}) collective-permute-start(bf16[4,32,256]{2,1,0:T(8,128)(2,1)S(1)} %pad_maximum_fusion.2), channel_id=1, source_target_pairs={{0,3},{1,2},{2,1},{3,0},{4,7},{5,6},{6,5},{7,4},{8,11},{9,10},{10,... | collective-permute-start | bytes 196616 | tf_op jit(solution)/shard_map/ppermute | solution.py:417
  13.2 1.5 %collective-permute-start.4 = (bf16[10,32,256]{2,1,0:T(8,128)(2,1)S(1)}, bf16[10,32,256]{2,1,0:T(8,128)(2,1)S(1)}, u32[]{:S(2)}, u32[]{:S(2)}) collective-permute-start(bf16[10,32,256]{2,1,0:T(8,128)(2,1)S(1)} %pad_maximum_fusion.own_ref), channel_id=1, source_target_pairs={{0,1},{1,0},{2,3},{3,2},{4,5},{5,4},{6,7},{7,6},{8,9},{9,8},{10,11... | collective-permute-start | bytes 491528 | tf_op jit(solution)/shard_map/ppermute | solution.py:417
  19.9 4.5 %collective-permute-start.5 = (f32[1,512]{1,0:T(1,128)S(1)}, f32[1,512]{1,0:T(1,128)S(1)}, u32[]{:S(2)}, u32[]{:S(2)}) collective-permute-start(f32[1,512]{1,0:T(1,128)S(1)} %get-tuple-element.42), channel_id=1, source_target_pairs={{0,9},{1,8},{2,11},{3,10},{4,13},{5,12},{6,15},{7,14},{8,1},{9,0},... | collective-permute-start | bytes 6152 | tf_op jit(solution)/shard_map/ppermute | solution.py:417
  24.4 3.0 %collective-permute-start.6 = (f32[1,512]{1,0:T(1,128)S(1)}, f32[1,512]{1,0:T(1,128)S(1)}, u32[]{:S(2)}, u32[]{:S(2)}) collective-permute-start(f32[1,512]{1,0:T(1,128)S(1)} %max.12), channel_id=1, source_target_pairs={{0,5},{1,4},{2,7},{3,6},{4,1},{5,0},{6,3},{7,2},{8,13},{9,12},{10,... | collective-permute-start | bytes 6152 | tf_op jit(solution)/shard_map/ppermute | solution.py:417
  27.4 3.0 %collective-permute-start.7 = (f32[1,512]{1,0:T(1,128)S(1)}, f32[1,512]{1,0:T(1,128)S(1)}, u32[]{:S(2)}, u32[]{:S(2)}) collective-permute-start(f32[1,512]{1,0:T(1,128)S(1)} %max.13), channel_id=1, source_target_pairs={{0,3},{1,2},{2,1},{3,0},{4,7},{5,6},{6,5},{7,4},{8,11},{9,10},{10,... | collective-permute-start | bytes 6152 | tf_op jit(solution)/shard_map/ppermute | solution.py:417
  30.4 1.2 %collective-permute-start.8 = (f32[1,512]{1,0:T(1,128)S(1)}, f32[1,512]{1,0:T(1,128)S(1)}, u32[]{:S(2)}, u32[]{:S(2)}) collective-permute-start(f32[1,512]{1,0:T(1,128)S(1)} %max.14), channel_id=1, source_target_pairs={{0,1},{1,0},{2,3},{3,2},{4,5},{5,4},{6,7},{7,6},{8,9},{9,8},{10,11... | collective-permute-start | bytes 6152 | tf_op jit(solution)/shard_map/ppermute | solution.py:417

commit v5 on v4

--- a/solution.py
+++ b/solution.py
@@ -128,10 +128,7 @@
     return high, (value - high.astype(F32)).astype(BF16)
 
 
-def first_weights(taps, at_ref, k, width):
-    col = lane((width, 128)) % width
-    diag = [sublane((width, 128)) + 1 - col == w for w in range(3)]
-    row = lane((1, 128)) // width
+def first_weights(taps, at_ref, k, width, diag, row_is):
     for net in range(2):
         lanes = slice(128 * net, 128 * net + 128)
         for cr in range(6):
@@ -140,7 +137,7 @@
                 per_lane = jnp.zeros((1, 128), F32)
                 for u in range(3):
                     if 0 <= cr - u <= 3:
-                        per_lane = jnp.where(row == cr - u, taps[net](u, w, k), per_lane)
+                        per_lane = jnp.where(row_is[cr - u], taps[net][3 * u + w], per_lane)
                 block = jnp.where(diag[w], per_lane, block)
             high, low = two_terms(block)
             at_ref[k, cr * width : (cr + 1) * width, lanes] = high
@@ -149,10 +146,7 @@
             at_ref[k, base * width : (base + 2) * width, lanes] = jnp.zeros((2 * width, 128), BF16)
 
 
-def second_weights(taps, at_ref, k, width, keep):
-    col = lane((width, 128)) % width
-    diag = [sublane((width, 128)) + 1 - col == w for w in range(3)]
-    row = lane((1, 128)) // width
+def second_weights(taps, at_ref, k, width, keep, diag, row_is):
     for net in range(2):
         for hr in range(4):
             block = jnp.zeros((width, 128), F32)
@@ -160,10 +154,11 @@
                 per_lane = jnp.zeros((1, 128), F32)
                 for u in range(3):
                     if 0 <= hr - u <= 1:
-                        tap = taps[net](u, w, k)
-                        if hr in keep:
-                            tap = tap * keep[hr]
-                        per_lane = jnp.where(row == 2 * net + hr - u, tap, per_lane)
+                        per_lane = jnp.where(
+                            row_is[2 * net + hr - u], taps[net][3 * u + w], per_lane
+                        )
+                if hr in keep:
+                    per_lane = per_lane * keep[hr]
                 block = jnp.where(diag[w], per_lane, block)
             high, low = two_terms(block)
             rows = slice((4 * net + hr) * width, (4 * net + hr + 1) * width)
@@ -219,25 +214,24 @@
         3: (index != lax.axis_size("arow") - 1).astype(F32),
     }
 
-    def bank(n):
-        return lambda u, w, k: packed_ref[3 * n + u, w, k]
-
-    first = (bank(0), bank(1))
-    second = (bank(2), bank(3))
     half_lanes = lane((1, 128)) < 64
+    col = lane((width, 128)) % width
+    diag = [sublane((width, 128)) + 1 - col == w for w in range(3)]
+    row_is = [lane((1, 128)) // width == r for r in range(4)]
     for k in range(8):
-        first_weights(first, at1_ref, k, width)
-        second_weights(second, at2_ref, k, width, keep)
-        places = [(tap // 3, tap % 3, k) for tap in range(9)]
+        banks = [
+            [jnp.full((1, 128), packed_ref[3 * n + tap // 3, tap % 3, k], F32) for tap in range(9)]
+            for n in range(4)
+        ]
+        first, second = banks[0:2], banks[2:4]
+        first_weights(first, at1_ref, k, width, diag, row_is)
+        second_weights(second, at2_ref, k, width, keep, diag, row_is)
         for net in range(2):
-            rows = minimal_filter([jnp.full((1, 128), first[1 - net](*at), F32) for at in places])
-            for n, row in enumerate(rows):
+            for n, row in enumerate(minimal_filter(first[1 - net])):
                 w1_ref[2 * k + net, n : n + 1] = row
             w1_ref[2 * k + net, 12:13] = jnp.full((1, 128), packed_ref[12, 0, k], F32)
-        rows = minimal_filter(
-            [jnp.where(half_lanes, second[1](*at), second[0](*at)) for at in places]
-        )
-        for n, row in enumerate(rows):
+        mixed = [jnp.where(half_lanes, second[1][tap], second[0][tap]) for tap in range(9)]
+        for n, row in enumerate(minimal_filter(mixed)):
             w2_ref[k, n : n + 1] = row
 
 
@@ -262,7 +256,7 @@
         out_specs=(vmem,) * 4,
         compiler_params=pltpu.CompilerParams(vmem_limit_bytes=16 << 20),
         cost_estimate=pl.CostEstimate(
-            flops=500_000_000, bytes_accessed=3_500_000, transcendentals=0
+            flops=2_000_000_000, bytes_accessed=3_500_000, transcendentals=0
         ),
     )(packed)
 
@@ -279,7 +273,6 @@
     mate_ref,
     outer_ref,
     score_ref,
-    part_ref,
     best_ref,
     fa_ref,
     vf_ref,
@@ -377,9 +370,7 @@
     turned = jnp.transpose(nat_ref[...], (1, 0))
     score = turned[0:64] + turned[64:128]
     best_ref[...] = jnp.max(score, axis=0, keepdims=True)
-    best_b = jnp.max(score, axis=1, keepdims=True)
     score_ref[...] = score
-    part_ref[...] = score * (score / (best_b + EPSILON))
 
 
 def consensus(bias_second, weights, own, mate, outer, offsets, width):
@@ -391,11 +382,10 @@
         functools.partial(consensus_kernel, offsets, width),
         out_shape=(
             jax.ShapeDtypeStruct((2 * width, cells), F32),
-            jax.ShapeDtypeStruct((2 * width, cells), F32),
             jax.ShapeDtypeStruct((1, cells), F32),
         ),
         in_specs=[pl.BlockSpec(memory_space=pltpu.SMEM)] + [vmem] * 7,
-        out_specs=(vmem, vmem, vmem),
+        out_specs=(vmem, vmem),
         scratch_shapes=[
             pltpu.VMEM((8, width, channels), BF16),
             pltpu.VMEM((2, cells, 128), F32),
@@ -446,7 +436,7 @@
             feat_a, held, packed = lax.optimization_barrier((feat_a, held, packed))
             outer = lax.ppermute(feat_a, ("groups", "arow"), outer_pairs(groups, count))
         if n == 2:
-            packed, outer = lax.optimization_barrier((packed, outer))
+            packed, held = lax.optimization_barrier((packed, held))
             weights = prepare(packed, width)
         received = exchange(held, mask, count)
         held = jnp.concatenate([near_b if n == 0 else held, received], axis=0)
@@ -457,7 +447,10 @@
     own = jnp.concatenate([held, near_a], axis=0)
     mate = exchange(own, 1, count)
 
-    score, part, best = consensus(bias_second, weights, own, mate, outer, offsets, width)
+    score, best = consensus(bias_second, weights, own, mate, outer, offsets, width)
+    part = lax.optimization_barrier(
+        score * (score / (jnp.max(score, axis=1, keepdims=True) + EPSILON))
+    )
     for mask in masks + [1]:
         best = jnp.maximum(best, exchange(best, mask, count))
     out = part * (score / (best + EPSILON))

time: 32.5 us -> 32.1 us (0.988)
  waiting for transfers between devices: 6.94 us -> 5.63 us
  starting transfers between devices: 15.1 us -> 15.9 us
    ppermute x8, starting transfers between devices: 13.6 us -> 14.4 us  [exchange(): return lax.ppermute(value, 'arow', [(i, i ^ mask) for i in range(count)])]
    ppermute x1, waiting for transfers between devices: 0.73 us -> 0.01 us  [fast(): outer = lax.ppermute(feat_a, ('groups', 'arow'), outer_pairs(groups, count))]
    ppermute x8, waiting for transfers between devices: 6.2 us -> 5.63 us  [exchange(): return lax.ppermute(value, 'arow', [(i, i ^ mask) for i in range(count)])]
  transfers between devices with their start and end apart: 9 -> 9, of which waited for: 8 -> 8; matrix products, arithmetic and copies ran while one was open for 5% -> 6% of each run, Pallas kernels for 6% -> 6%
where the time goes in v5:
time: 32.1 us; the launch traced here: 31.8 us
  starting transfers between devices  15.9 us (50%)
  Pallas kernels  7.09 us (22%)
  waiting for transfers between devices  5.63 us (18%)
  other arithmetic  2.47 us (8%)
  between operations  0.72 us (2%)
    ppermute x8, starting transfers between devices, exchange(): return lax.ppermute(value, 'arow', [(i, i ^ mask) for i in range(count)])  14.4 us
    ppermute x8, waiting for transfers between devices, exchange(): return lax.ppermute(value, 'arow', [(i, i ^ mask) for i in range(count)])  5.63 us
    pallas_call x1, Pallas kernels, consensus(): pl.pallas_call(functools.partial(consensus_kernel, offsets, width), out_s...  5.15 us
    pallas_call x1, Pallas kernels, prepare(): pl.pallas_call(functools.partial(prepare_kernel, width), out_shape=(jax.S...  1.94 us
    ppermute x1, starting transfers between devices, fast(): outer = lax.ppermute(feat_a, ('groups', 'arow'), outer_pairs(groups, count))  1.52 us
    concatenate x1, other arithmetic, fast(): near = lax.optimization_barrier(jnp.concatenate([feat_a, feat_b], axis=0))  0.78 us
    add x1, other arithmetic, pack(): packed += jnp.pad(f.transpose(1, 2, 0), ((3 * n, 10 - 3 * n), (0, 0), (0,...  0.75 us
    mul x1, other arithmetic, fast(): out = part * (score / (best + EPSILON))  0.68 us
  transfers between devices with their start and end apart: 9, of which 8 were waited for; matrix products, arithmetic and copies ran while one was open for 6% of the time, Pallas kernels for 6%

profile of v5, /device:TPU:0, one launch (start us, length us, event | category | flops | bytes accessed | tf_op | source)
XLA Modules:
  0.0 31.8 jit_solution(18245315604194075180)
XLA Ops:
  0.0 3.5 %collective-permute-start = (bf16[1,32,256]{2,1,0:T(8,128)(2,1)}, bf16[1,32,256]{2,1,0:T(8,128)(2,1)S(1)}, u32[]{:S(2)}, u32[]{:S(2)}) collective-permute-start(bf16[1,32,256]{2,1,0:T(8,128)(2,1)} %param.9), channel_id=1, source_target_pairs={{0,9},{1,8},{2,11},{3,10},{4,13},{5,12},{6,15},{7,14},{8,1},{9,0},... | collective-permute-start | bytes 49160 | tf_op jit(solution)/shard_map/ppermute | solution.py:407
  3.5 0.8 %pad_maximum_fusion.3 = bf16[3,32,256]{2,1,0:T(8,128)(2,1)S(1)} fusion(bf16[1,32,256]{2,1,0:T(8,128)(2,1)} %param.9, bf16[2,32,256]{2,1,0:T(8,128)(2,1)} %param.8), kind=kLoop, calls=%fused_computation.5 | loop fusion | flops 24576 | bytes 98304 | tf_op jit(solution)/shard_map/concatenate | solution.py:430
  4.3 0.8 %pad_add_fusion.packed_ref = f32[13,3,8]{2,1,0:T(4,128)S(1)} fusion(f32[3,3,8]{2,1,0:T(4,128)} %bitcast.8, f32[3,3,8]{2,1,0:T(4,128)} %bitcast.9, f32[3,3,8]{2,1,0:T(4,128)} %bitcast.10, f32[3,3,8]{2,1,0:T(4,128)} %bitcast.11, f32[1,1,8]{2,1,0:T(1,128)} %bitcast.12), kind=kLoop, calls=%fused_computation.7 | loop fusion | flops 1248 | bytes 2432 | tf_op jit(solution)/shard_map/add | solution.py:241
  5.0 0.1 collective-permute-done
  5.1 1.9 %collective-permute-start.1 = (bf16[2,32,256]{2,1,0:T(8,128)(2,1)S(1)}, bf16[2,32,256]{2,1,0:T(8,128)(2,1)S(1)}, u32[]{:S(2)}, u32[]{:S(2)}) collective-permute-start(bf16[2,32,256]{2,1,0:T(8,128)(2,1)S(1)} %pad_maximum_fusion.4), channel_id=1, source_target_pairs={{0,5},{1,4},{2,7},{3,6},{4,1},{5,0},{6,3},{7,2},{8,13},{9,12},{10,... | collective-permute-start | bytes 98312 | tf_op jit(solution)/shard_map/ppermute | solution.py:407
  7.0 1.5 %collective-permute-start.3 = (bf16[2,32,256]{2,1,0:T(8,128)(2,1)}, bf16[2,32,256]{2,1,0:T(8,128)(2,1)S(1)}, u32[]{:S(2)}, u32[]{:S(2)}) collective-permute-start(bf16[2,32,256]{2,1,0:T(8,128)(2,1)} %param.8), channel_id=1, source_target_pairs={{0,16},{1,2},{2,1},{3,4},{4,3},{5,6},{6,5},{7,8},{8,7},{9,10},{10,... | collective-permute-start | bytes 98312 | tf_op jit(solution)/shard_map/ppermute | solution.py:437
  8.5 0.1 collective-permute-done.1
  8.6 1.8 %collective-permute-start.2 = (bf16[4,32,256]{2,1,0:T(8,128)(2,1)S(1)}, bf16[4,32,256]{2,1,0:T(8,128)(2,1)S(1)}, u32[]{:S(2)}, u32[]{:S(2)}) collective-permute-start(bf16[4,32,256]{2,1,0:T(8,128)(2,1)S(1)} %pad_maximum_fusion.2), channel_id=1, source_target_pairs={{0,3},{1,2},{2,1},{3,0},{4,7},{5,6},{6,5},{7,4},{8,11},{9,10},{10,... | collective-permute-start | bytes 196616 | tf_op jit(solution)/shard_map/ppermute | solution.py:407
  10.4 1.9 %shard_map.82 = (bf16[8,512,256]{2,1,0:T(8,128)(2,1)S(1)}, bf16[8,256,256]{2,1,0:T(8,128)(2,1)S(1)}, f32[16,16,128]{2,1,0:T(8,128)S(1)}, f32[8,16,128]{2,1,0:T(8,128)S(1)}) custom-call(f32[13,3,8]{2,1,0:T(4,128)S(1)} %pad_add_fusion.packed_ref), custom_call_target="tpu_custom_call" | custom-call | flops 2000000000 | bytes 3500000 | tf_op jit(solution)/shard_map/pallas_call | solution.py:247
  12.4 0.2 collective-permute-done.2
  12.6 0.0 collective-permute-done.3.outer_ref
  12.7 0.4 %collective-permute-start.4 = (bf16[10,32,256]{2,1,0:T(8,128)(2,1)S(1)}, bf16[10,32,256]{2,1,0:T(8,128)(2,1)S(1)}, u32[]{:S(2)}, u32[]{:S(2)}) collective-permute-start(bf16[10,32,256]{2,1,0:T(8,128)(2,1)S(1)} %pad_maximum_fusion.own_ref), channel_id=1, source_target_pairs={{0,1},{1,0},{2,3},{3,2},{4,5},{5,4},{6,7},{7,6},{8,9},{9,8},{10,11... | collective-permute-start | bytes 491528 | tf_op jit(solution)/shard_map/ppermute | solution.py:407
  13.7 0.4 %collective-permute-done.4.mate_ref = bf16[10,32,256]{2,1,0:T(8,128)(2,1)S(1)} collective-permute-done((bf16[10,32,256]{2,1,0:T(8,128)(2,1)S(1)}, bf16[10,32,256]{2,1,0:T(8,128)(2,1)S(1)}, u32[]{:S(2)}, u32[]{:S(2)}) %collective-permute-start.4) | collective-permute-done | bytes 163872 | tf_op jit(solution)/shard_map/ppermute | solution.py:407
  14.1 5.2 %shard_map.83 = (f32[64,512]{1,0:T(8,128)S(1)}, f32[1,512]{1,0:T(1,128)S(1)}) custom-call(f32[1]{0:T(128)S(6)} %copy.9.bias2_ref, bf16[8,512,256]{2,1,0:T(8,128)(2,1)S(1)} %get-tuple-element.33.at1_ref, bf16[8,256,256]{2,1,0:T(8,128)(2,1)S(1)} %get-tuple-element.34.at2_ref, f32[16,16,128]{2,1,0:T(8,128)S(1)} %get-tuple-element.35.w1_ref, ...), custom_call_target="tpu_custom_call" | custom-call | flops 2000000000 | bytes 4500000 | tf_op jit(solution)/shard_map/pallas_call | solution.py:381
  19.3 3.3 %collective-permute-start.5 = (f32[1,512]{1,0:T(1,128)S(1)}, f32[1,512]{1,0:T(1,128)S(1)}, u32[]{:S(2)}, u32[]{:S(2)}) collective-permute-start(f32[1,512]{1,0:T(1,128)S(1)} %get-tuple-element.40), channel_id=1, source_target_pairs={{0,9},{1,8},{2,11},{3,10},{4,13},{5,12},{6,15},{7,14},{8,1},{9,0},... | collective-permute-start | bytes 6152 | tf_op jit(solution)/shard_map/ppermute | solution.py:407
  22.5 1.3 %collective-permute-done.5 = f32[1,512]{1,0:T(1,128)S(1)} collective-permute-done((f32[1,512]{1,0:T(1,128)S(1)}, f32[1,512]{1,0:T(1,128)S(1)}, u32[]{:S(2)}, u32[]{:S(2)}) %collective-permute-start.5) | collective-permute-done | bytes 2080 | tf_op jit(solution)/shard_map/ppermute | solution.py:407
  23.8 1.8 %collective-permute-start.6 = (f32[1,512]{1,0:T(1,128)S(1)}, f32[1,512]{1,0:T(1,128)S(1)}, u32[]{:S(2)}, u32[]{:S(2)}) collective-permute-start(f32[1,512]{1,0:T(1,128)S(1)} %max.12), channel_id=1, source_target_pairs={{0,5},{1,4},{2,7},{3,6},{4,1},{5,0},{6,3},{7,2},{8,13},{9,12},{10,... | collective-permute-start | bytes 6152 | tf_op jit(solution)/shard_map/ppermute | solution.py:407
  25.6 0.1 reduce_max.9
  25.7 1.2 %collective-permute-done.6 = f32[1,512]{1,0:T(1,128)S(1)} collective-permute-done((f32[1,512]{1,0:T(1,128)S(1)}, f32[1,512]{1,0:T(1,128)S(1)}, u32[]{:S(2)}, u32[]{:S(2)}) %collective-permute-start.6) | collective-permute-done | bytes 2080 | tf_op jit(solution)/shard_map/ppermute | solution.py:407
  26.9 1.6 %collective-permute-start.7 = (f32[1,512]{1,0:T(1,128)S(1)}, f32[1,512]{1,0:T(1,128)S(1)}, u32[]{:S(2)}, u32[]{:S(2)}) collective-permute-start(f32[1,512]{1,0:T(1,128)S(1)} %max.13), channel_id=1, source_target_pairs={{0,3},{1,2},{2,1},{3,0},{4,7},{5,6},{6,5},{7,4},{8,11},{9,10},{10,... | collective-permute-start | bytes 6152 | tf_op jit(solution)/shard_map/ppermute | solution.py:407
  28.5 1.5 %collective-permute-done.7 = f32[1,512]{1,0:T(1,128)S(1)} collective-permute-done((f32[1,512]{1,0:T(1,128)S(1)}, f32[1,512]{1,0:T(1,128)S(1)}, u32[]{:S(2)}, u32[]{:S(2)}) %collective-permute-start.7) | collective-permute-done | bytes 2080 | tf_op jit(solution)/shard_map/ppermute | solution.py:407
  29.9 0.3 collective-permute-start.8
  30.2 0.1 divide_multiply_fusion
  30.3 0.8 %collective-permute-done.8 = f32[1,512]{1,0:T(1,128)S(1)} collective-permute-done((f32[1,512]{1,0:T(1,128)S(1)}, f32[1,512]{1,0:T(1,128)S(1)}, u32[]{:S(2)}, u32[]{:S(2)}) %collective-permute-start.8) | collective-permute-done | bytes 2080 | tf_op jit(solution)/shard_map/ppermute | solution.py:407
  31.1 0.7 %divide_multiply_fusion.1 = f32[64,512]{1,0:T(8,128)} fusion(f32[64,512]{1,0:T(8,128)S(1)} %divide_multiply_fusion, f32[64,512]{1,0:T(8,128)S(1)} %get-tuple-element.39, f32[512]{0:T(512)S(1)} %bitcast.7), kind=kLoop, calls=%fused_computation.3 | loop fusion | flops 65536 | bytes 395264 | tf_op jit(solution)/shard_map/mul | solution.py:456
  (11 shorter events, 0.1 us)
Async XLA Ops:
  0.0 5.1 %collective-permute-start = (bf16[1,32,256]{2,1,0:T(8,128)(2,1)}, bf16[1,32,256]{2,1,0:T(8,128)(2,1)S(1)}, u32[]{:S(2)}, u32[]{:S(2)}) collective-permute-start(bf16[1,32,256]{2,1,0:T(8,128)(2,1)} %param.9), channel_id=1, source_target_pairs={{0,9},{1,8},{2,11},{3,10},{4,13},{5,12},{6,15},{7,14},{8,1},{9,0},... | collective-permute-start | bytes 49160 | tf_op jit(solution)/shard_map/ppermute | solution.py:407
  5.1 3.5 %collective-permute-start.1 = (bf16[2,32,256]{2,1,0:T(8,128)(2,1)S(1)}, bf16[2,32,256]{2,1,0:T(8,128)(2,1)S(1)}, u32[]{:S(2)}, u32[]{:S(2)}) collective-permute-start(bf16[2,32,256]{2,1,0:T(8,128)(2,1)S(1)} %pad_maximum_fusion.4), channel_id=1, source_target_pairs={{0,5},{1,4},{2,7},{3,6},{4,1},{5,0},{6,3},{7,2},{8,13},{9,12},{10,... | collective-permute-start | bytes 98312 | tf_op jit(solution)/shard_map/ppermute | solution.py:407
  7.0 5.6 %collective-permute-start.3 = (bf16[2,32,256]{2,1,0:T(8,128)(2,1)}, bf16[2,32,256]{2,1,0:T(8,128)(2,1)S(1)}, u32[]{:S(2)}, u32[]{:S(2)}) collective-permute-start(bf16[2,32,256]{2,1,0:T(8,128)(2,1)} %param.8), channel_id=1, source_target_pairs={{0,16},{1,2},{2,1},{3,4},{4,3},{5,6},{6,5},{7,8},{8,7},{9,10},{10,... | collective-permute-start | bytes 98312 | tf_op jit(solution)/shard_map/ppermute | solution.py:437
  8.6 4.0 %collective-permute-start.2 = (bf16[4,32,256]{2,1,0:T(8,128)(2,1)S(1)}, bf16[4,32,256]{2,1,0:T(8,128)(2,1)S(1)}, u32[]{:S(2)}, u32[]{:S(2)}) collective-permute-start(bf16[4,32,256]{2,1,0:T(8,128)(2,1)S(1)} %pad_maximum_fusion.2), channel_id=1, source_target_pairs={{0,3},{1,2},{2,1},{3,0},{4,7},{5,6},{6,5},{7,4},{8,11},{9,10},{10,... | collective-permute-start | bytes 196616 | tf_op jit(solution)/shard_map/ppermute | solution.py:407
  12.7 1.5 %collective-permute-start.4 = (bf16[10,32,256]{2,1,0:T(8,128)(2,1)S(1)}, bf16[10,32,256]{2,1,0:T(8,128)(2,1)S(1)}, u32[]{:S(2)}, u32[]{:S(2)}) collective-permute-start(bf16[10,32,256]{2,1,0:T(8,128)(2,1)S(1)} %pad_maximum_fusion.own_ref), channel_id=1, source_target_pairs={{0,1},{1,0},{2,3},{3,2},{4,5},{5,4},{6,7},{7,6},{8,9},{9,8},{10,11... | collective-permute-start | bytes 491528 | tf_op jit(solution)/shard_map/ppermute | solution.py:407
  19.3 4.6 %collective-permute-start.5 = (f32[1,512]{1,0:T(1,128)S(1)}, f32[1,512]{1,0:T(1,128)S(1)}, u32[]{:S(2)}, u32[]{:S(2)}) collective-permute-start(f32[1,512]{1,0:T(1,128)S(1)} %get-tuple-element.40), channel_id=1, source_target_pairs={{0,9},{1,8},{2,11},{3,10},{4,13},{5,12},{6,15},{7,14},{8,1},{9,0},... | collective-permute-start | bytes 6152 | tf_op jit(solution)/shard_map/ppermute | solution.py:407
  23.8 3.1 %collective-permute-start.6 = (f32[1,512]{1,0:T(1,128)S(1)}, f32[1,512]{1,0:T(1,128)S(1)}, u32[]{:S(2)}, u32[]{:S(2)}) collective-permute-start(f32[1,512]{1,0:T(1,128)S(1)} %max.12), channel_id=1, source_target_pairs={{0,5},{1,4},{2,7},{3,6},{4,1},{5,0},{6,3},{7,2},{8,13},{9,12},{10,... | collective-permute-start | bytes 6152 | tf_op jit(solution)/shard_map/ppermute | solution.py:407
  26.9 3.0 %collective-permute-start.7 = (f32[1,512]{1,0:T(1,128)S(1)}, f32[1,512]{1,0:T(1,128)S(1)}, u32[]{:S(2)}, u32[]{:S(2)}) collective-permute-start(f32[1,512]{1,0:T(1,128)S(1)} %max.13), channel_id=1, source_target_pairs={{0,3},{1,2},{2,1},{3,0},{4,7},{5,6},{6,5},{7,4},{8,11},{9,10},{10,... | collective-permute-start | bytes 6152 | tf_op jit(solution)/shard_map/ppermute | solution.py:407
  29.9 1.2 %collective-permute-start.8 = (f32[1,512]{1,0:T(1,128)S(1)}, f32[1,512]{1,0:T(1,128)S(1)}, u32[]{:S(2)}, u32[]{:S(2)}) collective-permute-start(f32[1,512]{1,0:T(1,128)S(1)} %max.14), channel_id=1, source_target_pairs={{0,1},{1,0},{2,3},{3,2},{4,5},{5,4},{6,7},{7,6},{8,9},{9,8},{10,11... | collective-permute-start | bytes 6152 | tf_op jit(solution)/shard_map/ppermute | solution.py:407

commit v6 on v5

--- a/solution.py
+++ b/solution.py
@@ -311,7 +311,7 @@
                     :, 128 * c : 128 * c + 128
                 ]
     for c in range(4):
-        vp_ref[:, 128 * c : 128 * c + 128] = vf_ref[c % 2].astype(BF16)
+        vp_ref[:, 128 * c : 128 * c + 128] = vf_ref[c % 2, 0 : 2 * half * width].astype(BF16)
 
     def spread(k):
         s_ref[k % 2] = jnp.dot(vp_ref[...], at1_ref[k], preferred_element_type=F32)
@@ -367,7 +367,7 @@
             next(twos, None)
             next(ones, None)
 
-    turned = jnp.transpose(nat_ref[...], (1, 0))
+    turned = jnp.transpose(nat_ref[0 : 2 * half * width], (1, 0))
     score = turned[0:64] + turned[64:128]
     best_ref[...] = jnp.max(score, axis=0, keepdims=True)
     score_ref[...] = score
@@ -388,13 +388,13 @@
         out_specs=(vmem, vmem),
         scratch_shapes=[
             pltpu.VMEM((8, width, channels), BF16),
-            pltpu.VMEM((2, cells, 128), F32),
+            pltpu.VMEM((2, cells + 16, 128), F32),
             pltpu.VMEM((cells, 512), BF16),
             pltpu.VMEM((2, cells, 256), F32),
             pltpu.VMEM((2, cells, 256), BF16),
             pltpu.VMEM((2, cells, 128), F32),
             pltpu.VMEM((4, cells // 2, 128), F32),
-            pltpu.VMEM((cells, 128), F32),
+            pltpu.VMEM((cells + 2 * width, 128), F32),
         ],
         compiler_params=pltpu.CompilerParams(vmem_limit_bytes=32 << 20),
         cost_estimate=pl.CostEstimate(

time: 32.1 us -> 32.1 us (level)
  no operation moved by 1% of the time
where the time goes in v6:
time: 32.1 us; the launch traced here: 31.8 us
  starting transfers between devices  15.9 us (50%)
  Pallas kernels  7.09 us (22%)
  waiting for transfers between devices  5.63 us (18%)
  other arithmetic  2.47 us (8%)
  between operations  0.72 us (2%)
    ppermute x8, starting transfers between devices, exchange(): return lax.ppermute(value, 'arow', [(i, i ^ mask) for i in range(count)])  14.4 us
    ppermute x8, waiting for transfers between devices, exchange(): return lax.ppermute(value, 'arow', [(i, i ^ mask) for i in range(count)])  5.63 us
    pallas_call x1, Pallas kernels, consensus(): pl.pallas_call(functools.partial(consensus_kernel, offsets, width), out_s...  5.15 us
    pallas_call x1, Pallas kernels, prepare(): pl.pallas_call(functools.partial(prepare_kernel, width), out_shape=(jax.S...  1.94 us
    ppermute x1, starting transfers between devices, fast(): outer = lax.ppermute(feat_a, ('groups', 'arow'), outer_pairs(groups, count))  1.52 us
    concatenate x1, other arithmetic, fast(): near = lax.optimization_barrier(jnp.concatenate([feat_a, feat_b], axis=0))  0.78 us
    add x1, other arithmetic, pack(): packed += jnp.pad(f.transpose(1, 2, 0), ((3 * n, 10 - 3 * n), (0, 0), (0,...  0.75 us
    mul x1, other arithmetic, fast(): out = part * (score / (best + EPSILON))  0.68 us
  transfers between devices with their start and end apart: 9, of which 8 were waited for; matrix products, arithmetic and copies ran while one was open for 6% of the time, Pallas kernels for 6%

profile of v6, /device:TPU:0, one launch (start us, length us, event | category | flops | bytes accessed | tf_op | source)
XLA Modules:
  0.0 31.8 jit_solution(7656009906001797767)
XLA Ops:
  0.0 3.5 %collective-permute-start = (bf16[1,32,256]{2,1,0:T(8,128)(2,1)}, bf16[1,32,256]{2,1,0:T(8,128)(2,1)S(1)}, u32[]{:S(2)}, u32[]{:S(2)}) collective-permute-start(bf16[1,32,256]{2,1,0:T(8,128)(2,1)} %param.9), channel_id=1, source_target_pairs={{0,9},{1,8},{2,11},{3,10},{4,13},{5,12},{6,15},{7,14},{8,1},{9,0},... | collective-permute-start | bytes 49160 | tf_op jit(solution)/shard_map/ppermute | solution.py:407
  3.5 0.8 %pad_maximum_fusion.3 = bf16[3,32,256]{2,1,0:T(8,128)(2,1)S(1)} fusion(bf16[1,32,256]{2,1,0:T(8,128)(2,1)} %param.9, bf16[2,32,256]{2,1,0:T(8,128)(2,1)} %param.8), kind=kLoop, calls=%fused_computation.5 | loop fusion | flops 24576 | bytes 98304 | tf_op jit(solution)/shard_map/concatenate | solution.py:430
  4.3 0.8 %pad_add_fusion.packed_ref = f32[13,3,8]{2,1,0:T(4,128)S(1)} fusion(f32[3,3,8]{2,1,0:T(4,128)} %bitcast.8, f32[3,3,8]{2,1,0:T(4,128)} %bitcast.9, f32[3,3,8]{2,1,0:T(4,128)} %bitcast.10, f32[3,3,8]{2,1,0:T(4,128)} %bitcast.11, f32[1,1,8]{2,1,0:T(1,128)} %bitcast.12), kind=kLoop, calls=%fused_computation.7 | loop fusion | flops 1248 | bytes 2432 | tf_op jit(solution)/shard_map/add | solution.py:241
  5.0 0.1 collective-permute-done
  5.1 1.9 %collective-permute-start.1 = (bf16[2,32,256]{2,1,0:T(8,128)(2,1)S(1)}, bf16[2,32,256]{2,1,0:T(8,128)(2,1)S(1)}, u32[]{:S(2)}, u32[]{:S(2)}) collective-permute-start(bf16[2,32,256]{2,1,0:T(8,128)(2,1)S(1)} %pad_maximum_fusion.4), channel_id=1, source_target_pairs={{0,5},{1,4},{2,7},{3,6},{4,1},{5,0},{6,3},{7,2},{8,13},{9,12},{10,... | collective-permute-start | bytes 98312 | tf_op jit(solution)/shard_map/ppermute | solution.py:407
  7.0 1.5 %collective-permute-start.3 = (bf16[2,32,256]{2,1,0:T(8,128)(2,1)}, bf16[2,32,256]{2,1,0:T(8,128)(2,1)S(1)}, u32[]{:S(2)}, u32[]{:S(2)}) collective-permute-start(bf16[2,32,256]{2,1,0:T(8,128)(2,1)} %param.8), channel_id=1, source_target_pairs={{0,16},{1,2},{2,1},{3,4},{4,3},{5,6},{6,5},{7,8},{8,7},{9,10},{10,... | collective-permute-start | bytes 98312 | tf_op jit(solution)/shard_map/ppermute | solution.py:437
  8.5 0.1 collective-permute-done.1
  8.6 1.8 %collective-permute-start.2 = (bf16[4,32,256]{2,1,0:T(8,128)(2,1)S(1)}, bf16[4,32,256]{2,1,0:T(8,128)(2,1)S(1)}, u32[]{:S(2)}, u32[]{:S(2)}) collective-permute-start(bf16[4,32,256]{2,1,0:T(8,128)(2,1)S(1)} %pad_maximum_fusion.2), channel_id=1, source_target_pairs={{0,3},{1,2},{2,1},{3,0},{4,7},{5,6},{6,5},{7,4},{8,11},{9,10},{10,... | collective-permute-start | bytes 196616 | tf_op jit(solution)/shard_map/ppermute | solution.py:407
  10.4 1.9 %shard_map.82 = (bf16[8,512,256]{2,1,0:T(8,128)(2,1)S(1)}, bf16[8,256,256]{2,1,0:T(8,128)(2,1)S(1)}, f32[16,16,128]{2,1,0:T(8,128)S(1)}, f32[8,16,128]{2,1,0:T(8,128)S(1)}) custom-call(f32[13,3,8]{2,1,0:T(4,128)S(1)} %pad_add_fusion.packed_ref), custom_call_target="tpu_custom_call" | custom-call | flops 2000000000 | bytes 3500000 | tf_op jit(solution)/shard_map/pallas_call | solution.py:247
  12.4 0.2 collective-permute-done.2
  12.6 0.0 collective-permute-done.3.outer_ref
  12.7 0.4 %collective-permute-start.4 = (bf16[10,32,256]{2,1,0:T(8,128)(2,1)S(1)}, bf16[10,32,256]{2,1,0:T(8,128)(2,1)S(1)}, u32[]{:S(2)}, u32[]{:S(2)}) collective-permute-start(bf16[10,32,256]{2,1,0:T(8,128)(2,1)S(1)} %pad_maximum_fusion.own_ref), channel_id=1, source_target_pairs={{0,1},{1,0},{2,3},{3,2},{4,5},{5,4},{6,7},{7,6},{8,9},{9,8},{10,11... | collective-permute-start | bytes 491528 | tf_op jit(solution)/shard_map/ppermute | solution.py:407
  13.7 0.4 %collective-permute-done.4.mate_ref = bf16[10,32,256]{2,1,0:T(8,128)(2,1)S(1)} collective-permute-done((bf16[10,32,256]{2,1,0:T(8,128)(2,1)S(1)}, bf16[10,32,256]{2,1,0:T(8,128)(2,1)S(1)}, u32[]{:S(2)}, u32[]{:S(2)}) %collective-permute-start.4) | collective-permute-done | bytes 163872 | tf_op jit(solution)/shard_map/ppermute | solution.py:407
  14.1 5.2 %shard_map.83 = (f32[64,512]{1,0:T(8,128)S(1)}, f32[1,512]{1,0:T(1,128)S(1)}) custom-call(f32[1]{0:T(128)S(6)} %copy.9.bias2_ref, bf16[8,512,256]{2,1,0:T(8,128)(2,1)S(1)} %get-tuple-element.33.at1_ref, bf16[8,256,256]{2,1,0:T(8,128)(2,1)S(1)} %get-tuple-element.34.at2_ref, f32[16,16,128]{2,1,0:T(8,128)S(1)} %get-tuple-element.35.w1_ref, ...), custom_call_target="tpu_custom_call" | custom-call | flops 2000000000 | bytes 4500000 | tf_op jit(solution)/shard_map/pallas_call | solution.py:381
  19.3 3.3 %collective-permute-start.5 = (f32[1,512]{1,0:T(1,128)S(1)}, f32[1,512]{1,0:T(1,128)S(1)}, u32[]{:S(2)}, u32[]{:S(2)}) collective-permute-start(f32[1,512]{1,0:T(1,128)S(1)} %get-tuple-element.40), channel_id=1, source_target_pairs={{0,9},{1,8},{2,11},{3,10},{4,13},{5,12},{6,15},{7,14},{8,1},{9,0},... | collective-permute-start | bytes 6152 | tf_op jit(solution)/shard_map/ppermute | solution.py:407
  22.5 1.3 %collective-permute-done.5 = f32[1,512]{1,0:T(1,128)S(1)} collective-permute-done((f32[1,512]{1,0:T(1,128)S(1)}, f32[1,512]{1,0:T(1,128)S(1)}, u32[]{:S(2)}, u32[]{:S(2)}) %collective-permute-start.5) | collective-permute-done | bytes 2080 | tf_op jit(solution)/shard_map/ppermute | solution.py:407
  23.8 1.8 %collective-permute-start.6 = (f32[1,512]{1,0:T(1,128)S(1)}, f32[1,512]{1,0:T(1,128)S(1)}, u32[]{:S(2)}, u32[]{:S(2)}) collective-permute-start(f32[1,512]{1,0:T(1,128)S(1)} %max.12), channel_id=1, source_target_pairs={{0,5},{1,4},{2,7},{3,6},{4,1},{5,0},{6,3},{7,2},{8,13},{9,12},{10,... | collective-permute-start | bytes 6152 | tf_op jit(solution)/shard_map/ppermute | solution.py:407
  25.6 0.1 reduce_max.9
  25.7 1.2 %collective-permute-done.6 = f32[1,512]{1,0:T(1,128)S(1)} collective-permute-done((f32[1,512]{1,0:T(1,128)S(1)}, f32[1,512]{1,0:T(1,128)S(1)}, u32[]{:S(2)}, u32[]{:S(2)}) %collective-permute-start.6) | collective-permute-done | bytes 2080 | tf_op jit(solution)/shard_map/ppermute | solution.py:407
  26.9 1.6 %collective-permute-start.7 = (f32[1,512]{1,0:T(1,128)S(1)}, f32[1,512]{1,0:T(1,128)S(1)}, u32[]{:S(2)}, u32[]{:S(2)}) collective-permute-start(f32[1,512]{1,0:T(1,128)S(1)} %max.13), channel_id=1, source_target_pairs={{0,3},{1,2},{2,1},{3,0},{4,7},{5,6},{6,5},{7,4},{8,11},{9,10},{10,... | collective-permute-start | bytes 6152 | tf_op jit(solution)/shard_map/ppermute | solution.py:407
  28.5 1.5 %collective-permute-done.7 = f32[1,512]{1,0:T(1,128)S(1)} collective-permute-done((f32[1,512]{1,0:T(1,128)S(1)}, f32[1,512]{1,0:T(1,128)S(1)}, u32[]{:S(2)}, u32[]{:S(2)}) %collective-permute-start.7) | collective-permute-done | bytes 2080 | tf_op jit(solution)/shard_map/ppermute | solution.py:407
  29.9 0.3 collective-permute-start.8
  30.2 0.1 divide_multiply_fusion
  30.3 0.8 %collective-permute-done.8 = f32[1,512]{1,0:T(1,128)S(1)} collective-permute-done((f32[1,512]{1,0:T(1,128)S(1)}, f32[1,512]{1,0:T(1,128)S(1)}, u32[]{:S(2)}, u32[]{:S(2)}) %collective-permute-start.8) | collective-permute-done | bytes 2080 | tf_op jit(solution)/shard_map/ppermute | solution.py:407
  31.1 0.7 %divide_multiply_fusion.1 = f32[64,512]{1,0:T(8,128)} fusion(f32[64,512]{1,0:T(8,128)S(1)} %divide_multiply_fusion, f32[64,512]{1,0:T(8,128)S(1)} %get-tuple-element.39, f32[512]{0:T(512)S(1)} %bitcast.7), kind=kLoop, calls=%fused_computation.3 | loop fusion | flops 65536 | bytes 395264 | tf_op jit(solution)/shard_map/mul | solution.py:456
  (11 shorter events, 0.1 us)
Async XLA Ops:
  0.0 5.1 %collective-permute-start = (bf16[1,32,256]{2,1,0:T(8,128)(2,1)}, bf16[1,32,256]{2,1,0:T(8,128)(2,1)S(1)}, u32[]{:S(2)}, u32[]{:S(2)}) collective-permute-start(bf16[1,32,256]{2,1,0:T(8,128)(2,1)} %param.9), channel_id=1, source_target_pairs={{0,9},{1,8},{2,11},{3,10},{4,13},{5,12},{6,15},{7,14},{8,1},{9,0},... | collective-permute-start | bytes 49160 | tf_op jit(solution)/shard_map/ppermute | solution.py:407
  5.1 3.5 %collective-permute-start.1 = (bf16[2,32,256]{2,1,0:T(8,128)(2,1)S(1)}, bf16[2,32,256]{2,1,0:T(8,128)(2,1)S(1)}, u32[]{:S(2)}, u32[]{:S(2)}) collective-permute-start(bf16[2,32,256]{2,1,0:T(8,128)(2,1)S(1)} %pad_maximum_fusion.4), channel_id=1, source_target_pairs={{0,5},{1,4},{2,7},{3,6},{4,1},{5,0},{6,3},{7,2},{8,13},{9,12},{10,... | collective-permute-start | bytes 98312 | tf_op jit(solution)/shard_map/ppermute | solution.py:407
  7.0 5.6 %collective-permute-start.3 = (bf16[2,32,256]{2,1,0:T(8,128)(2,1)}, bf16[2,32,256]{2,1,0:T(8,128)(2,1)S(1)}, u32[]{:S(2)}, u32[]{:S(2)}) collective-permute-start(bf16[2,32,256]{2,1,0:T(8,128)(2,1)} %param.8), channel_id=1, source_target_pairs={{0,16},{1,2},{2,1},{3,4},{4,3},{5,6},{6,5},{7,8},{8,7},{9,10},{10,... | collective-permute-start | bytes 98312 | tf_op jit(solution)/shard_map/ppermute | solution.py:437
  8.6 4.0 %collective-permute-start.2 = (bf16[4,32,256]{2,1,0:T(8,128)(2,1)S(1)}, bf16[4,32,256]{2,1,0:T(8,128)(2,1)S(1)}, u32[]{:S(2)}, u32[]{:S(2)}) collective-permute-start(bf16[4,32,256]{2,1,0:T(8,128)(2,1)S(1)} %pad_maximum_fusion.2), channel_id=1, source_target_pairs={{0,3},{1,2},{2,1},{3,0},{4,7},{5,6},{6,5},{7,4},{8,11},{9,10},{10,... | collective-permute-start | bytes 196616 | tf_op jit(solution)/shard_map/ppermute | solution.py:407
  12.7 1.5 %collective-permute-start.4 = (bf16[10,32,256]{2,1,0:T(8,128)(2,1)S(1)}, bf16[10,32,256]{2,1,0:T(8,128)(2,1)S(1)}, u32[]{:S(2)}, u32[]{:S(2)}) collective-permute-start(bf16[10,32,256]{2,1,0:T(8,128)(2,1)S(1)} %pad_maximum_fusion.own_ref), channel_id=1, source_target_pairs={{0,1},{1,0},{2,3},{3,2},{4,5},{5,4},{6,7},{7,6},{8,9},{9,8},{10,11... | collective-permute-start | bytes 491528 | tf_op jit(solution)/shard_map/ppermute | solution.py:407
  19.3 4.6 %collective-permute-start.5 = (f32[1,512]{1,0:T(1,128)S(1)}, f32[1,512]{1,0:T(1,128)S(1)}, u32[]{:S(2)}, u32[]{:S(2)}) collective-permute-start(f32[1,512]{1,0:T(1,128)S(1)} %get-tuple-element.40), channel_id=1, source_target_pairs={{0,9},{1,8},{2,11},{3,10},{4,13},{5,12},{6,15},{7,14},{8,1},{9,0},... | collective-permute-start | bytes 6152 | tf_op jit(solution)/shard_map/ppermute | solution.py:407
  23.8 3.1 %collective-permute-start.6 = (f32[1,512]{1,0:T(1,128)S(1)}, f32[1,512]{1,0:T(1,128)S(1)}, u32[]{:S(2)}, u32[]{:S(2)}) collective-permute-start(f32[1,512]{1,0:T(1,128)S(1)} %max.12), channel_id=1, source_target_pairs={{0,5},{1,4},{2,7},{3,6},{4,1},{5,0},{6,3},{7,2},{8,13},{9,12},{10,... | collective-permute-start | bytes 6152 | tf_op jit(solution)/shard_map/ppermute | solution.py:407
  26.9 3.0 %collective-permute-start.7 = (f32[1,512]{1,0:T(1,128)S(1)}, f32[1,512]{1,0:T(1,128)S(1)}, u32[]{:S(2)}, u32[]{:S(2)}) collective-permute-start(f32[1,512]{1,0:T(1,128)S(1)} %max.13), channel_id=1, source_target_pairs={{0,3},{1,2},{2,1},{3,0},{4,7},{5,6},{6,5},{7,4},{8,11},{9,10},{10,... | collective-permute-start | bytes 6152 | tf_op jit(solution)/shard_map/ppermute | solution.py:407
  29.9 1.2 %collective-permute-start.8 = (f32[1,512]{1,0:T(1,128)S(1)}, f32[1,512]{1,0:T(1,128)S(1)}, u32[]{:S(2)}, u32[]{:S(2)}) collective-permute-start(f32[1,512]{1,0:T(1,128)S(1)} %max.14), channel_id=1, source_target_pairs={{0,1},{1,0},{2,3},{3,2},{4,5},{5,4},{6,7},{7,6},{8,9},{9,8},{10,11... | collective-permute-start | bytes 6152 | tf_op jit(solution)/shard_map/ppermute | solution.py:407

commit v7 on v6

--- a/solution.py
+++ b/solution.py
@@ -451,7 +451,7 @@
     part = lax.optimization_barrier(
         score * (score / (jnp.max(score, axis=1, keepdims=True) + EPSILON))
     )
-    for mask in masks + [1]:
+    for mask in [1] + masks[::-1]:
         best = jnp.maximum(best, exchange(best, mask, count))
     out = part * (score / (best + EPSILON))
     return out.reshape(feat_a.shape[0], width, -1)

time: 32.1 us -> 32.1 us (level)
  no operation moved by 1% of the time
where the time goes in v7:
time: 32.1 us; the launch traced here: 31.8 us
  starting transfers between devices  16.1 us (50%)
  Pallas kernels  7.09 us (22%)
  waiting for transfers between devices  5.44 us (17%)
  other arithmetic  2.47 us (8%)
  between operations  0.72 us (2%)
    ppermute x8, starting transfers between devices, exchange(): return lax.ppermute(value, 'arow', [(i, i ^ mask) for i in range(count)])  14.6 us
    ppermute x8, waiting for transfers between devices, exchange(): return lax.ppermute(value, 'arow', [(i, i ^ mask) for i in range(count)])  5.43 us
    pallas_call x1, Pallas kernels, consensus(): pl.pallas_call(functools.partial(consensus_kernel, offsets, width), out_s...  5.15 us
    pallas_call x1, Pallas kernels, prepare(): pl.pallas_call(functools.partial(prepare_kernel, width), out_shape=(jax.S...  1.94 us
    ppermute x1, starting transfers between devices, fast(): outer = lax.ppermute(feat_a, ('groups', 'arow'), outer_pairs(groups, count))  1.52 us
    concatenate x1, other arithmetic, fast(): near = lax.optimization_barrier(jnp.concatenate([feat_a, feat_b], axis=0))  0.78 us
    add x1, other arithmetic, pack(): packed += jnp.pad(f.transpose(1, 2, 0), ((3 * n, 10 - 3 * n), (0, 0), (0,...  0.75 us
    mul x1, other arithmetic, fast(): out = part * (score / (best + EPSILON))  0.68 us
  transfers between devices with their start and end apart: 9, of which 8 were waited for; matrix products, arithmetic and copies ran while one was open for 6% of the time, Pallas kernels for 6%

profile of v7, /device:TPU:0, one launch (start us, length us, event | category | flops | bytes accessed | tf_op | source)
XLA Modules:
  0.0 31.8 jit_solution(6613025808764701967)
XLA Ops:
  0.0 3.5 %collective-permute-start = (bf16[1,32,256]{2,1,0:T(8,128)(2,1)}, bf16[1,32,256]{2,1,0:T(8,128)(2,1)S(1)}, u32[]{:S(2)}, u32[]{:S(2)}) collective-permute-start(bf16[1,32,256]{2,1,0:T(8,128)(2,1)} %param.9), channel_id=1, source_target_pairs={{0,9},{1,8},{2,11},{3,10},{4,13},{5,12},{6,15},{7,14},{8,1},{9,0},... | collective-permute-start | bytes 49160 | tf_op jit(solution)/shard_map/ppermute | solution.py:407
  3.5 0.8 %pad_maximum_fusion.3 = bf16[3,32,256]{2,1,0:T(8,128)(2,1)S(1)} fusion(bf16[1,32,256]{2,1,0:T(8,128)(2,1)} %param.9, bf16[2,32,256]{2,1,0:T(8,128)(2,1)} %param.8), kind=kLoop, calls=%fused_computation.5 | loop fusion | flops 24576 | bytes 98304 | tf_op jit(solution)/shard_map/concatenate | solution.py:430
  4.3 0.8 %pad_add_fusion.packed_ref = f32[13,3,8]{2,1,0:T(4,128)S(1)} fusion(f32[3,3,8]{2,1,0:T(4,128)} %bitcast.8, f32[3,3,8]{2,1,0:T(4,128)} %bitcast.9, f32[3,3,8]{2,1,0:T(4,128)} %bitcast.10, f32[3,3,8]{2,1,0:T(4,128)} %bitcast.11, f32[1,1,8]{2,1,0:T(1,128)} %bitcast.12), kind=kLoop, calls=%fused_computation.7 | loop fusion | flops 1248 | bytes 2432 | tf_op jit(solution)/shard_map/add | solution.py:241
  5.0 0.1 collective-permute-done
  5.1 1.9 %collective-permute-start.1 = (bf16[2,32,256]{2,1,0:T(8,128)(2,1)S(1)}, bf16[2,32,256]{2,1,0:T(8,128)(2,1)S(1)}, u32[]{:S(2)}, u32[]{:S(2)}) collective-permute-start(bf16[2,32,256]{2,1,0:T(8,128)(2,1)S(1)} %pad_maximum_fusion.4), channel_id=1, source_target_pairs={{0,5},{1,4},{2,7},{3,6},{4,1},{5,0},{6,3},{7,2},{8,13},{9,12},{10,... | collective-permute-start | bytes 98312 | tf_op jit(solution)/shard_map/ppermute | solution.py:407
  7.0 1.5 %collective-permute-start.3 = (bf16[2,32,256]{2,1,0:T(8,128)(2,1)}, bf16[2,32,256]{2,1,0:T(8,128)(2,1)S(1)}, u32[]{:S(2)}, u32[]{:S(2)}) collective-permute-start(bf16[2,32,256]{2,1,0:T(8,128)(2,1)} %param.8), channel_id=1, source_target_pairs={{0,16},{1,2},{2,1},{3,4},{4,3},{5,6},{6,5},{7,8},{8,7},{9,10},{10,... | collective-permute-start | bytes 98312 | tf_op jit(solution)/shard_map/ppermute | solution.py:437
  8.5 0.1 collective-permute-done.1
  8.6 1.8 %collective-permute-start.2 = (bf16[4,32,256]{2,1,0:T(8,128)(2,1)S(1)}, bf16[4,32,256]{2,1,0:T(8,128)(2,1)S(1)}, u32[]{:S(2)}, u32[]{:S(2)}) collective-permute-start(bf16[4,32,256]{2,1,0:T(8,128)(2,1)S(1)} %pad_maximum_fusion.2), channel_id=1, source_target_pairs={{0,3},{1,2},{2,1},{3,0},{4,7},{5,6},{6,5},{7,4},{8,11},{9,10},{10,... | collective-permute-start | bytes 196616 | tf_op jit(solution)/shard_map/ppermute | solution.py:407
  10.4 1.9 %shard_map.82 = (bf16[8,512,256]{2,1,0:T(8,128)(2,1)S(1)}, bf16[8,256,256]{2,1,0:T(8,128)(2,1)S(1)}, f32[16,16,128]{2,1,0:T(8,128)S(1)}, f32[8,16,128]{2,1,0:T(8,128)S(1)}) custom-call(f32[13,3,8]{2,1,0:T(4,128)S(1)} %pad_add_fusion.packed_ref), custom_call_target="tpu_custom_call" | custom-call | flops 2000000000 | bytes 3500000 | tf_op jit(solution)/shard_map/pallas_call | solution.py:247
  12.4 0.2 collective-permute-done.2
  12.6 0.0 collective-permute-done.3.outer_ref
  12.7 0.4 %collective-permute-start.4 = (bf16[10,32,256]{2,1,0:T(8,128)(2,1)S(1)}, bf16[10,32,256]{2,1,0:T(8,128)(2,1)S(1)}, u32[]{:S(2)}, u32[]{:S(2)}) collective-permute-start(bf16[10,32,256]{2,1,0:T(8,128)(2,1)S(1)} %pad_maximum_fusion.own_ref), channel_id=1, source_target_pairs={{0,1},{1,0},{2,3},{3,2},{4,5},{5,4},{6,7},{7,6},{8,9},{9,8},{10,11... | collective-permute-start | bytes 491528 | tf_op jit(solution)/shard_map/ppermute | solution.py:407
  13.7 0.4 %collective-permute-done.4.mate_ref = bf16[10,32,256]{2,1,0:T(8,128)(2,1)S(1)} collective-permute-done((bf16[10,32,256]{2,1,0:T(8,128)(2,1)S(1)}, bf16[10,32,256]{2,1,0:T(8,128)(2,1)S(1)}, u32[]{:S(2)}, u32[]{:S(2)}) %collective-permute-start.4) | collective-permute-done | bytes 163872 | tf_op jit(solution)/shard_map/ppermute | solution.py:407
  14.1 5.2 %shard_map.83 = (f32[64,512]{1,0:T(8,128)S(1)}, f32[1,512]{1,0:T(1,128)S(1)}) custom-call(f32[1]{0:T(128)S(6)} %copy.9.bias2_ref, bf16[8,512,256]{2,1,0:T(8,128)(2,1)S(1)} %get-tuple-element.33.at1_ref, bf16[8,256,256]{2,1,0:T(8,128)(2,1)S(1)} %get-tuple-element.34.at2_ref, f32[16,16,128]{2,1,0:T(8,128)S(1)} %get-tuple-element.35.w1_ref, ...), custom_call_target="tpu_custom_call" | custom-call | flops 2000000000 | bytes 4500000 | tf_op jit(solution)/shard_map/pallas_call | solution.py:381
  19.3 0.4 %collective-permute-start.5 = (f32[1,512]{1,0:T(1,128)S(1)}, f32[1,512]{1,0:T(1,128)S(1)}, u32[]{:S(2)}, u32[]{:S(2)}) collective-permute-start(f32[1,512]{1,0:T(1,128)S(1)} %get-tuple-element.40), channel_id=1, source_target_pairs={{0,1},{1,0},{2,3},{3,2},{4,5},{5,4},{6,7},{7,6},{8,9},{9,8},{10,11... | collective-permute-start | bytes 6152 | tf_op jit(solution)/shard_map/ppermute | solution.py:407
  19.7 0.8 %collective-permute-done.5 = f32[1,512]{1,0:T(1,128)S(1)} collective-permute-done((f32[1,512]{1,0:T(1,128)S(1)}, f32[1,512]{1,0:T(1,128)S(1)}, u32[]{:S(2)}, u32[]{:S(2)}) %collective-permute-start.5) | collective-permute-done | bytes 2080 | tf_op jit(solution)/shard_map/ppermute | solution.py:407
  20.5 2.0 %collective-permute-start.6 = (f32[1,512]{1,0:T(1,128)S(1)}, f32[1,512]{1,0:T(1,128)S(1)}, u32[]{:S(2)}, u32[]{:S(2)}) collective-permute-start(f32[1,512]{1,0:T(1,128)S(1)} %max.12), channel_id=1, source_target_pairs={{0,3},{1,2},{2,1},{3,0},{4,7},{5,6},{6,5},{7,4},{8,11},{9,10},{10,... | collective-permute-start | bytes 6152 | tf_op jit(solution)/shard_map/ppermute | solution.py:407
  22.5 0.1 reduce_max.9
  22.6 1.2 %collective-permute-done.6 = f32[1,512]{1,0:T(1,128)S(1)} collective-permute-done((f32[1,512]{1,0:T(1,128)S(1)}, f32[1,512]{1,0:T(1,128)S(1)}, u32[]{:S(2)}, u32[]{:S(2)}) %collective-permute-start.6) | collective-permute-done | bytes 2080 | tf_op jit(solution)/shard_map/ppermute | solution.py:407
  23.8 1.8 %collective-permute-start.7 = (f32[1,512]{1,0:T(1,128)S(1)}, f32[1,512]{1,0:T(1,128)S(1)}, u32[]{:S(2)}, u32[]{:S(2)}) collective-permute-start(f32[1,512]{1,0:T(1,128)S(1)} %max.13), channel_id=1, source_target_pairs={{0,5},{1,4},{2,7},{3,6},{4,1},{5,0},{6,3},{7,2},{8,13},{9,12},{10,... | collective-permute-start | bytes 6152 | tf_op jit(solution)/shard_map/ppermute | solution.py:407
  25.6 1.3 %collective-permute-done.7 = f32[1,512]{1,0:T(1,128)S(1)} collective-permute-done((f32[1,512]{1,0:T(1,128)S(1)}, f32[1,512]{1,0:T(1,128)S(1)}, u32[]{:S(2)}, u32[]{:S(2)}) %collective-permute-start.7) | collective-permute-done | bytes 2080 | tf_op jit(solution)/shard_map/ppermute | solution.py:407
  26.9 2.9 %collective-permute-start.8 = (f32[1,512]{1,0:T(1,128)S(1)}, f32[1,512]{1,0:T(1,128)S(1)}, u32[]{:S(2)}, u32[]{:S(2)}) collective-permute-start(f32[1,512]{1,0:T(1,128)S(1)} %max.14), channel_id=1, source_target_pairs={{0,9},{1,8},{2,11},{3,10},{4,13},{5,12},{6,15},{7,14},{8,1},{9,0},... | collective-permute-start | bytes 6152 | tf_op jit(solution)/shard_map/ppermute | solution.py:407
  29.8 0.1 divide_multiply_fusion
  29.9 1.2 %collective-permute-done.8 = f32[1,512]{1,0:T(1,128)S(1)} collective-permute-done((f32[1,512]{1,0:T(1,128)S(1)}, f32[1,512]{1,0:T(1,128)S(1)}, u32[]{:S(2)}, u32[]{:S(2)}) %collective-permute-start.8) | collective-permute-done | bytes 2080 | tf_op jit(solution)/shard_map/ppermute | solution.py:407
  31.1 0.7 %divide_multiply_fusion.1 = f32[64,512]{1,0:T(8,128)} fusion(f32[64,512]{1,0:T(8,128)S(1)} %divide_multiply_fusion, f32[64,512]{1,0:T(8,128)S(1)} %get-tuple-element.39, f32[512]{0:T(512)S(1)} %bitcast.7), kind=kLoop, calls=%fused_computation.3 | loop fusion | flops 65536 | bytes 395264 | tf_op jit(solution)/shard_map/mul | solution.py:456
  (11 shorter events, 0.1 us)
Async XLA Ops:
  0.0 5.1 %collective-permute-start = (bf16[1,32,256]{2,1,0:T(8,128)(2,1)}, bf16[1,32,256]{2,1,0:T(8,128)(2,1)S(1)}, u32[]{:S(2)}, u32[]{:S(2)}) collective-permute-start(bf16[1,32,256]{2,1,0:T(8,128)(2,1)} %param.9), channel_id=1, source_target_pairs={{0,9},{1,8},{2,11},{3,10},{4,13},{5,12},{6,15},{7,14},{8,1},{9,0},... | collective-permute-start | bytes 49160 | tf_op jit(solution)/shard_map/ppermute | solution.py:407
  5.1 3.5 %collective-permute-start.1 = (bf16[2,32,256]{2,1,0:T(8,128)(2,1)S(1)}, bf16[2,32,256]{2,1,0:T(8,128)(2,1)S(1)}, u32[]{:S(2)}, u32[]{:S(2)}) collective-permute-start(bf16[2,32,256]{2,1,0:T(8,128)(2,1)S(1)} %pad_maximum_fusion.4), channel_id=1, source_target_pairs={{0,5},{1,4},{2,7},{3,6},{4,1},{5,0},{6,3},{7,2},{8,13},{9,12},{10,... | collective-permute-start | bytes 98312 | tf_op jit(solution)/shard_map/ppermute | solution.py:407
  7.0 5.6 %collective-permute-start.3 = (bf16[2,32,256]{2,1,0:T(8,128)(2,1)}, bf16[2,32,256]{2,1,0:T(8,128)(2,1)S(1)}, u32[]{:S(2)}, u32[]{:S(2)}) collective-permute-start(bf16[2,32,256]{2,1,0:T(8,128)(2,1)} %param.8), channel_id=1, source_target_pairs={{0,16},{1,2},{2,1},{3,4},{4,3},{5,6},{6,5},{7,8},{8,7},{9,10},{10,... | collective-permute-start | bytes 98312 | tf_op jit(solution)/shard_map/ppermute | solution.py:437
  8.6 4.0 %collective-permute-start.2 = (bf16[4,32,256]{2,1,0:T(8,128)(2,1)S(1)}, bf16[4,32,256]{2,1,0:T(8,128)(2,1)S(1)}, u32[]{:S(2)}, u32[]{:S(2)}) collective-permute-start(bf16[4,32,256]{2,1,0:T(8,128)(2,1)S(1)} %pad_maximum_fusion.2), channel_id=1, source_target_pairs={{0,3},{1,2},{2,1},{3,0},{4,7},{5,6},{6,5},{7,4},{8,11},{9,10},{10,... | collective-permute-start | bytes 196616 | tf_op jit(solution)/shard_map/ppermute | solution.py:407
  12.7 1.5 %collective-permute-start.4 = (bf16[10,32,256]{2,1,0:T(8,128)(2,1)S(1)}, bf16[10,32,256]{2,1,0:T(8,128)(2,1)S(1)}, u32[]{:S(2)}, u32[]{:S(2)}) collective-permute-start(bf16[10,32,256]{2,1,0:T(8,128)(2,1)S(1)} %pad_maximum_fusion.own_ref), channel_id=1, source_target_pairs={{0,1},{1,0},{2,3},{3,2},{4,5},{5,4},{6,7},{7,6},{8,9},{9,8},{10,11... | collective-permute-start | bytes 491528 | tf_op jit(solution)/shard_map/ppermute | solution.py:407
  19.3 1.2 %collective-permute-start.5 = (f32[1,512]{1,0:T(1,128)S(1)}, f32[1,512]{1,0:T(1,128)S(1)}, u32[]{:S(2)}, u32[]{:S(2)}) collective-permute-start(f32[1,512]{1,0:T(1,128)S(1)} %get-tuple-element.40), channel_id=1, source_target_pairs={{0,1},{1,0},{2,3},{3,2},{4,5},{5,4},{6,7},{7,6},{8,9},{9,8},{10,11... | collective-permute-start | bytes 6152 | tf_op jit(solution)/shard_map/ppermute | solution.py:407
  20.5 3.3 %collective-permute-start.6 = (f32[1,512]{1,0:T(1,128)S(1)}, f32[1,512]{1,0:T(1,128)S(1)}, u32[]{:S(2)}, u32[]{:S(2)}) collective-permute-start(f32[1,512]{1,0:T(1,128)S(1)} %max.12), channel_id=1, source_target_pairs={{0,3},{1,2},{2,1},{3,0},{4,7},{5,6},{6,5},{7,4},{8,11},{9,10},{10,... | collective-permute-start | bytes 6152 | tf_op jit(solution)/shard_map/ppermute | solution.py:407
  23.8 3.1 %collective-permute-start.7 = (f32[1,512]{1,0:T(1,128)S(1)}, f32[1,512]{1,0:T(1,128)S(1)}, u32[]{:S(2)}, u32[]{:S(2)}) collective-permute-start(f32[1,512]{1,0:T(1,128)S(1)} %max.13), channel_id=1, source_target_pairs={{0,5},{1,4},{2,7},{3,6},{4,1},{5,0},{6,3},{7,2},{8,13},{9,12},{10,... | collective-permute-start | bytes 6152 | tf_op jit(solution)/shard_map/ppermute | solution.py:407
  26.9 4.2 %collective-permute-start.8 = (f32[1,512]{1,0:T(1,128)S(1)}, f32[1,512]{1,0:T(1,128)S(1)}, u32[]{:S(2)}, u32[]{:S(2)}) collective-permute-start(f32[1,512]{1,0:T(1,128)S(1)} %max.14), channel_id=1, source_target_pairs={{0,9},{1,8},{2,11},{3,10},{4,13},{5,12},{6,15},{7,14},{8,1},{9,0},... | collective-permute-start | bytes 6152 | tf_op jit(solution)/shard_map/ppermute | solution.py:407
